TPU v7x, 256 devices: a whole 4x4x8 slice. The times are simulated.
256 devices in a mesh: row: 16 (over y_hi, x, core), col: 16 (over y_lo, z).
Axes of the slice: x: 4, y: 4 (y_hi: 2, y_lo: 2; y = y_hi * 2 + y_lo), z: 8, core: 2. Of those that a mesh axis runs over, the one named last changes fastest.
Arguments:
- amplitudes: bfloat16 [1600, 40960], P('row', 'col'), may hold values from -6 to 6
- integrals: bfloat16 [32768, 40960], P('row', 'col'), may hold values from -0.0390625 to 0.0390625
- row_offsets: int32 [17], replicated, may hold values from 0 to 20438, as said below
- panel_owner: int32 [3], replicated, may hold values from 0 to 15
Outputs:
- residual: float32 [3, 100, 32768], P(None, None, ('row', 'col'))
Inputs may be any that keep to these rules, and one draw needn't show every extreme that they name: row_offsets[0] is 0 and they rise; row block q holds row_offsets[q + 1] - row_offsets[q] live rows, from 512 to 2048, in its first slots; block 0 holds exactly 2048.
All inputs are finite; a program needn't handle non-finite values.
Results may differ from a plain program's by a relative error of at most 0.0003.
Values may be sent and summed in bfloat16 or wider, within the bound.
No kernel may reach another device: no remote copies, remote signals or barrier semaphores. Data moves between devices by JAX's collectives and lax.ppermute only.
A program may use at most 64 MiB of HBM per device.

v0:
```python
import jax
import jax.numpy as jnp
from jax import lax
from jax.sharding import PartitionSpec as P

STEPS = 3


def from_root(block, axis, source):
    block = jnp.where(lax.axis_index(axis) == source, block, jnp.zeros_like(block))
    return lax.psum(block, axis)


def full_product(amp_panel, integrals):
    return lax.dot_general(
        amp_panel, integrals, (((1,), (1,)), ((), ())), preferred_element_type=jnp.float32
    )


def per_device(amplitudes, integrals, row_offsets, panel_owner):
    own_row = lax.axis_index("row")
    live_rows = row_offsets[own_row + 1] - row_offsets[own_row]
    slot_count = integrals.shape[0]
    live_mask = (jnp.arange(slot_count, dtype=jnp.int32) < live_rows).astype(jnp.float32)
    collected = []
    for step in range(STEPS):
        amp_panel = from_root(amplitudes, "row", panel_owner[step])
        product = full_product(amp_panel, integrals)
        term = product * live_mask[None, :]
        collected.append(lax.psum_scatter(term, "col", scatter_dimension=1, tiled=True))
    return jnp.stack(collected)


def solution(mesh):
    return jax.shard_map(
        per_device,
        mesh=mesh,
        in_specs=(P("row", "col"), P("row", "col"), P(), P()),
        out_specs=P(None, None, ("row", "col")),
        check_vma=False,
    )
```

profile of v0, /device:TPU:32, one launch (start us, length us, event | category | flops | bytes accessed | tf_op | source)
XLA Modules:
  0.0 388.0 jit_solution(16907724380133175974)
XLA Ops:
  6.5 0.0 all-reduce.3.cloned.1.call-start
  6.5 1.4 fusion.2
  9.9 2.3 broadcast_select_fusion.2
  12.1 0.0 all-reduce.3.cloned.1.call-update
  12.1 0.0 reduce-scatter.4.cloned.1.call-start
  12.2 1.3 fusion.1
  14.7 147.7 %all-reduce.3.cloned.1.call-done = (bf16[100,2560]{1,0:T(8,128)(2,1)}, bf16[100,2560]{1,0:T(8,128)(2,1)}, bf16[100,2560]{1,0:T(8,128)(2,1)}) async-done(((bf16[100,2560]{1,0:T(8,128)(2,1)}, bf16[100,2560]{1,0:T(8,128)(2,1)}, bf16[100,2560]{1,0:T(8,128)(2,1)}), (bf16[100,2560]{1,0:T(8,128)(2,1)}, bf16[100,2560]{1,0:T(8,128)(2,1)}, bf16[100,2560]{1,0:T(8,128)(2,1)})) %all-reduce.3.cloned.1.call-update) | async-done | bytes 1536016 | tf_op jit(solution)/shard_map/psum | solution.py:11
  162.5 0.0 copy-start.1
  162.5 0.0 copy-start
  162.5 8.5 %convolution_multiply_fusion.2 = f32[100,2048]{1,0:T(8,128)} fusion(bf16[100,2560]{1,0:T(8,128)(2,1)} %get-tuple-element.7, bf16[2048,2560]{1,0:T(8,128)(2,1)} %param.5, f32[2048]{0:T(1024)S(1)} %fusion), kind=kOutput, calls=%fused_computation.2 | convolution fusion | flops 1048780800 | bytes 11825152 | tf_op jit(solution)/shard_map/dot_general | solution.py:15
  170.9 0.0 reduce-scatter.4.cloned.1.call-update
  171.0 0.0 reduce-scatter.6.cloned.1.call-start
  171.0 0.0 copy-done.1
  171.0 8.2 %convolution_multiply_fusion.1 = f32[100,2048]{1,0:T(8,128)} fusion(bf16[100,2560]{1,0:T(8,128)(2,1)S(1)} %copy-done.1, bf16[2048,2560]{1,0:T(8,128)(2,1)} %param.5, f32[2048]{0:T(1024)S(1)} %fusion), kind=kOutput, calls=%fused_computation.1 | convolution fusion | flops 1048780800 | bytes 11825152 | tf_op jit(solution)/shard_map/dot_general | solution.py:15
  179.2 0.0 reduce-scatter.6.cloned.1.call-update
  179.2 0.0 reduce-scatter.8.cloned.1.call-start
  179.3 0.0 copy-done
  179.3 8.2 %convolution_multiply_fusion = f32[100,2048]{1,0:T(8,128)} fusion(bf16[100,2560]{1,0:T(8,128)(2,1)S(1)} %copy-done, bf16[2048,2560]{1,0:T(8,128)(2,1)} %param.5, f32[2048]{0:T(1024)S(1)} %fusion), kind=kOutput, calls=%fused_computation | convolution fusion | flops 1048780800 | bytes 11825152 | tf_op jit(solution)/shard_map/dot_general | solution.py:15
  187.5 0.0 reduce-scatter.8.cloned.1.call-update
  187.5 52.6 %reduce-scatter.4.cloned.1.call-done = f32[100,128]{1,0:T(8,128)} async-done(((f32[100,2048]{1,0:T(8,128)}), f32[100,128]{1,0:T(8,128)}) %reduce-scatter.4.cloned.1.call-update) | async-done | bytes 51216 | tf_op jit(solution)/shard_map/reduce_scatter | solution.py:30
  240.1 69.9 %reduce-scatter.6.cloned.1.call-done = f32[100,128]{1,0:T(8,128)} async-done(((f32[100,2048]{1,0:T(8,128)}), f32[100,128]{1,0:T(8,128)}) %reduce-scatter.6.cloned.1.call-update) | async-done | bytes 51216 | tf_op jit(solution)/shard_map/reduce_scatter | solution.py:30
  310.0 69.9 %reduce-scatter.8.cloned.1.call-done = f32[100,128]{1,0:T(8,128)} async-done(((f32[100,2048]{1,0:T(8,128)}), f32[100,128]{1,0:T(8,128)}) %reduce-scatter.8.cloned.1.call-update) | async-done | bytes 51216 | tf_op jit(solution)/shard_map/reduce_scatter | solution.py:30
  379.9 1.5 pad_maximum_fusion
  (1 shorter events, 0.0 us)
Async XLA Ops:
  6.5 155.9 %all-reduce.3.cloned.1.call-start = ((), (), s32[]{:S(2)}) async-start(), calls=%async_computation.6 | async-start | bytes 3194880 | tf_op jit(solution)/shard_map/psum | solution.py:11
  12.1 228.0 %reduce-scatter.4.cloned.1.call-start = ((), (), s32[]{:S(2)}) async-start(), calls=%async_computation.3 | async-start | bytes 905216 | tf_op jit(solution)/shard_map/reduce_scatter | solution.py:30
  162.5 8.5 %copy-start.1 = (bf16[100,2560]{1,0:T(8,128)(2,1)S(1)}, bf16[100,2560]{1,0:T(8,128)(2,1)}, u32[]{:S(2)}) copy-start(bf16[100,2560]{1,0:T(8,128)(2,1)} %get-tuple-element.6) | copy-start | bytes 1536004
  162.5 16.8 %copy-start = (bf16[100,2560]{1,0:T(8,128)(2,1)S(1)}, bf16[100,2560]{1,0:T(8,128)(2,1)}, u32[]{:S(2)}) copy-start(bf16[100,2560]{1,0:T(8,128)(2,1)} %get-tuple-element.5) | copy-start | bytes 1536004
  171.0 139.1 %reduce-scatter.6.cloned.1.call-start = ((), (), s32[]{:S(2)}) async-start(), calls=%async_computation.4 | async-start | bytes 905216 | tf_op jit(solution)/shard_map/reduce_scatter | solution.py:30
  179.2 200.7 %reduce-scatter.8.cloned.1.call-start = ((), (), s32[]{:S(2)}) async-start(), calls=%async_computation.5 | async-start | bytes 905216 | tf_op jit(solution)/shard_map/reduce_scatter | solution.py:30
Sparse Core Ops, SparseCore 0:
  12.3 150.1 all-reduce.2
  171.1 68.9 reduce-scatter.3
  242.6 67.3 reduce-scatter.5
  312.6 67.3 reduce-scatter.7
where the time goes:
time: 391 us; the launch traced here: 388 us
  waiting for transfers between devices  340 us (87%)
  matrix products  24.8 us (6%)
  between operations  16.3 us (4%)
    reduce_scatter x3, waiting for transfers between devices, per_device(): lax.psum_scatter(term, 'col', scatter_dimension=1, tiled=True)  192 us
    psum x1, waiting for transfers between devices, from_root(): return lax.psum(block, axis)  148 us
    dot_general x3, matrix products, full_product(): lax.dot_general(amp_panel, integrals, (((1,), (1,)), ((), ())), preferred...  24.8 us
  transfers between devices with their start and end apart: 4, of which 4 were waited for; matrix products, arithmetic and copies ran while one was open for 5% of the time, Pallas kernels for 0%

commit v1 on v0

v1 whole, which is shorter than its diff:
```python
import jax
import jax.numpy as jnp
from jax import lax
from jax.sharding import Mesh, PartitionSpec as P

STEPS = 3
PW = 100
ROW = ("yh", "x", "core")
COL = ("yl", "z")
SLOT = 128
PADDED = 104
CODE = 14


def shift(size, by):
    return [(i, (i + by) % size) for i in range(size)]


def gather_panels(amplitudes, panel_owner):
    padded = jnp.pad(amplitudes, ((0, 28), (0, 0)))
    pieces = padded.reshape(4, 32, 4, 640).transpose(0, 2, 1, 3).reshape(16, 32, 640)
    held = lax.all_to_all(pieces, ROW, 0, 0)
    mine = jnp.stack([lax.dynamic_index_in_dim(held, panel_owner[s], 0, keepdims=False) for s in range(STEPS)])
    held = jnp.stack([mine, lax.ppermute(mine, "yh", shift(2, 1))])
    held = jnp.stack([held] + [lax.ppermute(held, "x", shift(4, d)) for d in range(1, 4)])
    held = jnp.stack([held, lax.ppermute(held, "core", shift(2, 1))])
    yh, x, core = (lax.axis_index(a) for a in ROW)
    held = lax.dynamic_slice_in_dim(jnp.concatenate([held, held]), core, 2, 0)
    held = held.transpose(1, 2, 0, 3, 4, 5)
    held = held[::-1]
    held = lax.dynamic_slice_in_dim(jnp.concatenate([held, held]), 3 - x, 4, 0)
    held = held.transpose(1, 0, 2, 3, 4, 5)
    held = lax.dynamic_slice_in_dim(jnp.concatenate([held, held]), yh, 2, 0)
    held = held.reshape(4, 4, STEPS, 32, 640).transpose(2, 0, 3, 1, 4).reshape(STEPS, 128, 2560)
    return held[:, :PW]


def per_device(amplitudes, integrals, row_offsets, panel_owner):
    panels = gather_panels(amplitudes, panel_owner)
    product = lax.dot_general(
        panels, integrals, (((2,), (1,)), ((), ())), preferred_element_type=jnp.float32
    )
    term = product.reshape(STEPS, PW, 16, SLOT).transpose(2, 0, 1, 3)
    largest = jnp.max(jnp.abs(term), axis=2, keepdims=True)
    exponent = jnp.floor(jnp.log2(jnp.maximum(largest, 2.0**-100)))
    code = jnp.clip(jnp.round(term * jnp.exp2(CODE - exponent)), -32767, 32767)
    code = jnp.concatenate([code, exponent, jnp.zeros((16, STEPS, PADDED - PW - 1, SLOT), jnp.float32)], axis=2)
    got = lax.all_to_all(code.astype(jnp.int32).astype(jnp.int16), COL, 0, 0)
    got = got.astype(jnp.int32).astype(jnp.float32)
    total = jnp.sum(got[:, :, :PW] * jnp.exp2(got[:, :, PW : PW + 1] - CODE), axis=0)
    own_row = lax.axis_index(ROW)
    live_rows = row_offsets[own_row + 1] - row_offsets[own_row]
    slot = lax.axis_index(COL) * SLOT + jnp.arange(SLOT, dtype=jnp.int32)
    return total * (slot < live_rows).astype(jnp.float32)[None, None, :]


def solution(mesh):
    fine = Mesh(mesh.devices.reshape(2, 4, 2, 2, 8), ROW + COL)
    return jax.shard_map(
        per_device,
        mesh=fine,
        in_specs=(P(ROW, COL), P(ROW, COL), P(), P()),
        out_specs=P(None, None, ROW + COL),
        check_vma=False,
    )
```

time: 391 us -> 116 us (0.30)
  waiting for transfers between devices: 340 us -> 54.1 us
  starting transfers between devices: 0.13 us -> 21 us
  matrix products: 24.8 us -> 9.53 us
  between operations: 16.3 us -> 7.08 us
  local copies, waits for them, and re-layouts: 2.75 us -> 11.4 us
  other arithmetic: 3.8 us -> 11.4 us
    reduce_scatter x3 -> x0, waiting for transfers between devices: 192 us -> none  [per_device(): lax.psum_scatter(term, 'col', scatter_dimension=1, tiled=True)]
    psum x1 -> x0, waiting for transfers between devices: 148 us -> none  [from_root(): return lax.psum(block, axis)]
    all_to_all x0 -> x2, waiting for transfers between devices: none -> 37 us  [the longest x1 29.5 us: per_device(): got = lax.all_to_all(code.astype(jnp.int32).astype(jnp.int16), COL, 0, 0)]
    ppermute x0 -> x5, waiting for transfers between devices: none -> 17.1 us  [the longest x3 8.78 us: gather_panels(): lax.ppermute(held, 'x', shift(4, d))]
    all_to_all x0 -> x2, starting transfers between devices: none -> 15.7 us  [the longest x1 8.7 us: per_device(): got = lax.all_to_all(code.astype(jnp.int32).astype(jnp.int16), COL, 0, 0)]
    dot_general x3 -> x1, matrix products: 24.8 us -> 9.53 us  [per_device(): lax.dot_general(panels, integrals, (((2,), (1,)), ((), ())), preferred_el...]
    transpose x0 -> x2, other arithmetic: none -> 5.31 us  [the longest x1 2.98 us: gather_panels(): held = held.transpose(1, 2, 0, 3, 4, 5)]
    ppermute x0 -> x5, starting transfers between devices: none -> 5.27 us  [the longest x3 4.35 us: gather_panels(): lax.ppermute(held, 'x', shift(4, d))]
  transfers between devices with their start and end apart: 4 -> 7, of which waited for: 4 -> 6; matrix products, arithmetic and copies ran while one was open for 5% -> 1% of each run, Pallas kernels for 0% -> 0%
where the time goes in v1:
time: 116 us; the launch traced here: 114 us
  waiting for transfers between devices  54.1 us (47%)
  starting transfers between devices  21 us (18%)
  local copies, waits for them, and re-layouts  11.4 us (10%)
  other arithmetic  11.4 us (10%)
  matrix products  9.53 us (8%)
  between operations  7.08 us (6%)
    all_to_all x1, waiting for transfers between devices, per_device(): got = lax.all_to_all(code.astype(jnp.int32).astype(jnp.int16), COL, 0, 0)  29.5 us
    dot_general x1, matrix products, per_device(): lax.dot_general(panels, integrals, (((2,), (1,)), ((), ())), preferred_el...  9.53 us
    ppermute x3, waiting for transfers between devices, gather_panels(): lax.ppermute(held, 'x', shift(4, d))  8.78 us
    all_to_all x1, starting transfers between devices, per_device(): got = lax.all_to_all(code.astype(jnp.int32).astype(jnp.int16), COL, 0, 0)  8.7 us
    all_to_all x1, waiting for transfers between devices, gather_panels(): held = lax.all_to_all(pieces, ROW, 0, 0)  7.48 us
    all_to_all x1, starting transfers between devices, gather_panels(): held = lax.all_to_all(pieces, ROW, 0, 0)  7.03 us
    ppermute x1, waiting for transfers between devices, gather_panels(): held = jnp.stack([mine, lax.ppermute(mine, 'yh', shift(2, 1))])  5.82 us
    ppermute x3, starting transfers between devices, gather_panels(): lax.ppermute(held, 'x', shift(4, d))  4.35 us
  transfers between devices with their start and end apart: 7, of which 6 were waited for; matrix products, arithmetic and copies ran while one was open for 1% of the time, Pallas kernels for 0%

profile of v1, /device:TPU:32, one launch (start us, length us, event | category | flops | bytes accessed | tf_op | source)
XLA Modules:
  0.0 114.5 jit_solution(5525586590038393477)
XLA Ops:
  0.0 1.1 pad.4
  1.3 0.9 copy.28
  2.2 7.0 %all-to-all-start = ((bf16[16,32,640]{2,1,0:T(8,128)(2,1)}), bf16[16,32,640]{2,1,0:T(8,128)(2,1)S(1)}, u32[]{:S(2)}, u32[]{:S(2)}) async-start(bf16[16,32,640]{2,1,0:T(8,128)(2,1)} %bitcast.1), calls=%async_computation | async-start | bytes 1310720 | tf_op jit(solution)/shard_map/all_to_all | solution.py:22
  9.2 0.7 fusion.26
  15.5 7.5 %all-to-all-done = bf16[16,32,640]{2,1,0:T(8,128)(2,1)S(1)} async-done(((bf16[16,32,640]{2,1,0:T(8,128)(2,1)}), bf16[16,32,640]{2,1,0:T(8,128)(2,1)S(1)}, u32[]{:S(2)}, u32[]{:S(2)}) %all-to-all-start) | async-done | bytes 655392 | tf_op jit(solution)/shard_map/all_to_all | solution.py:22
  23.1 0.6 collective-permute-start
  23.7 5.8 %collective-permute-done = bf16[3,32,640]{2,1,0:T(8,128)(2,1)S(1)} collective-permute-done((bf16[3,32,640]{2,1,0:T(8,128)(2,1)S(1)}, bf16[3,32,640]{2,1,0:T(8,128)(2,1)S(1)}, u32[]{:S(2)}, u32[]{:S(2)}) %collective-permute-start) | collective-permute-done | bytes 122912 | tf_op jit(solution)/shard_map/ppermute | solution.py:24
  29.6 1.1 collective-permute-start.2
  30.7 1.0 collective-permute-start.1
  31.7 2.2 %collective-permute-start.3 = (bf16[2,3,32,640]{3,2,1,0:T(8,128)(2,1)S(1)}, bf16[2,3,32,640]{3,2,1,0:T(8,128)(2,1)S(1)}, u32[]{:S(2)}, u32[]{:S(2)}) collective-permute-start(bf16[2,3,32,640]{3,2,1,0:T(8,128)(2,1)S(1)} %get-tuple-element.11), channel_id=1, source_target_pairs={{0,96},{32,0},{64,32},{96,64},{1,97},{33,1},{65,33},{97,65},{2,98}... | collective-permute-start | bytes 737288 | tf_op jit(solution)/shard_map/ppermute | solution.py:25
  33.9 6.1 %collective-permute-done.2 = bf16[2,3,32,640]{3,2,1,0:T(8,128)(2,1)S(1)} collective-permute-done((bf16[2,3,32,640]{3,2,1,0:T(8,128)(2,1)S(1)}, bf16[2,3,32,640]{3,2,1,0:T(8,128)(2,1)S(1)}, u32[]{:S(2)}, u32[]{:S(2)}) %collective-permute-start.2) | collective-permute-done | bytes 245792 | tf_op jit(solution)/shard_map/ppermute | solution.py:25
  40.1 2.6 %collective-permute-done.1 = bf16[2,3,32,640]{3,2,1,0:T(8,128)(2,1)S(1)} collective-permute-done((bf16[2,3,32,640]{3,2,1,0:T(8,128)(2,1)S(1)}, bf16[2,3,32,640]{3,2,1,0:T(8,128)(2,1)S(1)}, u32[]{:S(2)}, u32[]{:S(2)}) %collective-permute-start.1) | collective-permute-done | bytes 245792 | tf_op jit(solution)/shard_map/ppermute | solution.py:25
  42.9 0.3 collective-permute-start.4
  43.3 2.5 %collective-permute-done.4 = bf16[4,2,3,32,640]{4,3,2,1,0:T(8,128)(2,1)S(1)} collective-permute-done((bf16[4,2,3,32,640]{4,3,2,1,0:T(8,128)(2,1)S(1)}, bf16[4,2,3,32,640]{4,3,2,1,0:T(8,128)(2,1)S(1)}, u32[]{:S(2)}, u32[]{:S(2)}) %collective-permute-start.4) | collective-permute-done | bytes 983072 | tf_op jit(solution)/shard_map/ppermute | solution.py:26
  45.7 0.9 copy-done
  46.7 3.0 %fusion.13 = bf16[4,2,2,3,32,640]{5,4,3,1,0,2:T(8,128)(2,1)S(1)} fusion(s32[]{:T(128)S(6)} %select_n.28, bf16[1,4,2,3,32,640]{5,4,3,2,1,0:T(8,128)(2,1)S(1)} %get-tuple-element.6, bf16[1,4,2,3,32,640]{5,4,3,2,1,0:T(8,128)(2,1)} %bitcast.42), kind=kLoop, calls=%fused_computation.26 | loop fusion | flops 2949120 | bytes 3932164 | tf_op jit(solution)/shard_map/transpose | solution.py:29
  49.7 1.5 %rev.3 = bf16[4,2,2,3,32,640]{5,4,3,1,0,2:T(8,128)(2,1)} reverse(bf16[4,2,2,3,32,640]{5,4,3,1,0,2:T(8,128)(2,1)S(1)} %fusion.13), dimensions={0} | reverse | bytes 3932160 | tf_op jit(solution)/shard_map/rev | solution.py:30
  51.2 2.3 %fusion.9 = bf16[2,4,2,3,32,640]{5,4,3,0,1,2:T(8,128)(2,1)S(1)} fusion(s32[]{:T(128)S(6)} %select_n.29, bf16[4,2,2,3,32,640]{5,4,3,1,0,2:T(8,128)(2,1)} %rev.3), kind=kLoop, calls=%fused_computation.22 | loop fusion | flops 983040 | bytes 3932164 | tf_op jit(solution)/shard_map/transpose | solution.py:32
  53.5 0.8 fusion.7
  54.6 1.0 copy.30
  55.6 2.2 %reshape.59 = bf16[3,128,2560]{2,1,0:T(8,128)(2,1)} reshape(bf16[3,4,32,4,640]{4,3,2,1,0:T(4,128)(2,1)S(1)} %copy.30) | data formatting | bytes 3932160 | tf_op jit(solution)/shard_map/reshape | solution.py:34
  57.8 9.5 %fusion = f32[3,100,2048]{2,1,0:T(8,128)} fusion(bf16[2048,2560]{1,0:T(8,128)(2,1)} %param.5, bf16[3,128,2560]{2,1,0:T(8,128)(2,1)} %reshape.59), kind=kOutput, calls=%fused_computation | convolution fusion | flops 3145728000 | bytes 14540800 | tf_op jit(solution)/shard_map/dot_general | solution.py:40
  67.3 1.9 %reshape.60 = f32[3,100,16,128]{3,2,1,0:T(8,128)S(1)} reshape(f32[3,100,2048]{2,1,0:T(8,128)} %fusion) | data formatting | bytes 4915200 | tf_op jit(solution)/shard_map/reshape | solution.py:43
  69.2 1.0 fusion.3
  70.2 1.0 fusion.5
  71.2 1.5 %fusion.2 = s16[16,3,104,128]{3,2,1,0:T(8,128)(2,1)} fusion(f32[16,3,1,128]{3,2,1,0:T(1,128)S(1)} %copy.34, f32[16,3,100,128]{3,2,1,0:T(8,128)S(1)} %fusion.5, f32[104]{0:T(128)S(1)} %pad.7.clone), kind=kLoop, calls=%fused_computation.11 | loop fusion | flops 2555904 | bytes 3760544 | tf_op jit(solution)/shard_map/convert_element_type | solution.py:48
  72.7 8.7 %all-to-all-start.1 = ((s16[16,3,104,128]{3,2,1,0:T(8,128)(2,1)}), s16[16,3,104,128]{3,2,1,0:T(8,128)(2,1)S(1)}, u32[]{:S(2)}, u32[]{:S(2)}) async-start(s16[16,3,104,128]{3,2,1,0:T(8,128)(2,1)} %fusion.2), calls=%async_computation.1 | async-start | bytes 2555904 | tf_op jit(solution)/shard_map/all_to_all | solution.py:48
  81.4 0.7 fusion.25
  83.4 29.5 %all-to-all-done.1 = s16[16,3,104,128]{3,2,1,0:T(8,128)(2,1)S(1)} async-done(((s16[16,3,104,128]{3,2,1,0:T(8,128)(2,1)}), s16[16,3,104,128]{3,2,1,0:T(8,128)(2,1)S(1)}, u32[]{:S(2)}, u32[]{:S(2)}) %all-to-all-start.1) | async-done | bytes 1277984 | tf_op jit(solution)/shard_map/all_to_all | solution.py:48
  112.9 0.3 convert_convert_fusion
  113.3 0.5 fusion.6
  113.8 0.7 broadcast_multiply_fusion
  (19 shorter events, 0.8 us)
Async XLA Ops:
  0.0 9.2 %copy-start.1 = (s32[3]{0:T(128)S(1)}, s32[3]{0:T(128)}, u32[]{:S(2)}) copy-start(s32[3]{0:T(128)} %param.7) | copy-start | bytes 40
  2.2 20.8 %all-to-all-start = ((bf16[16,32,640]{2,1,0:T(8,128)(2,1)}), bf16[16,32,640]{2,1,0:T(8,128)(2,1)S(1)}, u32[]{:S(2)}, u32[]{:S(2)}) async-start(bf16[16,32,640]{2,1,0:T(8,128)(2,1)} %bitcast.1), calls=%async_computation | async-start | bytes 1310720 | tf_op jit(solution)/shard_map/all_to_all | solution.py:22
  23.1 6.5 %collective-permute-start = (bf16[3,32,640]{2,1,0:T(8,128)(2,1)S(1)}, bf16[3,32,640]{2,1,0:T(8,128)(2,1)S(1)}, u32[]{:S(2)}, u32[]{:S(2)}) collective-permute-start(bf16[3,32,640]{2,1,0:T(8,128)(2,1)S(1)} %get-tuple-element.13), channel_id=1, source_target_pairs={{0,128},{128,0},{1,129},{129,1},{2,130},{130,2},{3,131},{131,3},{4... | collective-permute-start | bytes 368648 | tf_op jit(solution)/shard_map/ppermute | solution.py:24
  29.6 10.5 %collective-permute-start.2 = (bf16[2,3,32,640]{3,2,1,0:T(8,128)(2,1)S(1)}, bf16[2,3,32,640]{3,2,1,0:T(8,128)(2,1)S(1)}, u32[]{:S(2)}, u32[]{:S(2)}) collective-permute-start(bf16[2,3,32,640]{3,2,1,0:T(8,128)(2,1)S(1)} %get-tuple-element.11), channel_id=1, source_target_pairs={{0,64},{32,96},{64,0},{96,32},{1,65},{33,97},{65,1},{97,33},{2,66}... | collective-permute-start | bytes 737288 | tf_op jit(solution)/shard_map/ppermute | solution.py:25
  30.7 12.0 %collective-permute-start.1 = (bf16[2,3,32,640]{3,2,1,0:T(8,128)(2,1)S(1)}, bf16[2,3,32,640]{3,2,1,0:T(8,128)(2,1)S(1)}, u32[]{:S(2)}, u32[]{:S(2)}) collective-permute-start(bf16[2,3,32,640]{3,2,1,0:T(8,128)(2,1)S(1)} %get-tuple-element.11), channel_id=1, source_target_pairs={{0,32},{32,64},{64,96},{96,0},{1,33},{33,65},{65,97},{97,1},{2,34}... | collective-permute-start | bytes 737288 | tf_op jit(solution)/shard_map/ppermute | solution.py:25
  31.7 11.0 %collective-permute-start.3 = (bf16[2,3,32,640]{3,2,1,0:T(8,128)(2,1)S(1)}, bf16[2,3,32,640]{3,2,1,0:T(8,128)(2,1)S(1)}, u32[]{:S(2)}, u32[]{:S(2)}) collective-permute-start(bf16[2,3,32,640]{3,2,1,0:T(8,128)(2,1)S(1)} %get-tuple-element.11), channel_id=1, source_target_pairs={{0,96},{32,0},{64,32},{96,64},{1,97},{33,1},{65,33},{97,65},{2,98}... | collective-permute-start | bytes 737288 | tf_op jit(solution)/shard_map/ppermute | solution.py:25
  42.9 2.8 %collective-permute-start.4 = (bf16[4,2,3,32,640]{4,3,2,1,0:T(8,128)(2,1)S(1)}, bf16[4,2,3,32,640]{4,3,2,1,0:T(8,128)(2,1)S(1)}, u32[]{:S(2)}, u32[]{:S(2)}) collective-permute-start(bf16[4,2,3,32,640]{4,3,2,1,0:T(8,128)(2,1)S(1)} %get-tuple-element.5), channel_id=1, source_target_pairs={{0,16},{16,0},{1,17},{17,1},{2,18},{18,2},{3,19},{19,3},{4,20},{20... | collective-permute-start | bytes 2949128 | tf_op jit(solution)/shard_map/ppermute | solution.py:26
  45.7 0.9 copy-start
  71.2 10.2 %copy-start.2 = (s32[17]{0:T(128)S(1)}, s32[17]{0:T(128)}, u32[]{:S(2)}) copy-start(s32[17]{0:T(128)} %param.6) | copy-start | bytes 208
  72.7 40.2 %all-to-all-start.1 = ((s16[16,3,104,128]{3,2,1,0:T(8,128)(2,1)}), s16[16,3,104,128]{3,2,1,0:T(8,128)(2,1)S(1)}, u32[]{:S(2)}, u32[]{:S(2)}) async-start(s16[16,3,104,128]{3,2,1,0:T(8,128)(2,1)} %fusion.2), calls=%async_computation.1 | async-start | bytes 2555904 | tf_op jit(solution)/shard_map/all_to_all | solution.py:48

commit v2 on v1

v2 whole, which is shorter than its diff:
```python
import jax
import jax.numpy as jnp
from jax import lax
from jax.experimental import pallas as pl
from jax.experimental.pallas import tpu as pltpu
from jax.sharding import Mesh, PartitionSpec as P

STEPS = 3
ROW = ("yh", "x", "core")
COL = ("yl", "z")
SLOT = 128
RB = 25
BLK = 80
USED = STEPS * RB
KB = 640
CODE = 14
WIDE = 256
VMEM = pl.BlockSpec(memory_space=pltpu.VMEM)
SMEM = pl.BlockSpec(memory_space=pltpu.SMEM)


def shift(size, by):
    return [(i, (i + by) % size) for i in range(size)]


def gather_panels(amplitudes, panel_owner):
    pieces = jnp.pad(amplitudes.reshape(2, 2, RB, 4, KB), ((0, 0), (0, 0), (0, 7), (0, 0), (0, 0)))
    pieces = pieces.transpose(0, 3, 1, 2, 4).reshape(16, 32, KB)
    held = lax.all_to_all(pieces, ROW, 0, 0)
    mine = [lax.dynamic_index_in_dim(held, panel_owner[s], 0, keepdims=False)[:RB] for s in range(STEPS)]
    mine = jnp.concatenate(mine + [jnp.zeros((BLK - USED, KB), mine[0].dtype)])
    two = jnp.stack([mine, lax.ppermute(mine, "yh", shift(2, 1))])
    eight = jnp.stack([two] + [lax.ppermute(two, "x", shift(4, d)) for d in range(1, 4)])
    return eight, lax.ppermute(eight, "core", shift(2, 1))


def encode(block):
    largest = jnp.max(jnp.abs(block), axis=0, keepdims=True)
    exponent = jnp.floor(jnp.log2(jnp.maximum(largest, 2.0**-100)))
    code = jnp.clip(jnp.round(block * jnp.exp2(CODE - exponent)), -32767.0, 32767.0)
    row = lax.broadcasted_iota(jnp.int32, block.shape, 0)
    code = jnp.where(row < USED, code, jnp.where(row == USED, exponent, 0.0))
    return code.astype(jnp.int32).astype(jnp.int16)


def decode(code):
    value = code.astype(jnp.int32).astype(jnp.float32)
    return value * jnp.exp2(value[USED : USED + 1] - CODE)


def product_kernel(place, own, other, integrals, out, acc):
    x = place[0]
    half = 4 * BLK // 2
    for back in range(4):
        columns = pl.ds(pl.multiple_of(lax.rem(x - back + 4, 4) * KB, KB), KB)
        right = integrals[:, columns]
        for core, left in enumerate((own, other)):
            part = lax.dot_general(
                left[back].reshape(half, KB), right, (((1,), (1,)), ((), ())), preferred_element_type=jnp.float32
            )
            at = pl.ds(core * half, half)
            acc[at] = part if back == 0 else acc[at] + part
    for d in range(WIDE // SLOT):
        for b in range(4):
            out[d, b] = encode(acc[pl.ds(b * BLK, BLK), pl.ds(d * SLOT, SLOT)])


def sum_kernel(place, got, live, out):
    yh, core = place[1], place[2]
    for rb in range(4):
        b = lax.rem(core + rb, 2) * 2 + lax.rem(yh + rb // 2, 2)
        total = decode(got[0, b])
        for k in range(1, 16):
            total = total + decode(got[k, b])
        total = total * live[...]
        for s in range(STEPS):
            out[s, pl.ds(rb * RB, RB), :] = total[s * RB : (s + 1) * RB]


def per_device(amplitudes, integrals, row_offsets, panel_owner):
    yh, x, core = (lax.axis_index(a) for a in ROW)
    place = jnp.stack([x, yh, core]).astype(jnp.int32)
    own, other = gather_panels(amplitudes, panel_owner)
    whole = (4, 2, BLK, KB)
    codes = pl.pallas_call(
        product_kernel,
        out_shape=jax.ShapeDtypeStruct((16, 4, BLK, SLOT), jnp.int16),
        grid=(16 * SLOT // WIDE,),
        in_specs=[
            SMEM,
            pl.BlockSpec(whole, lambda n: (0, 0, 0, 0)),
            pl.BlockSpec(whole, lambda n: (0, 0, 0, 0)),
            pl.BlockSpec((WIDE, 4 * KB), lambda n: (n, 0)),
        ],
        out_specs=pl.BlockSpec((WIDE // SLOT, 4, BLK, SLOT), lambda n: (n, 0, 0, 0)),
        scratch_shapes=[pltpu.VMEM((4 * BLK, WIDE), jnp.float32)],
        compiler_params=pltpu.CompilerParams(vmem_limit_bytes=56 << 20),
        name="product",
    )(place, own, other, integrals)
    got = lax.all_to_all(codes, COL, 0, 0)
    own_row = lax.axis_index(ROW)
    slot = lax.axis_index(COL) * SLOT + jnp.arange(SLOT, dtype=jnp.int32)
    live = (slot < row_offsets[own_row + 1] - row_offsets[own_row]).astype(jnp.float32)[None, :]
    return pl.pallas_call(
        sum_kernel,
        out_shape=jax.ShapeDtypeStruct((STEPS, 4 * RB, SLOT), jnp.float32),
        in_specs=[SMEM, VMEM, VMEM],
        out_specs=VMEM,
        compiler_params=pltpu.CompilerParams(vmem_limit_bytes=8 << 20),
        name="sum",
    )(place, got, live)


def solution(mesh):
    fine = Mesh(mesh.devices.reshape(2, 4, 2, 2, 8), ROW + COL)
    return jax.shard_map(
        per_device,
        mesh=fine,
        in_specs=(P(ROW, COL), P(ROW, COL), P(), P()),
        out_specs=P(None, None, ROW + COL),
        check_vma=False,
    )
```

time: 116 us -> 100 us (0.86)
  Pallas kernels: 0 us -> 13.9 us
  other arithmetic: 11.4 us -> 1.05 us
  matrix products: 9.53 us -> 0 us
  local copies, waits for them, and re-layouts: 11.4 us -> 4.47 us
  waiting for transfers between devices: 54.1 us -> 51.9 us
    pallas_call x0 -> x2, Pallas kernels: none -> 13.9 us  [the longest x1 12.3 us: per_device(): pl.pallas_call(product_kernel, out_shape=jax.ShapeDtypeStruct((16, 4, BLK...]
    dot_general x1 -> x0, matrix products: 9.53 us -> none  [per_device(): lax.dot_general(panels, integrals, (((2,), (1,)), ((), ())), preferred_el...]
    transpose x2 -> x0, other arithmetic: 5.31 us -> none  [the longest x1 2.98 us: gather_panels(): held = held.transpose(1, 2, 0, 3, 4, 5)]
    reshape x3 -> x2, local copies, waits for them, and re-layouts: 4.21 us -> 1.29 us  [gather_panels(): amplitudes.reshape(2, 2, RB, 4, KB)]
    ppermute x5, waiting for transfers between devices: 17.1 us -> 14.4 us  [the longest x3 7.25 us: gather_panels(): lax.ppermute(two, 'x', shift(4, d))]
    transpose x2 -> x0, local copies, waits for them, and re-layouts: 1.95 us -> none  [the longest x1 1.01 us: gather_panels(): held.reshape(4, 4, STEPS, 32, 640).transpose(2, 0, 3, 1, 4)]
    convert_element_type x3 -> x1, other arithmetic: 1.86 us -> 0.01 us  [per_device(): (slot < row_offsets[own_row + 1] - row_offsets[own_row]).astype(jnp.float32)]
    rev x1 -> x0, local copies, waits for them, and re-layouts: 1.5 us -> none  [gather_panels(): held = held[::-1]]
  transfers between devices with their start and end apart: 7 -> 7, of which waited for: 6 -> 6; matrix products, arithmetic and copies ran while one was open for 1% -> 2% of each run, Pallas kernels for 0% -> 0%
where the time goes in v2:
time: 100 us; the launch traced here: 99.2 us
  waiting for transfers between devices  51.9 us (52%)
  starting transfers between devices  20.7 us (21%)
  Pallas kernels  13.9 us (14%)
  between operations  7.13 us (7%)
  local copies, waits for them, and re-layouts  4.47 us (4%)
  other arithmetic  1.05 us (1%)
    all_to_all x1, waiting for transfers between devices, per_device(): got = lax.all_to_all(codes, COL, 0, 0)  30.3 us
    pallas_call x1, Pallas kernels, per_device(): pl.pallas_call(product_kernel, out_shape=jax.ShapeDtypeStruct((16, 4, BLK...  12.3 us
    all_to_all x1, starting transfers between devices, per_device(): got = lax.all_to_all(codes, COL, 0, 0)  8.82 us
    all_to_all x1, waiting for transfers between devices, gather_panels(): held = lax.all_to_all(pieces, ROW, 0, 0)  7.3 us
    ppermute x3, waiting for transfers between devices, gather_panels(): lax.ppermute(two, 'x', shift(4, d))  7.25 us
    all_to_all x1, starting transfers between devices, gather_panels(): held = lax.all_to_all(pieces, ROW, 0, 0)  7.03 us
    ppermute x1, waiting for transfers between devices, gather_panels(): two = jnp.stack([mine, lax.ppermute(mine, 'yh', shift(2, 1))])  5.52 us
    ppermute x3, starting transfers between devices, gather_panels(): lax.ppermute(two, 'x', shift(4, d))  4.13 us
  transfers between devices with their start and end apart: 7, of which 6 were waited for; matrix products, arithmetic and copies ran while one was open for 2% of the time, Pallas kernels for 0%

profile of v2, /device:TPU:32, one launch (start us, length us, event | category | flops | bytes accessed | tf_op | source)
XLA Modules:
  0.0 99.2 jit_solution(2866056831462023254)
XLA Ops:
  0.0 1.2 %reshape.23 = bf16[2,2,25,4,640]{4,3,2,1,0:T(4,128)(2,1)S(1)} reshape(bf16[100,2560]{1,0:T(8,128)(2,1)} %param.4) | data formatting | bytes 1024000 | tf_op jit(solution)/shard_map/reshape | solution.py:27
  1.2 0.1 copy.5
  1.3 0.0 copy-start.3
  1.3 0.9 pad.4
  2.2 7.0 %all-to-all-start = ((bf16[16,32,640]{2,1,0:T(8,128)(2,1)}), bf16[16,32,640]{2,1,0:T(8,128)(2,1)S(1)}, u32[]{:S(2)}, u32[]{:S(2)}) async-start(bf16[16,32,640]{2,1,0:T(8,128)(2,1)} %bitcast.4), calls=%async_computation | async-start | bytes 1310720 | tf_op jit(solution)/shard_map/all_to_all | solution.py:29
  9.3 0.0 copy-done.3
  9.3 0.6 fusion.2
  13.8 0.1 pad.14.clone
  15.8 7.3 %all-to-all-done = bf16[16,32,640]{2,1,0:T(8,128)(2,1)S(1)} async-done(((bf16[16,32,640]{2,1,0:T(8,128)(2,1)}), bf16[16,32,640]{2,1,0:T(8,128)(2,1)S(1)}, u32[]{:S(2)}, u32[]{:S(2)}) %all-to-all-start) | async-done | bytes 655392 | tf_op jit(solution)/shard_map/all_to_all | solution.py:29
  23.1 0.1 maximum_maximum_fusion
  23.2 0.6 collective-permute-start
  23.8 0.1 fusion.3
  23.9 5.5 %collective-permute-done = bf16[80,640]{1,0:T(8,128)(2,1)S(1)} collective-permute-done((bf16[80,640]{1,0:T(8,128)(2,1)S(1)}, bf16[80,640]{1,0:T(8,128)(2,1)S(1)}, u32[]{:S(2)}, u32[]{:S(2)}) %collective-permute-start) | collective-permute-done | bytes 102432 | tf_op jit(solution)/shard_map/ppermute | solution.py:32
  29.4 0.9 collective-permute-start.2
  30.3 1.0 %collective-permute-start.1 = (bf16[2,80,640]{2,1,0:T(8,128)(2,1)S(1)}, bf16[2,80,640]{2,1,0:T(8,128)(2,1)S(1)}, u32[]{:S(2)}, u32[]{:S(2)}) collective-permute-start(bf16[2,80,640]{2,1,0:T(8,128)(2,1)S(1)} %get-tuple-element.9), channel_id=1, source_target_pairs={{0,32},{32,64},{64,96},{96,0},{1,33},{33,65},{65,97},{97,1},{2,34}... | collective-permute-start | bytes 614408 | tf_op jit(solution)/shard_map/ppermute | solution.py:33
  31.4 2.2 %collective-permute-start.3 = (bf16[2,80,640]{2,1,0:T(8,128)(2,1)S(1)}, bf16[2,80,640]{2,1,0:T(8,128)(2,1)S(1)}, u32[]{:S(2)}, u32[]{:S(2)}) collective-permute-start(bf16[2,80,640]{2,1,0:T(8,128)(2,1)S(1)} %get-tuple-element.9), channel_id=1, source_target_pairs={{0,96},{32,0},{64,32},{96,64},{1,97},{33,1},{65,33},{97,65},{2,98}... | collective-permute-start | bytes 614408 | tf_op jit(solution)/shard_map/ppermute | solution.py:33
  33.6 5.1 %collective-permute-done.2 = bf16[2,80,640]{2,1,0:T(8,128)(2,1)S(1)} collective-permute-done((bf16[2,80,640]{2,1,0:T(8,128)(2,1)S(1)}, bf16[2,80,640]{2,1,0:T(8,128)(2,1)S(1)}, u32[]{:S(2)}, u32[]{:S(2)}) %collective-permute-start.2) | collective-permute-done | bytes 204832 | tf_op jit(solution)/shard_map/ppermute | solution.py:33
  38.7 2.1 %collective-permute-done.1 = bf16[2,80,640]{2,1,0:T(8,128)(2,1)S(1)} collective-permute-done((bf16[2,80,640]{2,1,0:T(8,128)(2,1)S(1)}, bf16[2,80,640]{2,1,0:T(8,128)(2,1)S(1)}, u32[]{:S(2)}, u32[]{:S(2)}) %collective-permute-start.1) | collective-permute-done | bytes 204832 | tf_op jit(solution)/shard_map/ppermute | solution.py:33
  40.8 0.0 collective-permute-done.3
  40.8 0.1 pad_maximum_fusion.own
  41.0 0.0 copy-start.1
  41.0 0.1 collective-permute-start.4
  41.1 0.7 pad_add_fusion.place
  41.8 1.6 %collective-permute-done.4.other = bf16[4,2,80,640]{3,2,1,0:T(8,128)(2,1)S(1)} collective-permute-done((bf16[4,2,80,640]{3,2,1,0:T(8,128)(2,1)S(1)}, bf16[4,2,80,640]{3,2,1,0:T(8,128)(2,1)S(1)}, u32[]{:S(2)}, u32[]{:S(2)}) %collective-permute-start.4) | collective-permute-done | bytes 819232 | tf_op jit(solution)/shard_map/ppermute | solution.py:34
  43.4 0.0 copy-done.1
  43.4 0.9 copy-done.2
  44.3 12.3 %product.1 = s16[16,4,80,128]{3,2,1,0:T(8,128)(2,1)} custom-call(s32[3]{0:T(128)} %pad_add_fusion.place, bf16[4,2,80,640]{3,2,1,0:T(8,128)(2,1)} %copy-done.1, bf16[4,2,80,640]{3,2,1,0:T(8,128)(2,1)} %copy-done.2, bf16[2048,2560]{1,0:T(8,128)(2,1)} %integrals.1), custom_call_target="tpu_custom_call" | custom-call | tf_op jit(solution)/shard_map/product/pallas_call | solution.py:85
  56.5 8.8 %all-to-all-start.1 = ((s16[16,4,80,128]{3,2,1,0:T(8,128)(2,1)}), s16[16,4,80,128]{3,2,1,0:T(8,128)(2,1)S(1)}, u32[]{:S(2)}, u32[]{:S(2)}) async-start(s16[16,4,80,128]{3,2,1,0:T(8,128)(2,1)} %product.1), calls=%async_computation.1 | async-start | bytes 2621440 | tf_op jit(solution)/shard_map/all_to_all | solution.py:100
  65.4 0.0 copy-done.4
  65.4 0.6 fusion.1
  67.3 30.3 %all-to-all-done.1.got = s16[16,4,80,128]{3,2,1,0:T(8,128)(2,1)S(1)} async-done(((s16[16,4,80,128]{3,2,1,0:T(8,128)(2,1)}), s16[16,4,80,128]{3,2,1,0:T(8,128)(2,1)S(1)}, u32[]{:S(2)}, u32[]{:S(2)}) %all-to-all-start.1) | async-done | bytes 1310752 | tf_op jit(solution)/shard_map/all_to_all | solution.py:100
  97.6 1.6 %sum.1 = f32[3,100,128]{2,1,0:T(8,128)} custom-call(s32[3]{0:T(128)S(1)} %copy-done, s16[16,4,80,128]{3,2,1,0:T(8,128)(2,1)S(1)} %all-to-all-done.1.got, f32[1,128]{1,0:T(1,128)S(1)} %compare_convert_fusion.live), custom_call_target="tpu_custom_call" | custom-call | tf_op jit(solution)/shard_map/sum/pallas_call | solution.py:104
  (8 shorter events, 0.1 us)
Async XLA Ops:
  1.3 8.0 %copy-start.3 = (s32[3]{0:T(128)S(1)}, s32[3]{0:T(128)}, u32[]{:S(2)}) copy-start(s32[3]{0:T(128)} %param.7) | copy-start | bytes 40
  2.2 20.8 %all-to-all-start = ((bf16[16,32,640]{2,1,0:T(8,128)(2,1)}), bf16[16,32,640]{2,1,0:T(8,128)(2,1)S(1)}, u32[]{:S(2)}, u32[]{:S(2)}) async-start(bf16[16,32,640]{2,1,0:T(8,128)(2,1)} %bitcast.4), calls=%async_computation | async-start | bytes 1310720 | tf_op jit(solution)/shard_map/all_to_all | solution.py:29
  23.2 6.3 %collective-permute-start = (bf16[80,640]{1,0:T(8,128)(2,1)S(1)}, bf16[80,640]{1,0:T(8,128)(2,1)S(1)}, u32[]{:S(2)}, u32[]{:S(2)}) collective-permute-start(bf16[80,640]{1,0:T(8,128)(2,1)S(1)} %maximum_maximum_fusion), channel_id=1, source_target_pairs={{0,128},{128,0},{1,129},{129,1},{2,130},{130,2},{3,131},{131,3},{4... | collective-permute-start | bytes 307208 | tf_op jit(solution)/shard_map/ppermute | solution.py:32
  29.4 9.2 %collective-permute-start.2 = (bf16[2,80,640]{2,1,0:T(8,128)(2,1)S(1)}, bf16[2,80,640]{2,1,0:T(8,128)(2,1)S(1)}, u32[]{:S(2)}, u32[]{:S(2)}) collective-permute-start(bf16[2,80,640]{2,1,0:T(8,128)(2,1)S(1)} %get-tuple-element.9), channel_id=1, source_target_pairs={{0,64},{32,96},{64,0},{96,32},{1,65},{33,97},{65,1},{97,33},{2,66}... | collective-permute-start | bytes 614408 | tf_op jit(solution)/shard_map/ppermute | solution.py:33
  30.3 10.5 %collective-permute-start.1 = (bf16[2,80,640]{2,1,0:T(8,128)(2,1)S(1)}, bf16[2,80,640]{2,1,0:T(8,128)(2,1)S(1)}, u32[]{:S(2)}, u32[]{:S(2)}) collective-permute-start(bf16[2,80,640]{2,1,0:T(8,128)(2,1)S(1)} %get-tuple-element.9), channel_id=1, source_target_pairs={{0,32},{32,64},{64,96},{96,0},{1,33},{33,65},{65,97},{97,1},{2,34}... | collective-permute-start | bytes 614408 | tf_op jit(solution)/shard_map/ppermute | solution.py:33
  31.4 9.5 %collective-permute-start.3 = (bf16[2,80,640]{2,1,0:T(8,128)(2,1)S(1)}, bf16[2,80,640]{2,1,0:T(8,128)(2,1)S(1)}, u32[]{:S(2)}, u32[]{:S(2)}) collective-permute-start(bf16[2,80,640]{2,1,0:T(8,128)(2,1)S(1)} %get-tuple-element.9), channel_id=1, source_target_pairs={{0,96},{32,0},{64,32},{96,64},{1,97},{33,1},{65,33},{97,65},{2,98}... | collective-permute-start | bytes 614408 | tf_op jit(solution)/shard_map/ppermute | solution.py:33
  41.0 2.4 %copy-start.1 = (bf16[4,2,80,640]{3,2,1,0:T(8,128)(2,1)}, bf16[4,2,80,640]{3,2,1,0:T(8,128)(2,1)S(1)}, u32[]{:S(2)}) copy-start(bf16[4,2,80,640]{3,2,1,0:T(8,128)(2,1)S(1)} %pad_maximum_fusion.own) | copy-start | bytes 2457604
  41.0 2.4 %collective-permute-start.4 = (bf16[4,2,80,640]{3,2,1,0:T(8,128)(2,1)S(1)}, bf16[4,2,80,640]{3,2,1,0:T(8,128)(2,1)S(1)}, u32[]{:S(2)}, u32[]{:S(2)}) collective-permute-start(bf16[4,2,80,640]{3,2,1,0:T(8,128)(2,1)S(1)} %pad_maximum_fusion.own), channel_id=1, source_target_pairs={{0,16},{16,0},{1,17},{17,1},{2,18},{18,2},{3,19},{19,3},{4,20},{20... | collective-permute-start | bytes 2457608 | tf_op jit(solution)/shard_map/ppermute | solution.py:34
  43.4 0.9 copy-start.2
  56.5 8.8 %copy-start.4 = (s32[17]{0:T(128)S(1)}, s32[17]{0:T(128)}, u32[]{:S(2)}) copy-start(s32[17]{0:T(128)} %param.6) | copy-start | bytes 208
  56.5 41.0 %copy-start = (s32[3]{0:T(128)S(1)}, s32[3]{0:T(128)}, u32[]{:S(2)}) copy-start(s32[3]{0:T(128)} %pad_add_fusion.place) | copy-start | bytes 40
  56.5 41.0 %all-to-all-start.1 = ((s16[16,4,80,128]{3,2,1,0:T(8,128)(2,1)}), s16[16,4,80,128]{3,2,1,0:T(8,128)(2,1)S(1)}, u32[]{:S(2)}, u32[]{:S(2)}) async-start(s16[16,4,80,128]{3,2,1,0:T(8,128)(2,1)} %product.1), calls=%async_computation.1 | async-start | bytes 2621440 | tf_op jit(solution)/shard_map/all_to_all | solution.py:100

commit v3 on v2

v3 whole, which is shorter than its diff:
```python
import jax
import jax.numpy as jnp
from jax import lax
from jax.experimental import pallas as pl
from jax.experimental.pallas import tpu as pltpu
from jax.sharding import Mesh, PartitionSpec as P

STEPS = 3
ROW = ("yh", "x", "core")
COL = ("yl", "z")
SLOT = 128
RB = 25
USED = STEPS * RB
BLK = 80
ROWS = 4 * USED
TALL = 304
GROUPS = ((0, 80), (80, 160), (160, 240), (240, TALL))
KB = 640
WIDE = 512
SLABS = 4
CODE = 2.0**14 * (1 - 2.0**-13)
VMEM = pl.BlockSpec(memory_space=pltpu.VMEM)
SMEM = pl.BlockSpec(memory_space=pltpu.SMEM)
HBM = pl.BlockSpec(memory_space=pltpu.HBM)
SMALL = pltpu.CompilerParams(vmem_limit_bytes=8 << 20)
LARGE = pltpu.CompilerParams(vmem_limit_bytes=54 << 20)


def shift(size, by):
    return [(i, (i + by) % size) for i in range(size)]


def cut_kernel(panel, pieces):
    for yh in range(2):
        for core in range(2):
            rows = slice((yh * 2 + core) * RB, (yh * 2 + core + 1) * RB)
            for x in range(4):
                pieces[yh * 8 + x * 2 + core, pl.ds(0, RB), :] = panel[rows, x * KB : (x + 1) * KB]


def pick_kernel(owner, held, mine):
    for s in range(STEPS):
        mine[pl.ds(s * RB, RB), :] = held[owner[s], pl.ds(0, RB), :]


def gather_panels(amplitudes, panel_owner):
    pieces = pl.pallas_call(
        cut_kernel,
        out_shape=jax.ShapeDtypeStruct((16, 32, KB), jnp.bfloat16),
        in_specs=[VMEM],
        out_specs=VMEM,
        compiler_params=SMALL,
        name="cut",
    )(amplitudes)
    held = lax.all_to_all(pieces, ROW, 0, 0)
    mine = pl.pallas_call(
        pick_kernel,
        out_shape=jax.ShapeDtypeStruct((BLK, KB), jnp.bfloat16),
        in_specs=[SMEM, VMEM],
        out_specs=VMEM,
        compiler_params=SMALL,
        name="pick",
    )(panel_owner, held)
    two = jnp.stack([mine, lax.ppermute(mine, "yh", shift(2, 1))])
    eight = jnp.stack([two] + [lax.ppermute(two, "x", shift(4, d)) for d in range(1, 4)])
    return eight, lax.ppermute(eight, "core", shift(2, 1))


def encode(rows, out, at):
    exponents = []
    for lo, hi in GROUPS:
        block = rows(lo, hi)
        largest = jnp.max(jnp.abs(block), axis=0, keepdims=True)
        exponent = jnp.floor(jnp.log2(jnp.maximum(largest, 2.0**-100)))
        exponents.append(exponent)
        code = jnp.round(block * (jnp.exp2(-exponent) * CODE))
        if hi == TALL:
            row = lax.broadcasted_iota(jnp.int32, (16, SLOT), 0) + TALL - 16
            last = code[-16:]
            for g, e in enumerate(exponents):
                last = jnp.where(row == ROWS + g, e, last)
            code = jnp.concatenate([code[:-16], last])
        out[at, pl.ds(lo, hi - lo), :] = code.astype(jnp.int32).astype(jnp.int16)


def decode(codes, lo, hi, group):
    scale = jnp.exp2(codes[pl.ds(TALL - 16, 16), :].astype(jnp.int32).astype(jnp.float32)[12 + group : 13 + group])
    return codes[pl.ds(lo, hi - lo), :].astype(jnp.int32).astype(jnp.float32) * (scale * (1 / CODE))


def product_kernel(own, other, integrals, out, left, slabs, acc, sems):
    x = lax.axis_index("x")
    copies = []
    for n in range(SLABS):
        copies.append(pltpu.make_async_copy(integrals.at[pl.ds(n * WIDE, WIDE)], slabs.at[n], sems.at[n]))
        copies[-1].start()
    left[pl.ds(TALL - 16, 16), :] = jnp.zeros((16, 4 * KB), jnp.bfloat16)
    for back in range(4):
        columns = pl.ds(pl.multiple_of(lax.rem(x - back + 4, 4) * KB, KB), KB)
        for core, piece in enumerate((own, other)):
            for yh in range(2):
                left[pl.ds((core * 2 + yh) * USED, USED), columns] = piece[back, yh, pl.ds(0, USED), :]
    for n in range(SLABS):
        copies[n].wait()
        acc[n % 2] = lax.dot_general(
            left[...], slabs[n], (((1,), (1,)), ((), ())), preferred_element_type=jnp.float32
        )
        for d in range(WIDE // SLOT):
            encode(lambda lo, hi: acc[n % 2, pl.ds(lo, hi - lo), pl.ds(d * SLOT, SLOT)], out, n * 4 + d)


def sum_kernel(got, live, out, total):
    yh, core = lax.axis_index("yh"), lax.axis_index("core")
    for g, (lo, hi) in enumerate(GROUPS):
        part = decode(got.at[0], lo, hi, g)
        for k in range(1, 16):
            part = part + decode(got.at[k], lo, hi, g)
        total[pl.ds(lo, hi - lo), :] = part * live[...]
    for b in range(4):
        rb = lax.rem(yh + b % 2, 2) * 2 + lax.rem(core + b // 2, 2)
        for case in range(4):

            @pl.when(rb == case)
            def _():
                for s in range(STEPS):
                    out[s, pl.ds(case * RB, RB), :] = total[pl.ds(b * USED + s * RB, RB), :]


def per_device(amplitudes, integrals, row_offsets, panel_owner):
    own, other = gather_panels(amplitudes, panel_owner)
    codes = pl.pallas_call(
        product_kernel,
        out_shape=jax.ShapeDtypeStruct((16, TALL, SLOT), jnp.int16),
        in_specs=[VMEM, VMEM, HBM],
        out_specs=VMEM,
        scratch_shapes=[
            pltpu.VMEM((TALL, 4 * KB), jnp.bfloat16),
            pltpu.VMEM((SLABS, WIDE, 4 * KB), jnp.bfloat16),
            pltpu.VMEM((2, TALL, WIDE), jnp.float32),
            pltpu.SemaphoreType.DMA((SLABS,)),
        ],
        compiler_params=LARGE,
        name="product",
    )(own, other, integrals)
    got = lax.all_to_all(codes, COL, 0, 0)
    own_row = lax.axis_index(ROW)
    slot = lax.axis_index(COL) * SLOT + jnp.arange(SLOT, dtype=jnp.int32)
    live = (slot < row_offsets[own_row + 1] - row_offsets[own_row]).astype(jnp.float32)[None, :]
    return pl.pallas_call(
        sum_kernel,
        out_shape=jax.ShapeDtypeStruct((STEPS, 4 * RB, SLOT), jnp.float32),
        in_specs=[VMEM, VMEM],
        out_specs=VMEM,
        scratch_shapes=[pltpu.VMEM((TALL, SLOT), jnp.float32)],
        compiler_params=SMALL,
        name="sum",
    )(got, live)


def solution(mesh):
    fine = Mesh(mesh.devices.reshape(2, 4, 2, 2, 8), ROW + COL)
    return jax.shard_map(
        per_device,
        mesh=fine,
        in_specs=(P(ROW, COL), P(ROW, COL), P(), P()),
        out_specs=P(None, None, ROW + COL),
        check_vma=False,
    )
```

time: 100 us -> 94.9 us (0.949)
  blocking collectives: 0 us -> 20.4 us
  starting transfers between devices: 20.7 us -> 12.3 us
  between operations: 7.13 us -> 1.34 us
  waiting for transfers between devices: 51.9 us -> 47.5 us
  Pallas kernels: 13.9 us -> 10.4 us
  local copies, waits for them, and re-layouts: 4.47 us -> 2.57 us
    all_to_all x0 -> x1, blocking collectives: none -> 20.4 us  [gather_panels(): held = lax.all_to_all(pieces, ROW, 0, 0)]
    all_to_all x1 -> x0, waiting for transfers between devices: 7.3 us -> none  [gather_panels(): held = lax.all_to_all(pieces, ROW, 0, 0)]
    all_to_all x1 -> x0, starting transfers between devices: 7.03 us -> none  [gather_panels(): held = lax.all_to_all(pieces, ROW, 0, 0)]
    ppermute x3, waiting for transfers between devices: 7.25 us -> 10.6 us  [gather_panels(): lax.ppermute(two, 'x', shift(4, d))]
    pallas_call x1 -> x3, Pallas kernels: 12.3 us -> 9.32 us  [the longest x1 8.62 us: per_device(): pl.pallas_call(product_kernel, out_shape=jax.ShapeDtypeStruct((16, TALL,...]
    all_to_all x1, waiting for transfers between devices: 30.3 us -> 28.8 us  [per_device(): got = lax.all_to_all(codes, COL, 0, 0)]
    ppermute x3, starting transfers between devices: 4.13 us -> 2.76 us  [gather_panels(): lax.ppermute(two, 'x', shift(4, d))]
    reshape x2 -> x0, local copies, waits for them, and re-layouts: 1.29 us -> none  [gather_panels(): amplitudes.reshape(2, 2, RB, 4, KB)]
  transfers between devices with their start and end apart: 7 -> 6, of which waited for: 6 -> 6; matrix products, arithmetic and copies ran while one was open for 2% -> 1% of each run, Pallas kernels for 0% -> 0%
where the time goes in v3:
time: 94.9 us; the launch traced here: 94.7 us
  waiting for transfers between devices  47.5 us (50%)
  blocking collectives  20.4 us (21%)
  starting transfers between devices  12.3 us (13%)
  Pallas kernels  10.4 us (11%)
  local copies, waits for them, and re-layouts  2.57 us (3%)
  between operations  1.34 us (1%)
    all_to_all x1, waiting for transfers between devices, per_device(): got = lax.all_to_all(codes, COL, 0, 0)  28.8 us
    all_to_all x1, blocking collectives, gather_panels(): held = lax.all_to_all(pieces, ROW, 0, 0)  20.4 us
    ppermute x3, waiting for transfers between devices, gather_panels(): lax.ppermute(two, 'x', shift(4, d))  10.6 us
    all_to_all x1, starting transfers between devices, per_device(): got = lax.all_to_all(codes, COL, 0, 0)  8.71 us
    pallas_call x1, Pallas kernels, per_device(): pl.pallas_call(product_kernel, out_shape=jax.ShapeDtypeStruct((16, TALL,...  8.62 us
    ppermute x1, waiting for transfers between devices, gather_panels(): two = jnp.stack([mine, lax.ppermute(mine, 'yh', shift(2, 1))])  5.72 us
    ppermute x3, starting transfers between devices, gather_panels(): lax.ppermute(two, 'x', shift(4, d))  2.76 us
    ppermute x1, waiting for transfers between devices, gather_panels(): return (eight, lax.ppermute(eight, 'core', shift(2, 1)))  2.32 us
  transfers between devices with their start and end apart: 6, of which 6 were waited for; matrix products, arithmetic and copies ran while one was open for 1% of the time, Pallas kernels for 0%

profile of v3, /device:TPU:32, one launch (start us, length us, event | category | flops | bytes accessed | tf_op | source)
XLA Modules:
  0.0 94.7 jit_solution(9561168666474171038)
XLA Ops:
  0.0 0.0 copy-start
  0.0 1.0 %copy-done = bf16[100,2560]{1,0:T(8,128)(2,1)S(1)} copy-done((bf16[100,2560]{1,0:T(8,128)(2,1)S(1)}, bf16[100,2560]{1,0:T(8,128)(2,1)}, u32[]{:S(2)}) %copy-start) | copy-done | bytes 512024
  1.0 0.0 copy-start.1
  1.0 0.1 cut.1
  1.2 20.4 %all_to_all.10.held = bf16[16,32,640]{2,1,0:T(8,128)(2,1)S(1)} all-to-all(bf16[16,32,640]{2,1,0:T(8,128)(2,1)S(1)} %cut.1), channel_id=1, replica_groups=mesh['yh'=2,'x'=4,'core'=2,'yl'=2,'z'=8] {'yh','x','core'}, dimensions={0} | all-to-all | bytes 1310720 | tf_op jit(solution)/shard_map/all_to_all | solution.py:55
  21.5 0.0 copy-done.1
  21.5 0.6 pick.1
  22.1 0.8 collective-permute-start
  22.9 5.7 %collective-permute-done = bf16[80,640]{1,0:T(8,128)(2,1)S(1)} collective-permute-done((bf16[80,640]{1,0:T(8,128)(2,1)S(1)}, bf16[80,640]{1,0:T(8,128)(2,1)S(1)}, u32[]{:S(2)}, u32[]{:S(2)}) %collective-permute-start) | collective-permute-done | bytes 102432 | tf_op jit(solution)/shard_map/ppermute | solution.py:64
  28.6 1.4 %collective-permute-start.3 = (bf16[2,80,640]{2,1,0:T(8,128)(2,1)S(1)}, bf16[2,80,640]{2,1,0:T(8,128)(2,1)S(1)}, u32[]{:S(2)}, u32[]{:S(2)}) collective-permute-start(bf16[2,80,640]{2,1,0:T(8,128)(2,1)S(1)} %get-tuple-element.6), channel_id=1, source_target_pairs={{0,96},{32,0},{64,32},{96,64},{1,97},{33,1},{65,33},{97,65},{2,98}... | collective-permute-start | bytes 614408 | tf_op jit(solution)/shard_map/ppermute | solution.py:65
  30.1 1.3 %collective-permute-start.2 = (bf16[2,80,640]{2,1,0:T(8,128)(2,1)S(1)}, bf16[2,80,640]{2,1,0:T(8,128)(2,1)S(1)}, u32[]{:S(2)}, u32[]{:S(2)}) collective-permute-start(bf16[2,80,640]{2,1,0:T(8,128)(2,1)S(1)} %get-tuple-element.6), channel_id=1, source_target_pairs={{0,64},{32,96},{64,0},{96,32},{1,65},{33,97},{65,1},{97,33},{2,66}... | collective-permute-start | bytes 614408 | tf_op jit(solution)/shard_map/ppermute | solution.py:65
  31.3 0.0 collective-permute-start.1
  31.4 5.3 %collective-permute-done.3 = bf16[2,80,640]{2,1,0:T(8,128)(2,1)S(1)} collective-permute-done((bf16[2,80,640]{2,1,0:T(8,128)(2,1)S(1)}, bf16[2,80,640]{2,1,0:T(8,128)(2,1)S(1)}, u32[]{:S(2)}, u32[]{:S(2)}) %collective-permute-start.3) | collective-permute-done | bytes 204832 | tf_op jit(solution)/shard_map/ppermute | solution.py:65
  36.7 2.9 %collective-permute-done.2 = bf16[2,80,640]{2,1,0:T(8,128)(2,1)S(1)} collective-permute-done((bf16[2,80,640]{2,1,0:T(8,128)(2,1)S(1)}, bf16[2,80,640]{2,1,0:T(8,128)(2,1)S(1)}, u32[]{:S(2)}, u32[]{:S(2)}) %collective-permute-start.2) | collective-permute-done | bytes 204832 | tf_op jit(solution)/shard_map/ppermute | solution.py:65
  39.6 2.4 %collective-permute-done.1 = bf16[2,80,640]{2,1,0:T(8,128)(2,1)S(1)} collective-permute-done((bf16[2,80,640]{2,1,0:T(8,128)(2,1)S(1)}, bf16[2,80,640]{2,1,0:T(8,128)(2,1)S(1)}, u32[]{:S(2)}, u32[]{:S(2)}) %collective-permute-start.1) | collective-permute-done | bytes 204832 | tf_op jit(solution)/shard_map/ppermute | solution.py:65
  42.0 0.1 pad_maximum_fusion.own
  42.1 0.0 copy-start.2
  42.1 0.1 collective-permute-start.4
  42.2 2.3 %collective-permute-done.4.other = bf16[4,2,80,640]{3,2,1,0:T(8,128)(2,1)S(1)} collective-permute-done((bf16[4,2,80,640]{3,2,1,0:T(8,128)(2,1)S(1)}, bf16[4,2,80,640]{3,2,1,0:T(8,128)(2,1)S(1)}, u32[]{:S(2)}, u32[]{:S(2)}) %collective-permute-start.4) | collective-permute-done | bytes 819232 | tf_op jit(solution)/shard_map/ppermute | solution.py:66
  44.6 0.0 copy-done.2
  44.6 0.0 copy-start.3
  44.6 0.9 copy-done.3
  45.5 8.6 %product.1 = s16[16,304,128]{2,1,0:T(8,128)(2,1)} custom-call(bf16[4,2,80,640]{3,2,1,0:T(8,128)(2,1)} %copy-done.2, bf16[4,2,80,640]{3,2,1,0:T(8,128)(2,1)} %copy-done.3, bf16[2048,2560]{1,0:T(8,128)(2,1)} %integrals.1), custom_call_target="tpu_custom_call" | custom-call | tf_op jit(solution)/shard_map/product/pallas_call | solution.py:131
  54.1 0.0 copy-start.4
  54.1 8.7 %all-to-all-start.1 = ((s16[16,304,128]{2,1,0:T(8,128)(2,1)}), s16[16,304,128]{2,1,0:T(8,128)(2,1)S(1)}, u32[]{:S(2)}, u32[]{:S(2)}) async-start(s16[16,304,128]{2,1,0:T(8,128)(2,1)} %product.1), calls=%async_computation.1 | async-start | bytes 2490368 | tf_op jit(solution)/shard_map/all_to_all | solution.py:145
  62.8 0.0 copy-done.4
  62.8 0.6 fusion.1
  64.7 28.8 %all-to-all-done.1.got = s16[16,304,128]{2,1,0:T(8,128)(2,1)S(1)} async-done(((s16[16,304,128]{2,1,0:T(8,128)(2,1)}), s16[16,304,128]{2,1,0:T(8,128)(2,1)S(1)}, u32[]{:S(2)}, u32[]{:S(2)}) %all-to-all-start.1) | async-done | bytes 1245216 | tf_op jit(solution)/shard_map/all_to_all | solution.py:145
  93.6 1.1 %sum.1 = f32[3,100,128]{2,1,0:T(8,128)} custom-call(s16[16,304,128]{2,1,0:T(8,128)(2,1)S(1)} %all-to-all-done.1.got, f32[1,128]{1,0:T(1,128)S(1)} %compare_convert_fusion.live), custom_call_target="tpu_custom_call" | custom-call | tf_op jit(solution)/shard_map/sum/pallas_call | solution.py:149
  (2 shorter events, 0.0 us)
Async XLA Ops:
  0.0 1.0 %copy-start = (bf16[100,2560]{1,0:T(8,128)(2,1)S(1)}, bf16[100,2560]{1,0:T(8,128)(2,1)}, u32[]{:S(2)}) copy-start(bf16[100,2560]{1,0:T(8,128)(2,1)} %panel.1) | copy-start | bytes 1536004
  1.0 20.5 %copy-start.1 = (s32[3]{0:T(128)S(1)}, s32[3]{0:T(128)}, u32[]{:S(2)}) copy-start(s32[3]{0:T(128)} %owner.1) | copy-start | bytes 40
  22.1 6.5 %collective-permute-start = (bf16[80,640]{1,0:T(8,128)(2,1)S(1)}, bf16[80,640]{1,0:T(8,128)(2,1)S(1)}, u32[]{:S(2)}, u32[]{:S(2)}) collective-permute-start(bf16[80,640]{1,0:T(8,128)(2,1)S(1)} %pick.1), channel_id=1, source_target_pairs={{0,128},{128,0},{1,129},{129,1},{2,130},{130,2},{3,131},{131,3},{4... | collective-permute-start | bytes 307208 | tf_op jit(solution)/shard_map/ppermute | solution.py:64
  28.6 8.1 %collective-permute-start.3 = (bf16[2,80,640]{2,1,0:T(8,128)(2,1)S(1)}, bf16[2,80,640]{2,1,0:T(8,128)(2,1)S(1)}, u32[]{:S(2)}, u32[]{:S(2)}) collective-permute-start(bf16[2,80,640]{2,1,0:T(8,128)(2,1)S(1)} %get-tuple-element.6), channel_id=1, source_target_pairs={{0,96},{32,0},{64,32},{96,64},{1,97},{33,1},{65,33},{97,65},{2,98}... | collective-permute-start | bytes 614408 | tf_op jit(solution)/shard_map/ppermute | solution.py:65
  30.1 9.5 %collective-permute-start.2 = (bf16[2,80,640]{2,1,0:T(8,128)(2,1)S(1)}, bf16[2,80,640]{2,1,0:T(8,128)(2,1)S(1)}, u32[]{:S(2)}, u32[]{:S(2)}) collective-permute-start(bf16[2,80,640]{2,1,0:T(8,128)(2,1)S(1)} %get-tuple-element.6), channel_id=1, source_target_pairs={{0,64},{32,96},{64,0},{96,32},{1,65},{33,97},{65,1},{97,33},{2,66}... | collective-permute-start | bytes 614408 | tf_op jit(solution)/shard_map/ppermute | solution.py:65
  31.3 10.7 %collective-permute-start.1 = (bf16[2,80,640]{2,1,0:T(8,128)(2,1)S(1)}, bf16[2,80,640]{2,1,0:T(8,128)(2,1)S(1)}, u32[]{:S(2)}, u32[]{:S(2)}) collective-permute-start(bf16[2,80,640]{2,1,0:T(8,128)(2,1)S(1)} %get-tuple-element.6), channel_id=1, source_target_pairs={{0,32},{32,64},{64,96},{96,0},{1,33},{33,65},{65,97},{97,1},{2,34}... | collective-permute-start | bytes 614408 | tf_op jit(solution)/shard_map/ppermute | solution.py:65
  42.1 2.4 %copy-start.2 = (bf16[4,2,80,640]{3,2,1,0:T(8,128)(2,1)}, bf16[4,2,80,640]{3,2,1,0:T(8,128)(2,1)S(1)}, u32[]{:S(2)}) copy-start(bf16[4,2,80,640]{3,2,1,0:T(8,128)(2,1)S(1)} %pad_maximum_fusion.own) | copy-start | bytes 2457604
  42.1 2.4 %collective-permute-start.4 = (bf16[4,2,80,640]{3,2,1,0:T(8,128)(2,1)S(1)}, bf16[4,2,80,640]{3,2,1,0:T(8,128)(2,1)S(1)}, u32[]{:S(2)}, u32[]{:S(2)}) collective-permute-start(bf16[4,2,80,640]{3,2,1,0:T(8,128)(2,1)S(1)} %pad_maximum_fusion.own), channel_id=1, source_target_pairs={{0,16},{16,0},{1,17},{17,1},{2,18},{18,2},{3,19},{19,3},{4,20},{20... | collective-permute-start | bytes 2457608 | tf_op jit(solution)/shard_map/ppermute | solution.py:66
  44.6 0.9 copy-start.3
  54.1 8.7 %copy-start.4 = (s32[17]{0:T(128)S(1)}, s32[17]{0:T(128)}, u32[]{:S(2)}) copy-start(s32[17]{0:T(128)} %param.6) | copy-start | bytes 208
  54.1 39.5 %all-to-all-start.1 = ((s16[16,304,128]{2,1,0:T(8,128)(2,1)}), s16[16,304,128]{2,1,0:T(8,128)(2,1)S(1)}, u32[]{:S(2)}, u32[]{:S(2)}) async-start(s16[16,304,128]{2,1,0:T(8,128)(2,1)} %product.1), calls=%async_computation.1 | async-start | bytes 2490368 | tf_op jit(solution)/shard_map/all_to_all | solution.py:145

commit v4 on v3

--- a/solution.py
+++ b/solution.py
@@ -16,6 +16,7 @@
 TALL = 304
 GROUPS = ((0, 80), (80, 160), (160, 240), (240, TALL))
 KB = 640
+TILES = KB // 128
 WIDE = 512
 SLABS = 4
 CODE = 2.0**14 * (1 - 2.0**-13)
@@ -23,7 +24,7 @@
 SMEM = pl.BlockSpec(memory_space=pltpu.SMEM)
 HBM = pl.BlockSpec(memory_space=pltpu.HBM)
 SMALL = pltpu.CompilerParams(vmem_limit_bytes=8 << 20)
-LARGE = pltpu.CompilerParams(vmem_limit_bytes=54 << 20)
+LARGE = pltpu.CompilerParams(vmem_limit_bytes=46 << 20)
 
 
 def shift(size, by):
@@ -33,20 +34,22 @@
 def cut_kernel(panel, pieces):
     for yh in range(2):
         for core in range(2):
-            rows = slice((yh * 2 + core) * RB, (yh * 2 + core + 1) * RB)
             for x in range(4):
-                pieces[yh * 8 + x * 2 + core, pl.ds(0, RB), :] = panel[rows, x * KB : (x + 1) * KB]
+                for t in range(TILES):
+                    block = panel[pl.ds((yh * 2 + core) * RB, RB), pl.ds(x * KB + t * 128, 128)]
+                    pieces[yh * 8 + x * 2 + core, pl.ds(t * RB, RB), :] = block
 
 
 def pick_kernel(owner, held, mine):
     for s in range(STEPS):
-        mine[pl.ds(s * RB, RB), :] = held[owner[s], pl.ds(0, RB), :]
+        for t in range(TILES):
+            mine[pl.ds(s * RB, RB), pl.ds(t * 128, 128)] = held[owner[s], pl.ds(t * RB, RB), :]
 
 
 def gather_panels(amplitudes, panel_owner):
     pieces = pl.pallas_call(
         cut_kernel,
-        out_shape=jax.ShapeDtypeStruct((16, 32, KB), jnp.bfloat16),
+        out_shape=jax.ShapeDtypeStruct((16, 128, 128), jnp.bfloat16),
         in_specs=[VMEM],
         out_specs=VMEM,
         compiler_params=SMALL,

time: 94.9 us -> 91.5 us (0.964)
  Pallas kernels: 10.4 us -> 9.18 us
  blocking collectives: 20.4 us -> 19.2 us
    pallas_call x1, Pallas kernels: 8.62 us -> 7.22 us  [per_device(): pl.pallas_call(product_kernel, out_shape=jax.ShapeDtypeStruct((16, TALL,...]
    all_to_all x1, blocking collectives: 20.4 us -> 19.2 us  [gather_panels(): held = lax.all_to_all(pieces, ROW, 0, 0)]
    unnamed x10 -> x6, local copies, waits for them, and re-layouts: 1.96 us -> 1.05 us
where the time goes in v4:
time: 91.5 us; the launch traced here: 91.3 us
  waiting for transfers between devices  48 us (52%)
  blocking collectives  19.2 us (21%)
  starting transfers between devices  11.8 us (13%)
  Pallas kernels  9.18 us (10%)
  local copies, waits for them, and re-layouts  1.67 us (2%)
  between operations  1.34 us (1%)
    all_to_all x1, waiting for transfers between devices, per_device(): got = lax.all_to_all(codes, COL, 0, 0)  28.8 us
    all_to_all x1, blocking collectives, gather_panels(): held = lax.all_to_all(pieces, ROW, 0, 0)  19.2 us
    ppermute x3, waiting for transfers between devices, gather_panels(): lax.ppermute(two, 'x', shift(4, d))  11.2 us
    all_to_all x1, starting transfers between devices, per_device(): got = lax.all_to_all(codes, COL, 0, 0)  8.71 us
    pallas_call x1, Pallas kernels, per_device(): pl.pallas_call(product_kernel, out_shape=jax.ShapeDtypeStruct((16, TALL,...  7.22 us
    ppermute x1, waiting for transfers between devices, gather_panels(): two = jnp.stack([mine, lax.ppermute(mine, 'yh', shift(2, 1))])  5.61 us
    ppermute x1, waiting for transfers between devices, gather_panels(): return (eight, lax.ppermute(eight, 'core', shift(2, 1)))  2.32 us
    ppermute x3, starting transfers between devices, gather_panels(): lax.ppermute(two, 'x', shift(4, d))  2.3 us
  transfers between devices with their start and end apart: 6, of which 6 were waited for; matrix products, arithmetic and copies ran while one was open for 1% of the time, Pallas kernels for 0%

profile of v4, /device:TPU:32, one launch (start us, length us, event | category | flops | bytes accessed | tf_op | source)
XLA Modules:
  0.0 91.3 jit_solution(15229283944641450933)
XLA Ops:
  0.0 0.0 copy-start
  0.0 1.0 %copy-done = bf16[100,2560]{1,0:T(8,128)(2,1)S(1)} copy-done((bf16[100,2560]{1,0:T(8,128)(2,1)S(1)}, bf16[100,2560]{1,0:T(8,128)(2,1)}, u32[]{:S(2)}) %copy-start) | copy-done | bytes 512024
  1.0 0.0 copy-start.1
  1.0 0.3 cut.1
  1.3 19.2 %all_to_all.10.held = bf16[16,128,128]{2,1,0:T(8,128)(2,1)S(1)} all-to-all(bf16[16,128,128]{2,1,0:T(8,128)(2,1)S(1)} %cut.1), channel_id=1, replica_groups=mesh['yh'=2,'x'=4,'core'=2,'yl'=2,'z'=8] {'yh','x','core'}, dimensions={0} | all-to-all | bytes 1048576 | tf_op jit(solution)/shard_map/all_to_all | solution.py:58
  20.5 0.0 copy-done.1
  20.5 0.6 pick.1
  21.1 0.6 collective-permute-start
  21.8 5.6 %collective-permute-done = bf16[80,640]{1,0:T(8,128)(2,1)S(1)} collective-permute-done((bf16[80,640]{1,0:T(8,128)(2,1)S(1)}, bf16[80,640]{1,0:T(8,128)(2,1)S(1)}, u32[]{:S(2)}, u32[]{:S(2)}) %collective-permute-start) | collective-permute-done | bytes 102432 | tf_op jit(solution)/shard_map/ppermute | solution.py:67
  27.4 1.1 %collective-permute-start.3 = (bf16[2,80,640]{2,1,0:T(8,128)(2,1)S(1)}, bf16[2,80,640]{2,1,0:T(8,128)(2,1)S(1)}, u32[]{:S(2)}, u32[]{:S(2)}) collective-permute-start(bf16[2,80,640]{2,1,0:T(8,128)(2,1)S(1)} %get-tuple-element.6), channel_id=1, source_target_pairs={{0,96},{32,0},{64,32},{96,64},{1,97},{33,1},{65,33},{97,65},{2,98}... | collective-permute-start | bytes 614408 | tf_op jit(solution)/shard_map/ppermute | solution.py:68
  28.5 0.4 collective-permute-start.2
  28.9 0.8 collective-permute-start.1
  29.7 7.5 %collective-permute-done.3 = bf16[2,80,640]{2,1,0:T(8,128)(2,1)S(1)} collective-permute-done((bf16[2,80,640]{2,1,0:T(8,128)(2,1)S(1)}, bf16[2,80,640]{2,1,0:T(8,128)(2,1)S(1)}, u32[]{:S(2)}, u32[]{:S(2)}) %collective-permute-start.3) | collective-permute-done | bytes 204832 | tf_op jit(solution)/shard_map/ppermute | solution.py:68
  37.2 0.8 collective-permute-done.2
  38.1 2.8 %collective-permute-done.1 = bf16[2,80,640]{2,1,0:T(8,128)(2,1)S(1)} collective-permute-done((bf16[2,80,640]{2,1,0:T(8,128)(2,1)S(1)}, bf16[2,80,640]{2,1,0:T(8,128)(2,1)S(1)}, u32[]{:S(2)}, u32[]{:S(2)}) %collective-permute-start.1) | collective-permute-done | bytes 204832 | tf_op jit(solution)/shard_map/ppermute | solution.py:68
  40.9 0.1 pad_maximum_fusion.own
  41.0 0.1 collective-permute-start.4
  41.2 2.3 %collective-permute-done.4.other = bf16[4,2,80,640]{3,2,1,0:T(8,128)(2,1)S(1)} collective-permute-done((bf16[4,2,80,640]{3,2,1,0:T(8,128)(2,1)S(1)}, bf16[4,2,80,640]{3,2,1,0:T(8,128)(2,1)S(1)}, u32[]{:S(2)}, u32[]{:S(2)}) %collective-permute-start.4) | collective-permute-done | bytes 819232 | tf_op jit(solution)/shard_map/ppermute | solution.py:69
  43.5 7.2 %product.1 = s16[16,304,128]{2,1,0:T(8,128)(2,1)} custom-call(bf16[4,2,80,640]{3,2,1,0:T(8,128)(2,1)S(1)} %pad_maximum_fusion.own, bf16[4,2,80,640]{3,2,1,0:T(8,128)(2,1)S(1)} %collective-permute-done.4.other, bf16[2048,2560]{1,0:T(8,128)(2,1)} %integrals.1), custom_call_target="tpu_custom_call" | custom-call | tf_op jit(solution)/shard_map/product/pallas_call | solution.py:134
  50.7 0.0 copy-start.2
  50.7 8.7 %all-to-all-start.1 = ((s16[16,304,128]{2,1,0:T(8,128)(2,1)}), s16[16,304,128]{2,1,0:T(8,128)(2,1)S(1)}, u32[]{:S(2)}, u32[]{:S(2)}) async-start(s16[16,304,128]{2,1,0:T(8,128)(2,1)} %product.1), calls=%async_computation.1 | async-start | bytes 2490368 | tf_op jit(solution)/shard_map/all_to_all | solution.py:148
  59.4 0.0 copy-done.2
  59.4 0.6 fusion.1
  61.3 28.8 %all-to-all-done.1.got = s16[16,304,128]{2,1,0:T(8,128)(2,1)S(1)} async-done(((s16[16,304,128]{2,1,0:T(8,128)(2,1)}), s16[16,304,128]{2,1,0:T(8,128)(2,1)S(1)}, u32[]{:S(2)}, u32[]{:S(2)}) %all-to-all-start.1) | async-done | bytes 1245216 | tf_op jit(solution)/shard_map/all_to_all | solution.py:148
  90.2 1.1 %sum.1 = f32[3,100,128]{2,1,0:T(8,128)} custom-call(s16[16,304,128]{2,1,0:T(8,128)(2,1)S(1)} %all-to-all-done.1.got, f32[1,128]{1,0:T(1,128)S(1)} %compare_convert_fusion.live), custom_call_target="tpu_custom_call" | custom-call | tf_op jit(solution)/shard_map/sum/pallas_call | solution.py:152
  (2 shorter events, 0.0 us)
Async XLA Ops:
  0.0 1.0 %copy-start = (bf16[100,2560]{1,0:T(8,128)(2,1)S(1)}, bf16[100,2560]{1,0:T(8,128)(2,1)}, u32[]{:S(2)}) copy-start(bf16[100,2560]{1,0:T(8,128)(2,1)} %panel.1) | copy-start | bytes 1536004
  1.0 19.5 %copy-start.1 = (s32[3]{0:T(128)S(1)}, s32[3]{0:T(128)}, u32[]{:S(2)}) copy-start(s32[3]{0:T(128)} %owner.1) | copy-start | bytes 40
  21.1 6.3 %collective-permute-start = (bf16[80,640]{1,0:T(8,128)(2,1)S(1)}, bf16[80,640]{1,0:T(8,128)(2,1)S(1)}, u32[]{:S(2)}, u32[]{:S(2)}) collective-permute-start(bf16[80,640]{1,0:T(8,128)(2,1)S(1)} %pick.1), channel_id=1, source_target_pairs={{0,128},{128,0},{1,129},{129,1},{2,130},{130,2},{3,131},{131,3},{4... | collective-permute-start | bytes 307208 | tf_op jit(solution)/shard_map/ppermute | solution.py:67
  27.4 9.8 %collective-permute-start.3 = (bf16[2,80,640]{2,1,0:T(8,128)(2,1)S(1)}, bf16[2,80,640]{2,1,0:T(8,128)(2,1)S(1)}, u32[]{:S(2)}, u32[]{:S(2)}) collective-permute-start(bf16[2,80,640]{2,1,0:T(8,128)(2,1)S(1)} %get-tuple-element.6), channel_id=1, source_target_pairs={{0,96},{32,0},{64,32},{96,64},{1,97},{33,1},{65,33},{97,65},{2,98}... | collective-permute-start | bytes 614408 | tf_op jit(solution)/shard_map/ppermute | solution.py:68
  28.5 9.6 %collective-permute-start.2 = (bf16[2,80,640]{2,1,0:T(8,128)(2,1)S(1)}, bf16[2,80,640]{2,1,0:T(8,128)(2,1)S(1)}, u32[]{:S(2)}, u32[]{:S(2)}) collective-permute-start(bf16[2,80,640]{2,1,0:T(8,128)(2,1)S(1)} %get-tuple-element.6), channel_id=1, source_target_pairs={{0,64},{32,96},{64,0},{96,32},{1,65},{33,97},{65,1},{97,33},{2,66}... | collective-permute-start | bytes 614408 | tf_op jit(solution)/shard_map/ppermute | solution.py:68
  28.9 12.0 %collective-permute-start.1 = (bf16[2,80,640]{2,1,0:T(8,128)(2,1)S(1)}, bf16[2,80,640]{2,1,0:T(8,128)(2,1)S(1)}, u32[]{:S(2)}, u32[]{:S(2)}) collective-permute-start(bf16[2,80,640]{2,1,0:T(8,128)(2,1)S(1)} %get-tuple-element.6), channel_id=1, source_target_pairs={{0,32},{32,64},{64,96},{96,0},{1,33},{33,65},{65,97},{97,1},{2,34}... | collective-permute-start | bytes 614408 | tf_op jit(solution)/shard_map/ppermute | solution.py:68
  41.0 2.4 %collective-permute-start.4 = (bf16[4,2,80,640]{3,2,1,0:T(8,128)(2,1)S(1)}, bf16[4,2,80,640]{3,2,1,0:T(8,128)(2,1)S(1)}, u32[]{:S(2)}, u32[]{:S(2)}) collective-permute-start(bf16[4,2,80,640]{3,2,1,0:T(8,128)(2,1)S(1)} %pad_maximum_fusion.own), channel_id=1, source_target_pairs={{0,16},{16,0},{1,17},{17,1},{2,18},{18,2},{3,19},{19,3},{4,20},{20... | collective-permute-start | bytes 2457608 | tf_op jit(solution)/shard_map/ppermute | solution.py:69
  50.7 8.7 %copy-start.2 = (s32[17]{0:T(128)S(1)}, s32[17]{0:T(128)}, u32[]{:S(2)}) copy-start(s32[17]{0:T(128)} %param.6) | copy-start | bytes 208
  50.7 39.4 %all-to-all-start.1 = ((s16[16,304,128]{2,1,0:T(8,128)(2,1)}), s16[16,304,128]{2,1,0:T(8,128)(2,1)S(1)}, u32[]{:S(2)}, u32[]{:S(2)}) async-start(s16[16,304,128]{2,1,0:T(8,128)(2,1)} %product.1), calls=%async_computation.1 | async-start | bytes 2490368 | tf_op jit(solution)/shard_map/all_to_all | solution.py:148

commit v5 on v4

--- a/solution.py
+++ b/solution.py
@@ -17,12 +17,13 @@
 GROUPS = ((0, 80), (80, 160), (160, 240), (240, TALL))
 KB = 640
 TILES = KB // 128
-WIDE = 512
-SLABS = 4
+FAR = (4, 3, 5)
+NEAR = (2, 6, 1, 7, 0)
 CODE = 2.0**14 * (1 - 2.0**-13)
 VMEM = pl.BlockSpec(memory_space=pltpu.VMEM)
 SMEM = pl.BlockSpec(memory_space=pltpu.SMEM)
 HBM = pl.BlockSpec(memory_space=pltpu.HBM)
+ANY = pl.BlockSpec(memory_space=pl.ANY)
 SMALL = pltpu.CompilerParams(vmem_limit_bytes=8 << 20)
 LARGE = pltpu.CompilerParams(vmem_limit_bytes=46 << 20)
 
@@ -67,6 +68,10 @@
     two = jnp.stack([mine, lax.ppermute(mine, "yh", shift(2, 1))])
     eight = jnp.stack([two] + [lax.ppermute(two, "x", shift(4, d)) for d in range(1, 4)])
     return eight, lax.ppermute(eight, "core", shift(2, 1))
+
+
+def last_rows():
+    return lax.broadcasted_iota(jnp.int32, (16, SLOT), 0) + TALL - 16
 
 
 def encode(rows, out, at):
@@ -78,12 +83,12 @@
         exponents.append(exponent)
         code = jnp.round(block * (jnp.exp2(-exponent) * CODE))
         if hi == TALL:
-            row = lax.broadcasted_iota(jnp.int32, (16, SLOT), 0) + TALL - 16
             last = code[-16:]
             for g, e in enumerate(exponents):
-                last = jnp.where(row == ROWS + g, e, last)
+                last = jnp.where(last_rows() == ROWS + g, e, last)
             code = jnp.concatenate([code[:-16], last])
-        out[at, pl.ds(lo, hi - lo), :] = code.astype(jnp.int32).astype(jnp.int16)
+        rows_out = (pl.ds(lo, hi - lo), slice(None))
+        out[rows_out if at is None else (at,) + rows_out] = code.astype(jnp.int32).astype(jnp.int16)
 
 
 def decode(codes, lo, hi, group):
@@ -91,34 +96,92 @@
     return codes[pl.ds(lo, hi - lo), :].astype(jnp.int32).astype(jnp.float32) * (scale * (1 / CODE))
 
 
-def product_kernel(own, other, integrals, out, left, slabs, acc, sems):
+def fetch(integrals, slabs, sems, yl, places):
+    z = lax.axis_index("z")
+    copies = []
+    for n, d in enumerate(places):
+        rows = pl.ds(pl.multiple_of((yl * 8 + lax.rem(z + d, 8)) * SLOT, SLOT), SLOT)
+        copies.append(pltpu.make_async_copy(integrals.at[rows], slabs.at[pl.ds(n * SLOT, SLOT)], sems.at[n]))
+        copies[-1].start()
+    return copies
+
+
+def multiply(left, slabs, copies, acc):
+    count, n = len(copies), 0
+    for some in (count - 3 * ((count - 1) // 3),) + (3,) * ((count - 1) // 3):
+        for copy in copies[n : n + some]:
+            copy.wait()
+        columns = pl.ds(n * SLOT, some * SLOT)
+        acc[:, columns] = lax.dot_general(
+            left[...], slabs[columns, :], (((1,), (1,)), ((), ())), preferred_element_type=jnp.float32
+        )
+        n += some
+
+
+def encode_all(acc, out):
+    for n in range(out.shape[0]):
+        encode(lambda lo, hi: acc[pl.ds(lo, hi - lo), pl.ds(n * SLOT, SLOT)], out, n)
+
+
+def away_far_kernel(own, other, integrals, out, left, slabs, acc, sems):
     x = lax.axis_index("x")
-    copies = []
-    for n in range(SLABS):
-        copies.append(pltpu.make_async_copy(integrals.at[pl.ds(n * WIDE, WIDE)], slabs.at[n], sems.at[n]))
-        copies[-1].start()
+    copies = fetch(integrals, slabs, sems, 1 - lax.axis_index("yl"), FAR)
     left[pl.ds(TALL - 16, 16), :] = jnp.zeros((16, 4 * KB), jnp.bfloat16)
     for back in range(4):
         columns = pl.ds(pl.multiple_of(lax.rem(x - back + 4, 4) * KB, KB), KB)
         for core, piece in enumerate((own, other)):
             for yh in range(2):
                 left[pl.ds((core * 2 + yh) * USED, USED), columns] = piece[back, yh, pl.ds(0, USED), :]
-    for n in range(SLABS):
-        copies[n].wait()
-        acc[n % 2] = lax.dot_general(
-            left[...], slabs[n], (((1,), (1,)), ((), ())), preferred_element_type=jnp.float32
-        )
-        for d in range(WIDE // SLOT):
-            encode(lambda lo, hi: acc[n % 2, pl.ds(lo, hi - lo), pl.ds(d * SLOT, SLOT)], out, n * 4 + d)
-
-
-def sum_kernel(got, live, out, total):
-    yh, core = lax.axis_index("yh"), lax.axis_index("core")
+    multiply(left, slabs, copies, acc)
+    encode_all(acc, out)
+
+
+def away_near_kernel(left, integrals, out, slabs, acc, sems):
+    multiply(left, slabs, fetch(integrals, slabs, sems, 1 - lax.axis_index("yl"), NEAR), acc)
+    encode_all(acc, out)
+
+
+def home_kernel(left, integrals, after, out, slabs, sems):
+    multiply(left, slabs, fetch(integrals, slabs, sems, lax.axis_index("yl"), FAR + NEAR), out)
+
+
+def added(got, kept, n, column):
+    sums = []
     for g, (lo, hi) in enumerate(GROUPS):
-        part = decode(got.at[0], lo, hi, g)
-        for k in range(1, 16):
-            part = part + decode(got.at[k], lo, hi, g)
-        total[pl.ds(lo, hi - lo), :] = part * live[...]
+        part = kept[pl.ds(lo, hi - lo), pl.ds(column * SLOT, SLOT)] + decode(got.at[n], lo, hi, g)
+        if hi == TALL:
+            part = jnp.concatenate([part[:-16], jnp.where(last_rows() < ROWS, part[-16:], 0.0)])
+        sums.append(part)
+    return sums
+
+
+def meet_far_kernel(got, kept, *outs):
+    for n, out in enumerate(outs):
+        sums = added(got, kept, n, n)
+        encode(lambda lo, hi: sums[GROUPS.index((lo, hi))], out, None)
+
+
+def meet_near_kernel(got, kept, after, *outs):
+    for n, out in enumerate(outs):
+        sums = added(got, kept, n, len(FAR) + n)
+        if NEAR[n] == 0:
+            for (lo, hi), part in zip(GROUPS, sums):
+                out[pl.ds(lo, hi - lo), :] = part
+        else:
+            encode(lambda lo, hi: sums[GROUPS.index((lo, hi))], out, None)
+
+
+def sum_kernel(*refs):
+    offsets, *got, kept, out, total = refs
+    yh, x, core, yl, z = (lax.axis_index(a) for a in ROW + COL)
+    row = (yh * 4 + x) * 2 + core
+    slot = (yl * 8 + z) * SLOT + lax.broadcasted_iota(jnp.int32, (1, SLOT), 1)
+    live = (slot < offsets[row + 1] - offsets[row]).astype(jnp.float32)
+    for g, (lo, hi) in enumerate(GROUPS):
+        part = kept[pl.ds(lo, hi - lo), :]
+        for codes in got:
+            part = part + decode(codes, lo, hi, g)
+        total[pl.ds(lo, hi - lo), :] = part * live
     for b in range(4):
         rb = lax.rem(yh + b % 2, 2) * 2 + lax.rem(core + b // 2, 2)
         for case in range(4):
@@ -131,33 +194,84 @@
 
 def per_device(amplitudes, integrals, row_offsets, panel_owner):
     own, other = gather_panels(amplitudes, panel_owner)
-    codes = pl.pallas_call(
-        product_kernel,
-        out_shape=jax.ShapeDtypeStruct((16, TALL, SLOT), jnp.int16),
+    def codes(*n):
+        return jax.ShapeDtypeStruct(n + (TALL, SLOT), jnp.int16)
+
+    def cost(n):
+        return pl.CostEstimate(
+            flops=2 * TALL * 4 * KB * n * SLOT, bytes_accessed=8 * KB * n * SLOT, transcendentals=0
+        )
+
+    def room(n):
+        return [pltpu.VMEM((n * SLOT, 4 * KB), jnp.bfloat16)]
+
+    def wide(n):
+        return [pltpu.VMEM((TALL, n * SLOT), jnp.float32)]
+
+    def sems(n):
+        return [pltpu.SemaphoreType.DMA((n,))]
+
+    far, near = len(FAR), len(NEAR)
+    away_far, left = pl.pallas_call(
+        away_far_kernel,
+        out_shape=[codes(far), jax.ShapeDtypeStruct((TALL, 4 * KB), jnp.bfloat16)],
         in_specs=[VMEM, VMEM, HBM],
-        out_specs=VMEM,
-        scratch_shapes=[
-            pltpu.VMEM((TALL, 4 * KB), jnp.bfloat16),
-            pltpu.VMEM((SLABS, WIDE, 4 * KB), jnp.bfloat16),
-            pltpu.VMEM((2, TALL, WIDE), jnp.float32),
-            pltpu.SemaphoreType.DMA((SLABS,)),
-        ],
+        out_specs=[VMEM, VMEM],
+        scratch_shapes=room(far) + wide(far) + sems(far),
         compiler_params=LARGE,
-        name="product",
+        cost_estimate=cost(far),
+        name="away_far",
     )(own, other, integrals)
-    got = lax.all_to_all(codes, COL, 0, 0)
-    own_row = lax.axis_index(ROW)
-    slot = lax.axis_index(COL) * SLOT + jnp.arange(SLOT, dtype=jnp.int32)
-    live = (slot < row_offsets[own_row + 1] - row_offsets[own_row]).astype(jnp.float32)[None, :]
+    got_far = lax.ppermute(away_far, "yl", shift(2, 1))
+    away_near = pl.pallas_call(
+        away_near_kernel,
+        out_shape=codes(near),
+        in_specs=[VMEM, HBM],
+        out_specs=VMEM,
+        scratch_shapes=room(near) + wide(near) + sems(near),
+        compiler_params=LARGE,
+        cost_estimate=cost(near),
+        name="away_near",
+    )(left, integrals)
+    kept = pl.pallas_call(
+        home_kernel,
+        out_shape=jax.ShapeDtypeStruct((TALL, 8 * SLOT), jnp.float32),
+        in_specs=[VMEM, HBM, ANY],
+        out_specs=VMEM,
+        scratch_shapes=room(8) + sems(8),
+        compiler_params=LARGE,
+        cost_estimate=cost(8),
+        name="home",
+    )(left, integrals, away_near)
+    got_far, away_near, kept = lax.optimization_barrier((got_far, away_near, kept))
+    got_near = lax.ppermute(away_near, "yl", shift(2, 1))
+    met_far = pl.pallas_call(
+        meet_far_kernel,
+        out_shape=[codes()] * far,
+        in_specs=[VMEM, VMEM],
+        out_specs=[VMEM] * far,
+        compiler_params=SMALL,
+        name="meet_far",
+    )(got_far, kept)
+    met_near = pl.pallas_call(
+        meet_near_kernel,
+        out_shape=[codes()] * (near - 1) + [jax.ShapeDtypeStruct((TALL, SLOT), jnp.float32)],
+        in_specs=[VMEM, VMEM, ANY],
+        out_specs=[VMEM] * near,
+        compiler_params=SMALL,
+        name="meet_near",
+    )(got_near, kept, met_far[0])
+    got = [lax.ppermute(c, "z", shift(8, d)) for c, d in zip(met_far, FAR)]
+    got += [lax.ppermute(c, "z", shift(8, d)) for c, d in zip(met_near, NEAR[:-1])]
     return pl.pallas_call(
         sum_kernel,
         out_shape=jax.ShapeDtypeStruct((STEPS, 4 * RB, SLOT), jnp.float32),
-        in_specs=[VMEM, VMEM],
+        in_specs=[SMEM] + [VMEM] * 8,
         out_specs=VMEM,
         scratch_shapes=[pltpu.VMEM((TALL, SLOT), jnp.float32)],
         compiler_params=SMALL,
         name="sum",
-    )(got, live)
+    )(row_offsets, *got, met_near[-1])
 
 
 def solution(mesh):

time: 91.5 us -> 77.3 us (0.84)
  waiting for transfers between devices: 48 us -> 19.4 us
  starting transfers between devices: 11.8 us -> 24.6 us
  Pallas kernels: 9.18 us -> 12.2 us
  between operations: 1.34 us -> 0.09 us
    all_to_all x1 -> x0, waiting for transfers between devices: 28.8 us -> none  [per_device(): got = lax.all_to_all(codes, COL, 0, 0)]
    ppermute x0 -> x9, starting transfers between devices: none -> 19.8 us  [the longest x3 11.4 us: per_device(): got = [lax.ppermute(c, 'z', shift(8, d)) for c, d in zip(met_far, FAR)]]
    all_to_all x1 -> x0, starting transfers between devices: 8.71 us -> none  [per_device(): got = lax.all_to_all(codes, COL, 0, 0)]
    ppermute x0 -> x9, waiting for transfers between devices: none -> 4.31 us  [the longest x4 2.88 us: per_device(): lax.ppermute(c, 'z', shift(8, d))]
    ppermute x3, waiting for transfers between devices: 11.2 us -> 7.12 us  [gather_panels(): lax.ppermute(two, 'x', shift(4, d))]
    pallas_call x1 -> x5, Pallas kernels: 7.22 us -> 9.91 us  [the longest x1 3.94 us: per_device(): pl.pallas_call(home_kernel, out_shape=jax.ShapeDtypeStruct((TALL, 8 * SLO...]
    ppermute x3, starting transfers between devices: 2.3 us -> 4.13 us  [gather_panels(): lax.ppermute(two, 'x', shift(4, d))]
  transfers between devices with their start and end apart: 6 -> 14, of which waited for: 6 -> 9; matrix products, arithmetic and copies ran while one was open for 1% -> 0% of each run, Pallas kernels for 0% -> 10%
where the time goes in v5:
time: 77.3 us; the launch traced here: 76.7 us
  starting transfers between devices  24.6 us (32%)
  waiting for transfers between devices  19.4 us (25%)
  blocking collectives  19.2 us (25%)
  Pallas kernels  12.2 us (16%)
  local copies, waits for them, and re-layouts  1.05 us (1%)
    all_to_all x1, blocking collectives, gather_panels(): held = lax.all_to_all(pieces, ROW, 0, 0)  19.2 us
    ppermute x3, starting transfers between devices, per_device(): got = [lax.ppermute(c, 'z', shift(8, d)) for c, d in zip(met_far, FAR)]  11.4 us
    ppermute x3, waiting for transfers between devices, gather_panels(): lax.ppermute(two, 'x', shift(4, d))  7.12 us
    ppermute x4, starting transfers between devices, per_device(): lax.ppermute(c, 'z', shift(8, d))  6.24 us
    ppermute x1, waiting for transfers between devices, gather_panels(): two = jnp.stack([mine, lax.ppermute(mine, 'yh', shift(2, 1))])  5.61 us
    ppermute x3, starting transfers between devices, gather_panels(): lax.ppermute(two, 'x', shift(4, d))  4.13 us
    pallas_call x1, Pallas kernels, per_device(): pl.pallas_call(home_kernel, out_shape=jax.ShapeDtypeStruct((TALL, 8 * SLO...  3.94 us
    pallas_call x1, Pallas kernels, per_device(): pl.pallas_call(away_near_kernel, out_shape=codes(near), in_specs=[VMEM, H...  2.99 us
  transfers between devices with their start and end apart: 14, of which 9 were waited for; matrix products, arithmetic and copies ran while one was open for 0% of the time, Pallas kernels for 10%

profile of v5, /device:TPU:32, one launch (start us, length us, event | category | flops | bytes accessed | tf_op | source)
XLA Modules:
  0.0 76.7 jit_solution(18375757387673149737)
XLA Ops:
  0.0 1.0 %copy-done = bf16[100,2560]{1,0:T(8,128)(2,1)S(1)} copy-done((bf16[100,2560]{1,0:T(8,128)(2,1)S(1)}, bf16[100,2560]{1,0:T(8,128)(2,1)}, u32[]{:S(2)}) %copy-start) | copy-done | bytes 512024
  1.0 0.3 cut.1
  1.3 19.2 %all_to_all.5.held = bf16[16,128,128]{2,1,0:T(8,128)(2,1)S(1)} all-to-all(bf16[16,128,128]{2,1,0:T(8,128)(2,1)S(1)} %cut.1), channel_id=1, replica_groups=mesh['yh'=2,'x'=4,'core'=2,'yl'=2,'z'=8] {'yh','x','core'}, dimensions={0} | all-to-all | bytes 1048576 | tf_op jit(solution)/shard_map/all_to_all | solution.py:59
  20.5 0.6 pick.1
  21.1 0.6 collective-permute-start
  21.8 5.6 %collective-permute-done = bf16[80,640]{1,0:T(8,128)(2,1)S(1)} collective-permute-done((bf16[80,640]{1,0:T(8,128)(2,1)S(1)}, bf16[80,640]{1,0:T(8,128)(2,1)S(1)}, u32[]{:S(2)}, u32[]{:S(2)}) %collective-permute-start) | collective-permute-done | bytes 102432 | tf_op jit(solution)/shard_map/ppermute | solution.py:68
  27.4 0.9 %collective-permute-start.2 = (bf16[2,80,640]{2,1,0:T(8,128)(2,1)S(1)}, bf16[2,80,640]{2,1,0:T(8,128)(2,1)S(1)}, u32[]{:S(2)}, u32[]{:S(2)}) collective-permute-start(bf16[2,80,640]{2,1,0:T(8,128)(2,1)S(1)} %get-tuple-element.32), channel_id=1, source_target_pairs={{0,64},{32,96},{64,0},{96,32},{1,65},{33,97},{65,1},{97,33},{2,66}... | collective-permute-start | bytes 614408 | tf_op jit(solution)/shard_map/ppermute | solution.py:69
  28.3 1.1 %collective-permute-start.1 = (bf16[2,80,640]{2,1,0:T(8,128)(2,1)S(1)}, bf16[2,80,640]{2,1,0:T(8,128)(2,1)S(1)}, u32[]{:S(2)}, u32[]{:S(2)}) collective-permute-start(bf16[2,80,640]{2,1,0:T(8,128)(2,1)S(1)} %get-tuple-element.32), channel_id=1, source_target_pairs={{0,32},{32,64},{64,96},{96,0},{1,33},{33,65},{65,97},{97,1},{2,34}... | collective-permute-start | bytes 614408 | tf_op jit(solution)/shard_map/ppermute | solution.py:69
  29.4 2.1 %collective-permute-start.3 = (bf16[2,80,640]{2,1,0:T(8,128)(2,1)S(1)}, bf16[2,80,640]{2,1,0:T(8,128)(2,1)S(1)}, u32[]{:S(2)}, u32[]{:S(2)}) collective-permute-start(bf16[2,80,640]{2,1,0:T(8,128)(2,1)S(1)} %get-tuple-element.32), channel_id=1, source_target_pairs={{0,96},{32,0},{64,32},{96,64},{1,97},{33,1},{65,33},{97,65},{2,98}... | collective-permute-start | bytes 614408 | tf_op jit(solution)/shard_map/ppermute | solution.py:69
  31.5 5.0 %collective-permute-done.2 = bf16[2,80,640]{2,1,0:T(8,128)(2,1)S(1)} collective-permute-done((bf16[2,80,640]{2,1,0:T(8,128)(2,1)S(1)}, bf16[2,80,640]{2,1,0:T(8,128)(2,1)S(1)}, u32[]{:S(2)}, u32[]{:S(2)}) %collective-permute-start.2) | collective-permute-done | bytes 204832 | tf_op jit(solution)/shard_map/ppermute | solution.py:69
  36.5 2.1 %collective-permute-done.1 = bf16[2,80,640]{2,1,0:T(8,128)(2,1)S(1)} collective-permute-done((bf16[2,80,640]{2,1,0:T(8,128)(2,1)S(1)}, bf16[2,80,640]{2,1,0:T(8,128)(2,1)S(1)}, u32[]{:S(2)}, u32[]{:S(2)}) %collective-permute-start.1) | collective-permute-done | bytes 204832 | tf_op jit(solution)/shard_map/ppermute | solution.py:69
  38.7 0.1 pad_maximum_fusion.own
  38.8 0.1 collective-permute-start.4
  38.9 2.3 %collective-permute-done.4.other = bf16[4,2,80,640]{3,2,1,0:T(8,128)(2,1)S(1)} collective-permute-done((bf16[4,2,80,640]{3,2,1,0:T(8,128)(2,1)S(1)}, bf16[4,2,80,640]{3,2,1,0:T(8,128)(2,1)S(1)}, u32[]{:S(2)}, u32[]{:S(2)}) %collective-permute-start.4) | collective-permute-done | bytes 819232 | tf_op jit(solution)/shard_map/ppermute | solution.py:70
  41.2 2.6 %away_far.1 = (s16[3,304,128]{2,1,0:T(8,128)(2,1)S(1)}, bf16[304,2560]{1,0:T(8,128)(2,1)S(1)}) custom-call(bf16[4,2,80,640]{3,2,1,0:T(8,128)(2,1)S(1)} %pad_maximum_fusion.own, bf16[4,2,80,640]{3,2,1,0:T(8,128)(2,1)S(1)} %collective-permute-done.4.other, bf16[2048,2560]{1,0:T(8,128)(2,1)} %integrals.5), custom_call_target="tpu_custom_call" | custom-call | flops 597688320 | bytes 1966080 | tf_op jit(solution)/shard_map/away_far/pallas_call | solution.py:215
  43.8 0.8 collective-permute-start.5
  44.6 3.0 %away_near.1.after = s16[5,304,128]{2,1,0:T(8,128)(2,1)S(1)} custom-call(bf16[304,2560]{1,0:T(8,128)(2,1)S(1)} %get-tuple-element.19.left, bf16[2048,2560]{1,0:T(8,128)(2,1)} %integrals.5), custom_call_target="tpu_custom_call" | custom-call | flops 996147200 | bytes 3276800 | tf_op jit(solution)/shard_map/away_near/pallas_call | solution.py:226
  47.5 3.9 %home.1.kept = f32[304,1024]{1,0:T(8,128)S(1)} custom-call(bf16[304,2560]{1,0:T(8,128)(2,1)S(1)} %get-tuple-element.19.left, bf16[2048,2560]{1,0:T(8,128)(2,1)} %integrals.5, s16[5,304,128]{2,1,0:T(8,128)(2,1)S(1)} %away_near.1.after), custom_call_target="tpu_custom_call" | custom-call | flops 1593835520 | bytes 5242880 | tf_op jit(solution)/shard_map/home/pallas_call | solution.py:236
  51.6 1.4 %collective-permute-start.9 = (s16[5,304,128]{2,1,0:T(8,128)(2,1)S(1)}, s16[5,304,128]{2,1,0:T(8,128)(2,1)S(1)}, u32[]{:S(2)}, u32[]{:S(2)}) collective-permute-start(s16[5,304,128]{2,1,0:T(8,128)(2,1)S(1)} %away_near.1.after), channel_id=1, source_target_pairs={{0,8},{8,0},{1,9},{9,1},{2,10},{10,2},{3,11},{11,3},{4,12},{12,4},... | collective-permute-start | bytes 1167368 | tf_op jit(solution)/shard_map/ppermute | solution.py:247
  53.0 0.2 meet_far.1
  53.1 5.9 %collective-permute-start.7 = (s16[304,128]{1,0:T(8,128)(2,1)S(1)}, s16[304,128]{1,0:T(8,128)(2,1)S(1)}, u32[]{:S(2)}, u32[]{:S(2)}) collective-permute-start(s16[304,128]{1,0:T(8,128)(2,1)S(1)} %get-tuple-element.23), channel_id=1, source_target_pairs={{0,3},{1,4},{2,5},{3,6},{4,7},{5,0},{6,1},{7,2},{8,11},{9,12},{10,... | collective-permute-start | bytes 233480 | tf_op jit(solution)/shard_map/ppermute | solution.py:264
  59.0 0.1 collective-permute-start.8
  59.1 5.4 %collective-permute-start.6 = (s16[304,128]{1,0:T(8,128)(2,1)S(1)}, s16[304,128]{1,0:T(8,128)(2,1)S(1)}, u32[]{:S(2)}, u32[]{:S(2)}) collective-permute-start(s16[304,128]{1,0:T(8,128)(2,1)S(1)} %get-tuple-element.22.after), channel_id=1, source_target_pairs={{0,4},{1,5},{2,6},{3,7},{4,0},{5,1},{6,2},{7,3},{8,12},{9,13},{10,... | collective-permute-start | bytes 233480 | tf_op jit(solution)/shard_map/ppermute | solution.py:264
  64.5 0.2 meet_near.1
  64.8 1.2 %collective-permute-start.10 = (s16[304,128]{1,0:T(8,128)(2,1)S(1)}, s16[304,128]{1,0:T(8,128)(2,1)S(1)}, u32[]{:S(2)}, u32[]{:S(2)}) collective-permute-start(s16[304,128]{1,0:T(8,128)(2,1)S(1)} %get-tuple-element.26), channel_id=1, source_target_pairs={{0,2},{1,3},{2,4},{3,5},{4,6},{5,7},{6,0},{7,1},{8,10},{9,11},{10,... | collective-permute-start | bytes 233480 | tf_op jit(solution)/shard_map/ppermute | solution.py:265
  66.0 3.0 %collective-permute-start.11 = (s16[304,128]{1,0:T(8,128)(2,1)S(1)}, s16[304,128]{1,0:T(8,128)(2,1)S(1)}, u32[]{:S(2)}, u32[]{:S(2)}) collective-permute-start(s16[304,128]{1,0:T(8,128)(2,1)S(1)} %get-tuple-element.27), channel_id=1, source_target_pairs={{0,6},{1,7},{2,0},{3,1},{4,2},{5,3},{6,4},{7,5},{8,14},{9,15},{10,... | collective-permute-start | bytes 233480 | tf_op jit(solution)/shard_map/ppermute | solution.py:265
  69.0 0.1 collective-permute-start.12
  69.1 1.9 %collective-permute-start.13 = (s16[304,128]{1,0:T(8,128)(2,1)S(1)}, s16[304,128]{1,0:T(8,128)(2,1)S(1)}, u32[]{:S(2)}, u32[]{:S(2)}) collective-permute-start(s16[304,128]{1,0:T(8,128)(2,1)S(1)} %get-tuple-element.29), channel_id=1, source_target_pairs={{0,7},{1,0},{2,1},{3,2},{4,3},{5,4},{6,5},{7,6},{8,15},{9,8},{10,9... | collective-permute-start | bytes 233480 | tf_op jit(solution)/shard_map/ppermute | solution.py:265
  71.0 1.3 %collective-permute-done.6.refs_1_ = s16[304,128]{1,0:T(8,128)(2,1)S(1)} collective-permute-done((s16[304,128]{1,0:T(8,128)(2,1)S(1)}, s16[304,128]{1,0:T(8,128)(2,1)S(1)}, u32[]{:S(2)}, u32[]{:S(2)}) %collective-permute-start.6) | collective-permute-done | bytes 77856 | tf_op jit(solution)/shard_map/ppermute | solution.py:264
  72.4 0.5 collective-permute-done.10.refs_4_
  72.9 2.3 %collective-permute-done.11.refs_5_ = s16[304,128]{1,0:T(8,128)(2,1)S(1)} collective-permute-done((s16[304,128]{1,0:T(8,128)(2,1)S(1)}, s16[304,128]{1,0:T(8,128)(2,1)S(1)}, u32[]{:S(2)}, u32[]{:S(2)}) %collective-permute-start.11) | collective-permute-done | bytes 77856 | tf_op jit(solution)/shard_map/ppermute | solution.py:265
  75.2 1.4 %sum.1 = f32[3,100,128]{2,1,0:T(8,128)} custom-call(s32[17]{0:T(128)S(1)} %copy-done.1, s16[304,128]{1,0:T(8,128)(2,1)S(1)} %collective-permute-done.6.refs_1_, s16[304,128]{1,0:T(8,128)(2,1)S(1)} %collective-permute-done.7.refs_2_, s16[304,128]{1,0:T(8,128)(2,1)S(1)} %collective-permute-done.8.refs_3_, s16[304,128]{1,0:T(8,128)(2,1)S(1)} %collective-permute-done.10.refs_4_, ...), custom_call_target="tpu_custom_call" | custom-call | tf_op jit(solution)/shard_map/sum/pallas_call | solution.py:266
  (13 shorter events, 0.2 us)
Async XLA Ops:
  0.0 1.0 %copy-start = (bf16[100,2560]{1,0:T(8,128)(2,1)S(1)}, bf16[100,2560]{1,0:T(8,128)(2,1)}, u32[]{:S(2)}) copy-start(bf16[100,2560]{1,0:T(8,128)(2,1)} %panel.1) | copy-start | bytes 1536004
  1.0 19.5 %copy-start.2 = (s32[3]{0:T(128)S(1)}, s32[3]{0:T(128)}, u32[]{:S(2)}) copy-start(s32[3]{0:T(128)} %owner.1) | copy-start | bytes 40
  21.1 6.3 %collective-permute-start = (bf16[80,640]{1,0:T(8,128)(2,1)S(1)}, bf16[80,640]{1,0:T(8,128)(2,1)S(1)}, u32[]{:S(2)}, u32[]{:S(2)}) collective-permute-start(bf16[80,640]{1,0:T(8,128)(2,1)S(1)} %pick.1), channel_id=1, source_target_pairs={{0,128},{128,0},{1,129},{129,1},{2,130},{130,2},{3,131},{131,3},{4... | collective-permute-start | bytes 307208 | tf_op jit(solution)/shard_map/ppermute | solution.py:68
  27.4 9.1 %collective-permute-start.2 = (bf16[2,80,640]{2,1,0:T(8,128)(2,1)S(1)}, bf16[2,80,640]{2,1,0:T(8,128)(2,1)S(1)}, u32[]{:S(2)}, u32[]{:S(2)}) collective-permute-start(bf16[2,80,640]{2,1,0:T(8,128)(2,1)S(1)} %get-tuple-element.32), channel_id=1, source_target_pairs={{0,64},{32,96},{64,0},{96,32},{1,65},{33,97},{65,1},{97,33},{2,66}... | collective-permute-start | bytes 614408 | tf_op jit(solution)/shard_map/ppermute | solution.py:69
  28.3 10.4 %collective-permute-start.1 = (bf16[2,80,640]{2,1,0:T(8,128)(2,1)S(1)}, bf16[2,80,640]{2,1,0:T(8,128)(2,1)S(1)}, u32[]{:S(2)}, u32[]{:S(2)}) collective-permute-start(bf16[2,80,640]{2,1,0:T(8,128)(2,1)S(1)} %get-tuple-element.32), channel_id=1, source_target_pairs={{0,32},{32,64},{64,96},{96,0},{1,33},{33,65},{65,97},{97,1},{2,34}... | collective-permute-start | bytes 614408 | tf_op jit(solution)/shard_map/ppermute | solution.py:69
  29.4 9.2 %collective-permute-start.3 = (bf16[2,80,640]{2,1,0:T(8,128)(2,1)S(1)}, bf16[2,80,640]{2,1,0:T(8,128)(2,1)S(1)}, u32[]{:S(2)}, u32[]{:S(2)}) collective-permute-start(bf16[2,80,640]{2,1,0:T(8,128)(2,1)S(1)} %get-tuple-element.32), channel_id=1, source_target_pairs={{0,96},{32,0},{64,32},{96,64},{1,97},{33,1},{65,33},{97,65},{2,98}... | collective-permute-start | bytes 614408 | tf_op jit(solution)/shard_map/ppermute | solution.py:69
  38.8 2.4 %collective-permute-start.4 = (bf16[4,2,80,640]{3,2,1,0:T(8,128)(2,1)S(1)}, bf16[4,2,80,640]{3,2,1,0:T(8,128)(2,1)S(1)}, u32[]{:S(2)}, u32[]{:S(2)}) collective-permute-start(bf16[4,2,80,640]{3,2,1,0:T(8,128)(2,1)S(1)} %pad_maximum_fusion.own), channel_id=1, source_target_pairs={{0,16},{16,0},{1,17},{17,1},{2,18},{18,2},{3,19},{19,3},{4,20},{20... | collective-permute-start | bytes 2457608 | tf_op jit(solution)/shard_map/ppermute | solution.py:70
  43.8 7.8 %collective-permute-start.5 = (s16[3,304,128]{2,1,0:T(8,128)(2,1)S(1)}, s16[3,304,128]{2,1,0:T(8,128)(2,1)S(1)}, u32[]{:S(2)}, u32[]{:S(2)}) collective-permute-start(s16[3,304,128]{2,1,0:T(8,128)(2,1)S(1)} %get-tuple-element.18), channel_id=1, source_target_pairs={{0,8},{8,0},{1,9},{9,1},{2,10},{10,2},{3,11},{11,3},{4,12},{12,4},... | collective-permute-start | bytes 700424 | tf_op jit(solution)/shard_map/ppermute | solution.py:225
  51.5 23.7 %copy-start.1 = (s32[17]{0:T(128)S(1)}, s32[17]{0:T(128)}, u32[]{:S(2)}) copy-start(s32[17]{0:T(128)} %refs_0_.1) | copy-start | bytes 208
  51.6 12.9 %collective-permute-start.9 = (s16[5,304,128]{2,1,0:T(8,128)(2,1)S(1)}, s16[5,304,128]{2,1,0:T(8,128)(2,1)S(1)}, u32[]{:S(2)}, u32[]{:S(2)}) collective-permute-start(s16[5,304,128]{2,1,0:T(8,128)(2,1)S(1)} %away_near.1.after), channel_id=1, source_target_pairs={{0,8},{8,0},{1,9},{9,1},{2,10},{10,2},{3,11},{11,3},{4,12},{12,4},... | collective-permute-start | bytes 1167368 | tf_op jit(solution)/shard_map/ppermute | solution.py:247
  53.1 15.9 %collective-permute-start.7 = (s16[304,128]{1,0:T(8,128)(2,1)S(1)}, s16[304,128]{1,0:T(8,128)(2,1)S(1)}, u32[]{:S(2)}, u32[]{:S(2)}) collective-permute-start(s16[304,128]{1,0:T(8,128)(2,1)S(1)} %get-tuple-element.23), channel_id=1, source_target_pairs={{0,3},{1,4},{2,5},{3,6},{4,7},{5,0},{6,1},{7,2},{8,11},{9,12},{10,... | collective-permute-start | bytes 233480 | tf_op jit(solution)/shard_map/ppermute | solution.py:264
  59.0 10.1 %collective-permute-start.8 = (s16[304,128]{1,0:T(8,128)(2,1)S(1)}, s16[304,128]{1,0:T(8,128)(2,1)S(1)}, u32[]{:S(2)}, u32[]{:S(2)}) collective-permute-start(s16[304,128]{1,0:T(8,128)(2,1)S(1)} %get-tuple-element.24), channel_id=1, source_target_pairs={{0,5},{1,6},{2,7},{3,0},{4,1},{5,2},{6,3},{7,4},{8,13},{9,14},{10,... | collective-permute-start | bytes 233480 | tf_op jit(solution)/shard_map/ppermute | solution.py:264
  59.1 13.2 %collective-permute-start.6 = (s16[304,128]{1,0:T(8,128)(2,1)S(1)}, s16[304,128]{1,0:T(8,128)(2,1)S(1)}, u32[]{:S(2)}, u32[]{:S(2)}) collective-permute-start(s16[304,128]{1,0:T(8,128)(2,1)S(1)} %get-tuple-element.22.after), channel_id=1, source_target_pairs={{0,4},{1,5},{2,6},{3,7},{4,0},{5,1},{6,2},{7,3},{8,12},{9,13},{10,... | collective-permute-start | bytes 233480 | tf_op jit(solution)/shard_map/ppermute | solution.py:264
  64.8 8.1 %collective-permute-start.10 = (s16[304,128]{1,0:T(8,128)(2,1)S(1)}, s16[304,128]{1,0:T(8,128)(2,1)S(1)}, u32[]{:S(2)}, u32[]{:S(2)}) collective-permute-start(s16[304,128]{1,0:T(8,128)(2,1)S(1)} %get-tuple-element.26), channel_id=1, source_target_pairs={{0,2},{1,3},{2,4},{3,5},{4,6},{5,7},{6,0},{7,1},{8,10},{9,11},{10,... | collective-permute-start | bytes 233480 | tf_op jit(solution)/shard_map/ppermute | solution.py:265
  66.0 9.2 %collective-permute-start.11 = (s16[304,128]{1,0:T(8,128)(2,1)S(1)}, s16[304,128]{1,0:T(8,128)(2,1)S(1)}, u32[]{:S(2)}, u32[]{:S(2)}) collective-permute-start(s16[304,128]{1,0:T(8,128)(2,1)S(1)} %get-tuple-element.27), channel_id=1, source_target_pairs={{0,6},{1,7},{2,0},{3,1},{4,2},{5,3},{6,4},{7,5},{8,14},{9,15},{10,... | collective-permute-start | bytes 233480 | tf_op jit(solution)/shard_map/ppermute | solution.py:265
  69.0 6.2 %collective-permute-start.12 = (s16[304,128]{1,0:T(8,128)(2,1)S(1)}, s16[304,128]{1,0:T(8,128)(2,1)S(1)}, u32[]{:S(2)}, u32[]{:S(2)}) collective-permute-start(s16[304,128]{1,0:T(8,128)(2,1)S(1)} %get-tuple-element.28), channel_id=1, source_target_pairs={{0,1},{1,2},{2,3},{3,4},{4,5},{5,6},{6,7},{7,0},{8,9},{9,10},{10,1... | collective-permute-start | bytes 233480 | tf_op jit(solution)/shard_map/ppermute | solution.py:265
  69.1 6.1 %collective-permute-start.13 = (s16[304,128]{1,0:T(8,128)(2,1)S(1)}, s16[304,128]{1,0:T(8,128)(2,1)S(1)}, u32[]{:S(2)}, u32[]{:S(2)}) collective-permute-start(s16[304,128]{1,0:T(8,128)(2,1)S(1)} %get-tuple-element.29), channel_id=1, source_target_pairs={{0,7},{1,0},{2,1},{3,2},{4,3},{5,4},{6,5},{7,6},{8,15},{9,8},{10,9... | collective-permute-start | bytes 233480 | tf_op jit(solution)/shard_map/ppermute | solution.py:265

commit v6 on v5

--- a/solution.py
+++ b/solution.py
@@ -65,8 +65,10 @@
         compiler_params=SMALL,
         name="pick",
     )(panel_owner, held)
-    two = jnp.stack([mine, lax.ppermute(mine, "yh", shift(2, 1))])
-    eight = jnp.stack([two] + [lax.ppermute(two, "x", shift(4, d)) for d in range(1, 4)])
+    across = lax.ppermute(mine, "yh", shift(2, 1))
+    straight = [mine] + [lax.ppermute(mine, "x", shift(4, d)) for d in range(1, 4)]
+    turned = [across] + [lax.ppermute(across, "x", shift(4, d)) for d in range(1, 4)]
+    eight = jnp.stack([jnp.stack(pair) for pair in zip(straight, turned)])
     return eight, lax.ppermute(eight, "core", shift(2, 1))
 
 

time: 77.3 us -> 75.1 us (0.972)
  waiting for transfers between devices: 19.4 us -> 16.6 us
    ppermute x4 -> x7, waiting for transfers between devices: 12.7 us -> 9.84 us  [the longest x3 6.63 us: gather_panels(): lax.ppermute(across, 'x', shift(4, d))]
    ppermute x4 -> x7, starting transfers between devices: 4.77 us -> 5.36 us  [the longest x3 2.41 us: gather_panels(): lax.ppermute(mine, 'x', shift(4, d))]
  transfers between devices with their start and end apart: 14 -> 17, of which waited for: 9 -> 9; matrix products, arithmetic and copies ran while one was open for 0% -> 0% of each run, Pallas kernels for 10% -> 10%
where the time goes in v6:
time: 75.1 us; the launch traced here: 74.6 us
  starting transfers between devices  25.2 us (34%)
  blocking collectives  19.2 us (26%)
  waiting for transfers between devices  16.6 us (22%)
  Pallas kernels  12.2 us (16%)
  local copies, waits for them, and re-layouts  1.05 us (1%)
    all_to_all x1, blocking collectives, gather_panels(): held = lax.all_to_all(pieces, ROW, 0, 0)  19.2 us
    ppermute x3, starting transfers between devices, per_device(): got = [lax.ppermute(c, 'z', shift(8, d)) for c, d in zip(met_far, FAR)]  11.4 us
    ppermute x3, waiting for transfers between devices, gather_panels(): lax.ppermute(across, 'x', shift(4, d))  6.63 us
    ppermute x4, starting transfers between devices, per_device(): lax.ppermute(c, 'z', shift(8, d))  6.24 us
    pallas_call x1, Pallas kernels, per_device(): pl.pallas_call(home_kernel, out_shape=jax.ShapeDtypeStruct((TALL, 8 * SLO...  3.95 us
    ppermute x1, waiting for transfers between devices, gather_panels(): across = lax.ppermute(mine, 'yh', shift(2, 1))  3.19 us
    pallas_call x1, Pallas kernels, per_device(): pl.pallas_call(away_near_kernel, out_shape=codes(near), in_specs=[VMEM, H...  2.99 us
    ppermute x4, waiting for transfers between devices, per_device(): lax.ppermute(c, 'z', shift(8, d))  2.92 us
  transfers between devices with their start and end apart: 17, of which 9 were waited for; matrix products, arithmetic and copies ran while one was open for 0% of the time, Pallas kernels for 10%

profile of v6, /device:TPU:32, one launch (start us, length us, event | category | flops | bytes accessed | tf_op | source)
XLA Modules:
  0.0 74.6 jit_solution(15298548369477288206)
XLA Ops:
  0.0 1.0 %copy-done = bf16[100,2560]{1,0:T(8,128)(2,1)S(1)} copy-done((bf16[100,2560]{1,0:T(8,128)(2,1)S(1)}, bf16[100,2560]{1,0:T(8,128)(2,1)}, u32[]{:S(2)}) %copy-start) | copy-done | bytes 512024
  1.0 0.3 cut.1
  1.3 19.2 %all_to_all.5.held = bf16[16,128,128]{2,1,0:T(8,128)(2,1)S(1)} all-to-all(bf16[16,128,128]{2,1,0:T(8,128)(2,1)S(1)} %cut.1), channel_id=1, replica_groups=mesh['yh'=2,'x'=4,'core'=2,'yl'=2,'z'=8] {'yh','x','core'}, dimensions={0} | all-to-all | bytes 1048576 | tf_op jit(solution)/shard_map/all_to_all | solution.py:59
  20.5 0.6 pick.1
  21.1 0.6 collective-permute-start
  21.8 0.9 %collective-permute-start.5 = (bf16[80,640]{1,0:T(8,128)(2,1)S(1)}, bf16[80,640]{1,0:T(8,128)(2,1)S(1)}, u32[]{:S(2)}, u32[]{:S(2)}) collective-permute-start(bf16[80,640]{1,0:T(8,128)(2,1)S(1)} %pick.1), channel_id=1, source_target_pairs={{0,96},{32,0},{64,32},{96,64},{1,97},{33,1},{65,33},{97,65},{2,98}... | collective-permute-start | bytes 307208 | tf_op jit(solution)/shard_map/ppermute | solution.py:69
  22.6 0.9 %collective-permute-start.3 = (bf16[80,640]{1,0:T(8,128)(2,1)S(1)}, bf16[80,640]{1,0:T(8,128)(2,1)S(1)}, u32[]{:S(2)}, u32[]{:S(2)}) collective-permute-start(bf16[80,640]{1,0:T(8,128)(2,1)S(1)} %pick.1), channel_id=1, source_target_pairs={{0,64},{32,96},{64,0},{96,32},{1,65},{33,97},{65,1},{97,33},{2,66}... | collective-permute-start | bytes 307208 | tf_op jit(solution)/shard_map/ppermute | solution.py:69
  23.5 0.6 collective-permute-start.1
  24.2 3.2 %collective-permute-done = bf16[80,640]{1,0:T(8,128)(2,1)S(1)} collective-permute-done((bf16[80,640]{1,0:T(8,128)(2,1)S(1)}, bf16[80,640]{1,0:T(8,128)(2,1)S(1)}, u32[]{:S(2)}, u32[]{:S(2)}) %collective-permute-start) | collective-permute-done | bytes 102432 | tf_op jit(solution)/shard_map/ppermute | solution.py:68
  27.4 1.1 %collective-permute-start.6 = (bf16[80,640]{1,0:T(8,128)(2,1)S(1)}, bf16[80,640]{1,0:T(8,128)(2,1)S(1)}, u32[]{:S(2)}, u32[]{:S(2)}) collective-permute-start(bf16[80,640]{1,0:T(8,128)(2,1)S(1)} %collective-permute-done), channel_id=1, source_target_pairs={{0,96},{32,0},{64,32},{96,64},{1,97},{33,1},{65,33},{97,65},{2,98}... | collective-permute-start | bytes 307208 | tf_op jit(solution)/shard_map/ppermute | solution.py:70
  28.4 0.4 collective-permute-start.4
  28.8 0.9 %collective-permute-start.2 = (bf16[80,640]{1,0:T(8,128)(2,1)S(1)}, bf16[80,640]{1,0:T(8,128)(2,1)S(1)}, u32[]{:S(2)}, u32[]{:S(2)}) collective-permute-start(bf16[80,640]{1,0:T(8,128)(2,1)S(1)} %collective-permute-done), channel_id=1, source_target_pairs={{0,32},{32,64},{64,96},{96,0},{1,33},{33,65},{65,97},{97,1},{2,34}... | collective-permute-start | bytes 307208 | tf_op jit(solution)/shard_map/ppermute | solution.py:70
  29.7 3.0 %collective-permute-done.6 = bf16[80,640]{1,0:T(8,128)(2,1)S(1)} collective-permute-done((bf16[80,640]{1,0:T(8,128)(2,1)S(1)}, bf16[80,640]{1,0:T(8,128)(2,1)S(1)}, u32[]{:S(2)}, u32[]{:S(2)}) %collective-permute-start.6) | collective-permute-done | bytes 102432 | tf_op jit(solution)/shard_map/ppermute | solution.py:70
  32.8 2.6 %collective-permute-done.4 = bf16[80,640]{1,0:T(8,128)(2,1)S(1)} collective-permute-done((bf16[80,640]{1,0:T(8,128)(2,1)S(1)}, bf16[80,640]{1,0:T(8,128)(2,1)S(1)}, u32[]{:S(2)}, u32[]{:S(2)}) %collective-permute-start.4) | collective-permute-done | bytes 102432 | tf_op jit(solution)/shard_map/ppermute | solution.py:70
  35.4 1.0 %collective-permute-done.2 = bf16[80,640]{1,0:T(8,128)(2,1)S(1)} collective-permute-done((bf16[80,640]{1,0:T(8,128)(2,1)S(1)}, bf16[80,640]{1,0:T(8,128)(2,1)S(1)}, u32[]{:S(2)}, u32[]{:S(2)}) %collective-permute-start.2) | collective-permute-done | bytes 102432 | tf_op jit(solution)/shard_map/ppermute | solution.py:70
  36.7 2.3 %collective-permute-done.7.other = bf16[4,2,80,640]{3,2,1,0:T(8,128)(2,1)S(1)} collective-permute-done((bf16[4,2,80,640]{3,2,1,0:T(8,128)(2,1)S(1)}, bf16[4,2,80,640]{3,2,1,0:T(8,128)(2,1)S(1)}, u32[]{:S(2)}, u32[]{:S(2)}) %collective-permute-start.7) | collective-permute-done | bytes 819232 | tf_op jit(solution)/shard_map/ppermute | solution.py:72
  39.0 2.6 %away_far.1 = (s16[3,304,128]{2,1,0:T(8,128)(2,1)S(1)}, bf16[304,2560]{1,0:T(8,128)(2,1)S(1)}) custom-call(bf16[4,2,80,640]{3,2,1,0:T(8,128)(2,1)S(1)} %pad_maximum_fusion.own, bf16[4,2,80,640]{3,2,1,0:T(8,128)(2,1)S(1)} %collective-permute-done.7.other, bf16[2048,2560]{1,0:T(8,128)(2,1)} %integrals.5), custom_call_target="tpu_custom_call" | custom-call | flops 597688320 | bytes 1966080 | tf_op jit(solution)/shard_map/away_far/pallas_call | solution.py:217
  41.6 0.8 %collective-permute-start.8 = (s16[3,304,128]{2,1,0:T(8,128)(2,1)S(1)}, s16[3,304,128]{2,1,0:T(8,128)(2,1)S(1)}, u32[]{:S(2)}, u32[]{:S(2)}) collective-permute-start(s16[3,304,128]{2,1,0:T(8,128)(2,1)S(1)} %get-tuple-element.18), channel_id=1, source_target_pairs={{0,8},{8,0},{1,9},{9,1},{2,10},{10,2},{3,11},{11,3},{4,12},{12,4},... | collective-permute-start | bytes 700424 | tf_op jit(solution)/shard_map/ppermute | solution.py:227
  42.4 3.0 %away_near.1.after = s16[5,304,128]{2,1,0:T(8,128)(2,1)S(1)} custom-call(bf16[304,2560]{1,0:T(8,128)(2,1)S(1)} %get-tuple-element.19.left, bf16[2048,2560]{1,0:T(8,128)(2,1)} %integrals.5), custom_call_target="tpu_custom_call" | custom-call | flops 996147200 | bytes 3276800 | tf_op jit(solution)/shard_map/away_near/pallas_call | solution.py:228
  45.3 3.9 %home.1.kept = f32[304,1024]{1,0:T(8,128)S(1)} custom-call(bf16[304,2560]{1,0:T(8,128)(2,1)S(1)} %get-tuple-element.19.left, bf16[2048,2560]{1,0:T(8,128)(2,1)} %integrals.5, s16[5,304,128]{2,1,0:T(8,128)(2,1)S(1)} %away_near.1.after), custom_call_target="tpu_custom_call" | custom-call | flops 1593835520 | bytes 5242880 | tf_op jit(solution)/shard_map/home/pallas_call | solution.py:238
  49.4 1.4 %collective-permute-start.12 = (s16[5,304,128]{2,1,0:T(8,128)(2,1)S(1)}, s16[5,304,128]{2,1,0:T(8,128)(2,1)S(1)}, u32[]{:S(2)}, u32[]{:S(2)}) collective-permute-start(s16[5,304,128]{2,1,0:T(8,128)(2,1)S(1)} %away_near.1.after), channel_id=1, source_target_pairs={{0,8},{8,0},{1,9},{9,1},{2,10},{10,2},{3,11},{11,3},{4,12},{12,4},... | collective-permute-start | bytes 1167368 | tf_op jit(solution)/shard_map/ppermute | solution.py:249
  50.9 5.9 %collective-permute-start.10 = (s16[304,128]{1,0:T(8,128)(2,1)S(1)}, s16[304,128]{1,0:T(8,128)(2,1)S(1)}, u32[]{:S(2)}, u32[]{:S(2)}) collective-permute-start(s16[304,128]{1,0:T(8,128)(2,1)S(1)} %get-tuple-element.23), channel_id=1, source_target_pairs={{0,3},{1,4},{2,5},{3,6},{4,7},{5,0},{6,1},{7,2},{8,11},{9,12},{10,... | collective-permute-start | bytes 233480 | tf_op jit(solution)/shard_map/ppermute | solution.py:266
  56.8 0.3 collective-permute-start.11
  57.1 5.2 %collective-permute-start.9 = (s16[304,128]{1,0:T(8,128)(2,1)S(1)}, s16[304,128]{1,0:T(8,128)(2,1)S(1)}, u32[]{:S(2)}, u32[]{:S(2)}) collective-permute-start(s16[304,128]{1,0:T(8,128)(2,1)S(1)} %get-tuple-element.22.after), channel_id=1, source_target_pairs={{0,4},{1,5},{2,6},{3,7},{4,0},{5,1},{6,2},{7,3},{8,12},{9,13},{10,... | collective-permute-start | bytes 233480 | tf_op jit(solution)/shard_map/ppermute | solution.py:266
  62.3 0.2 meet_near.1
  62.6 1.2 %collective-permute-start.13 = (s16[304,128]{1,0:T(8,128)(2,1)S(1)}, s16[304,128]{1,0:T(8,128)(2,1)S(1)}, u32[]{:S(2)}, u32[]{:S(2)}) collective-permute-start(s16[304,128]{1,0:T(8,128)(2,1)S(1)} %get-tuple-element.26), channel_id=1, source_target_pairs={{0,2},{1,3},{2,4},{3,5},{4,6},{5,7},{6,0},{7,1},{8,10},{9,11},{10,... | collective-permute-start | bytes 233480 | tf_op jit(solution)/shard_map/ppermute | solution.py:267
  63.8 3.0 %collective-permute-start.14 = (s16[304,128]{1,0:T(8,128)(2,1)S(1)}, s16[304,128]{1,0:T(8,128)(2,1)S(1)}, u32[]{:S(2)}, u32[]{:S(2)}) collective-permute-start(s16[304,128]{1,0:T(8,128)(2,1)S(1)} %get-tuple-element.27), channel_id=1, source_target_pairs={{0,6},{1,7},{2,0},{3,1},{4,2},{5,3},{6,4},{7,5},{8,14},{9,15},{10,... | collective-permute-start | bytes 233480 | tf_op jit(solution)/shard_map/ppermute | solution.py:267
  66.9 1.9 %collective-permute-start.16 = (s16[304,128]{1,0:T(8,128)(2,1)S(1)}, s16[304,128]{1,0:T(8,128)(2,1)S(1)}, u32[]{:S(2)}, u32[]{:S(2)}) collective-permute-start(s16[304,128]{1,0:T(8,128)(2,1)S(1)} %get-tuple-element.29), channel_id=1, source_target_pairs={{0,7},{1,0},{2,1},{3,2},{4,3},{5,4},{6,5},{7,6},{8,15},{9,8},{10,9... | collective-permute-start | bytes 233480 | tf_op jit(solution)/shard_map/ppermute | solution.py:267
  68.8 1.4 %collective-permute-done.9.refs_1_ = s16[304,128]{1,0:T(8,128)(2,1)S(1)} collective-permute-done((s16[304,128]{1,0:T(8,128)(2,1)S(1)}, s16[304,128]{1,0:T(8,128)(2,1)S(1)}, u32[]{:S(2)}, u32[]{:S(2)}) %collective-permute-start.9) | collective-permute-done | bytes 77856 | tf_op jit(solution)/shard_map/ppermute | solution.py:266
  70.3 0.5 collective-permute-done.13.refs_4_
  70.7 2.4 %collective-permute-done.14.refs_5_ = s16[304,128]{1,0:T(8,128)(2,1)S(1)} collective-permute-done((s16[304,128]{1,0:T(8,128)(2,1)S(1)}, s16[304,128]{1,0:T(8,128)(2,1)S(1)}, u32[]{:S(2)}, u32[]{:S(2)}) %collective-permute-start.14) | collective-permute-done | bytes 77856 | tf_op jit(solution)/shard_map/ppermute | solution.py:267
  73.2 1.4 %sum.1 = f32[3,100,128]{2,1,0:T(8,128)} custom-call(s32[17]{0:T(128)S(1)} %copy-done.1, s16[304,128]{1,0:T(8,128)(2,1)S(1)} %collective-permute-done.9.refs_1_, s16[304,128]{1,0:T(8,128)(2,1)S(1)} %collective-permute-done.10.refs_2_, s16[304,128]{1,0:T(8,128)(2,1)S(1)} %collective-permute-done.11.refs_3_, ...), custom_call_target="tpu_custom_call" | custom-call | tf_op jit(solution)/shard_map/sum/pallas_call | solution.py:268
  (22 shorter events, 0.7 us)
Async XLA Ops:
  0.0 1.0 %copy-start = (bf16[100,2560]{1,0:T(8,128)(2,1)S(1)}, bf16[100,2560]{1,0:T(8,128)(2,1)}, u32[]{:S(2)}) copy-start(bf16[100,2560]{1,0:T(8,128)(2,1)} %panel.1) | copy-start | bytes 1536004
  1.0 19.5 %copy-start.2 = (s32[3]{0:T(128)S(1)}, s32[3]{0:T(128)}, u32[]{:S(2)}) copy-start(s32[3]{0:T(128)} %owner.1) | copy-start | bytes 40
  21.1 6.3 %collective-permute-start = (bf16[80,640]{1,0:T(8,128)(2,1)S(1)}, bf16[80,640]{1,0:T(8,128)(2,1)S(1)}, u32[]{:S(2)}, u32[]{:S(2)}) collective-permute-start(bf16[80,640]{1,0:T(8,128)(2,1)S(1)} %pick.1), channel_id=1, source_target_pairs={{0,128},{128,0},{1,129},{129,1},{2,130},{130,2},{3,131},{131,3},{4... | collective-permute-start | bytes 307208 | tf_op jit(solution)/shard_map/ppermute | solution.py:68
  21.8 7.1 %collective-permute-start.5 = (bf16[80,640]{1,0:T(8,128)(2,1)S(1)}, bf16[80,640]{1,0:T(8,128)(2,1)S(1)}, u32[]{:S(2)}, u32[]{:S(2)}) collective-permute-start(bf16[80,640]{1,0:T(8,128)(2,1)S(1)} %pick.1), channel_id=1, source_target_pairs={{0,96},{32,0},{64,32},{96,64},{1,97},{33,1},{65,33},{97,65},{2,98}... | collective-permute-start | bytes 307208 | tf_op jit(solution)/shard_map/ppermute | solution.py:69
  22.6 10.2 %collective-permute-start.3 = (bf16[80,640]{1,0:T(8,128)(2,1)S(1)}, bf16[80,640]{1,0:T(8,128)(2,1)S(1)}, u32[]{:S(2)}, u32[]{:S(2)}) collective-permute-start(bf16[80,640]{1,0:T(8,128)(2,1)S(1)} %pick.1), channel_id=1, source_target_pairs={{0,64},{32,96},{64,0},{96,32},{1,65},{33,97},{65,1},{97,33},{2,66}... | collective-permute-start | bytes 307208 | tf_op jit(solution)/shard_map/ppermute | solution.py:69
  23.5 11.9 %collective-permute-start.1 = (bf16[80,640]{1,0:T(8,128)(2,1)S(1)}, bf16[80,640]{1,0:T(8,128)(2,1)S(1)}, u32[]{:S(2)}, u32[]{:S(2)}) collective-permute-start(bf16[80,640]{1,0:T(8,128)(2,1)S(1)} %pick.1), channel_id=1, source_target_pairs={{0,32},{32,64},{64,96},{96,0},{1,33},{33,65},{65,97},{97,1},{2,34}... | collective-permute-start | bytes 307208 | tf_op jit(solution)/shard_map/ppermute | solution.py:69
  27.4 5.4 %collective-permute-start.6 = (bf16[80,640]{1,0:T(8,128)(2,1)S(1)}, bf16[80,640]{1,0:T(8,128)(2,1)S(1)}, u32[]{:S(2)}, u32[]{:S(2)}) collective-permute-start(bf16[80,640]{1,0:T(8,128)(2,1)S(1)} %collective-permute-done), channel_id=1, source_target_pairs={{0,96},{32,0},{64,32},{96,64},{1,97},{33,1},{65,33},{97,65},{2,98}... | collective-permute-start | bytes 307208 | tf_op jit(solution)/shard_map/ppermute | solution.py:70
  28.4 6.9 %collective-permute-start.4 = (bf16[80,640]{1,0:T(8,128)(2,1)S(1)}, bf16[80,640]{1,0:T(8,128)(2,1)S(1)}, u32[]{:S(2)}, u32[]{:S(2)}) collective-permute-start(bf16[80,640]{1,0:T(8,128)(2,1)S(1)} %collective-permute-done), channel_id=1, source_target_pairs={{0,64},{32,96},{64,0},{96,32},{1,65},{33,97},{65,1},{97,33},{2,66}... | collective-permute-start | bytes 307208 | tf_op jit(solution)/shard_map/ppermute | solution.py:70
  28.8 7.6 %collective-permute-start.2 = (bf16[80,640]{1,0:T(8,128)(2,1)S(1)}, bf16[80,640]{1,0:T(8,128)(2,1)S(1)}, u32[]{:S(2)}, u32[]{:S(2)}) collective-permute-start(bf16[80,640]{1,0:T(8,128)(2,1)S(1)} %collective-permute-done), channel_id=1, source_target_pairs={{0,32},{32,64},{64,96},{96,0},{1,33},{33,65},{65,97},{97,1},{2,34}... | collective-permute-start | bytes 307208 | tf_op jit(solution)/shard_map/ppermute | solution.py:70
  36.6 2.4 %collective-permute-start.7 = (bf16[4,2,80,640]{3,2,1,0:T(8,128)(2,1)S(1)}, bf16[4,2,80,640]{3,2,1,0:T(8,128)(2,1)S(1)}, u32[]{:S(2)}, u32[]{:S(2)}) collective-permute-start(bf16[4,2,80,640]{3,2,1,0:T(8,128)(2,1)S(1)} %pad_maximum_fusion.own), channel_id=1, source_target_pairs={{0,16},{16,0},{1,17},{17,1},{2,18},{18,2},{3,19},{19,3},{4,20},{20... | collective-permute-start | bytes 2457608 | tf_op jit(solution)/shard_map/ppermute | solution.py:72
  41.6 7.8 %collective-permute-start.8 = (s16[3,304,128]{2,1,0:T(8,128)(2,1)S(1)}, s16[3,304,128]{2,1,0:T(8,128)(2,1)S(1)}, u32[]{:S(2)}, u32[]{:S(2)}) collective-permute-start(s16[3,304,128]{2,1,0:T(8,128)(2,1)S(1)} %get-tuple-element.18), channel_id=1, source_target_pairs={{0,8},{8,0},{1,9},{9,1},{2,10},{10,2},{3,11},{11,3},{4,12},{12,4},... | collective-permute-start | bytes 700424 | tf_op jit(solution)/shard_map/ppermute | solution.py:227
  49.3 23.9 %copy-start.1 = (s32[17]{0:T(128)S(1)}, s32[17]{0:T(128)}, u32[]{:S(2)}) copy-start(s32[17]{0:T(128)} %refs_0_.1) | copy-start | bytes 208
  49.4 12.9 %collective-permute-start.12 = (s16[5,304,128]{2,1,0:T(8,128)(2,1)S(1)}, s16[5,304,128]{2,1,0:T(8,128)(2,1)S(1)}, u32[]{:S(2)}, u32[]{:S(2)}) collective-permute-start(s16[5,304,128]{2,1,0:T(8,128)(2,1)S(1)} %away_near.1.after), channel_id=1, source_target_pairs={{0,8},{8,0},{1,9},{9,1},{2,10},{10,2},{3,11},{11,3},{4,12},{12,4},... | collective-permute-start | bytes 1167368 | tf_op jit(solution)/shard_map/ppermute | solution.py:249
  50.9 15.9 %collective-permute-start.10 = (s16[304,128]{1,0:T(8,128)(2,1)S(1)}, s16[304,128]{1,0:T(8,128)(2,1)S(1)}, u32[]{:S(2)}, u32[]{:S(2)}) collective-permute-start(s16[304,128]{1,0:T(8,128)(2,1)S(1)} %get-tuple-element.23), channel_id=1, source_target_pairs={{0,3},{1,4},{2,5},{3,6},{4,7},{5,0},{6,1},{7,2},{8,11},{9,12},{10,... | collective-permute-start | bytes 233480 | tf_op jit(solution)/shard_map/ppermute | solution.py:266
  56.8 10.1 %collective-permute-start.11 = (s16[304,128]{1,0:T(8,128)(2,1)S(1)}, s16[304,128]{1,0:T(8,128)(2,1)S(1)}, u32[]{:S(2)}, u32[]{:S(2)}) collective-permute-start(s16[304,128]{1,0:T(8,128)(2,1)S(1)} %get-tuple-element.24), channel_id=1, source_target_pairs={{0,5},{1,6},{2,7},{3,0},{4,1},{5,2},{6,3},{7,4},{8,13},{9,14},{10,... | collective-permute-start | bytes 233480 | tf_op jit(solution)/shard_map/ppermute | solution.py:266
  57.1 13.1 %collective-permute-start.9 = (s16[304,128]{1,0:T(8,128)(2,1)S(1)}, s16[304,128]{1,0:T(8,128)(2,1)S(1)}, u32[]{:S(2)}, u32[]{:S(2)}) collective-permute-start(s16[304,128]{1,0:T(8,128)(2,1)S(1)} %get-tuple-element.22.after), channel_id=1, source_target_pairs={{0,4},{1,5},{2,6},{3,7},{4,0},{5,1},{6,2},{7,3},{8,12},{9,13},{10,... | collective-permute-start | bytes 233480 | tf_op jit(solution)/shard_map/ppermute | solution.py:266
  62.6 8.1 %collective-permute-start.13 = (s16[304,128]{1,0:T(8,128)(2,1)S(1)}, s16[304,128]{1,0:T(8,128)(2,1)S(1)}, u32[]{:S(2)}, u32[]{:S(2)}) collective-permute-start(s16[304,128]{1,0:T(8,128)(2,1)S(1)} %get-tuple-element.26), channel_id=1, source_target_pairs={{0,2},{1,3},{2,4},{3,5},{4,6},{5,7},{6,0},{7,1},{8,10},{9,11},{10,... | collective-permute-start | bytes 233480 | tf_op jit(solution)/shard_map/ppermute | solution.py:267
  63.8 9.4 %collective-permute-start.14 = (s16[304,128]{1,0:T(8,128)(2,1)S(1)}, s16[304,128]{1,0:T(8,128)(2,1)S(1)}, u32[]{:S(2)}, u32[]{:S(2)}) collective-permute-start(s16[304,128]{1,0:T(8,128)(2,1)S(1)} %get-tuple-element.27), channel_id=1, source_target_pairs={{0,6},{1,7},{2,0},{3,1},{4,2},{5,3},{6,4},{7,5},{8,14},{9,15},{10,... | collective-permute-start | bytes 233480 | tf_op jit(solution)/shard_map/ppermute | solution.py:267
  66.8 6.4 %collective-permute-start.15 = (s16[304,128]{1,0:T(8,128)(2,1)S(1)}, s16[304,128]{1,0:T(8,128)(2,1)S(1)}, u32[]{:S(2)}, u32[]{:S(2)}) collective-permute-start(s16[304,128]{1,0:T(8,128)(2,1)S(1)} %get-tuple-element.28), channel_id=1, source_target_pairs={{0,1},{1,2},{2,3},{3,4},{4,5},{5,6},{6,7},{7,0},{8,9},{9,10},{10,1... | collective-permute-start | bytes 233480 | tf_op jit(solution)/shard_map/ppermute | solution.py:267
  66.9 6.2 %collective-permute-start.16 = (s16[304,128]{1,0:T(8,128)(2,1)S(1)}, s16[304,128]{1,0:T(8,128)(2,1)S(1)}, u32[]{:S(2)}, u32[]{:S(2)}) collective-permute-start(s16[304,128]{1,0:T(8,128)(2,1)S(1)} %get-tuple-element.29), channel_id=1, source_target_pairs={{0,7},{1,0},{2,1},{3,2},{4,3},{5,4},{6,5},{7,6},{8,15},{9,8},{10,9... | collective-permute-start | bytes 233480 | tf_op jit(solution)/shard_map/ppermute | solution.py:267

commit v7 on v6

--- a/solution.py
+++ b/solution.py
@@ -41,13 +41,17 @@
                     pieces[yh * 8 + x * 2 + core, pl.ds(t * RB, RB), :] = block
 
 
-def pick_kernel(owner, held, mine):
+def pick_kernel(owner, offsets, held, mine, live):
+    yh, x, core, yl, z = (lax.axis_index(a) for a in ROW + COL)
+    row = (yh * 4 + x) * 2 + core
+    slot = (yl * 8 + z) * SLOT + lax.broadcasted_iota(jnp.int32, (1, SLOT), 1)
+    live[...] = (slot < offsets[row + 1] - offsets[row]).astype(jnp.float32)
     for s in range(STEPS):
         for t in range(TILES):
             mine[pl.ds(s * RB, RB), pl.ds(t * 128, 128)] = held[owner[s], pl.ds(t * RB, RB), :]
 
 
-def gather_panels(amplitudes, panel_owner):
+def gather_panels(amplitudes, row_offsets, panel_owner):
     pieces = pl.pallas_call(
         cut_kernel,
         out_shape=jax.ShapeDtypeStruct((16, 128, 128), jnp.bfloat16),
@@ -57,19 +61,20 @@
         name="cut",
     )(amplitudes)
     held = lax.all_to_all(pieces, ROW, 0, 0)
-    mine = pl.pallas_call(
+    mine, live = pl.pallas_call(
         pick_kernel,
-        out_shape=jax.ShapeDtypeStruct((BLK, KB), jnp.bfloat16),
-        in_specs=[SMEM, VMEM],
-        out_specs=VMEM,
+        out_shape=[jax.ShapeDtypeStruct((BLK, KB), jnp.bfloat16), jax.ShapeDtypeStruct((1, SLOT), jnp.float32)],
+        in_specs=[SMEM, SMEM, VMEM],
+        out_specs=[VMEM, VMEM],
         compiler_params=SMALL,
         name="pick",
-    )(panel_owner, held)
+    )(panel_owner, row_offsets, held)
     across = lax.ppermute(mine, "yh", shift(2, 1))
     straight = [mine] + [lax.ppermute(mine, "x", shift(4, d)) for d in range(1, 4)]
     turned = [across] + [lax.ppermute(across, "x", shift(4, d)) for d in range(1, 4)]
-    eight = jnp.stack([jnp.stack(pair) for pair in zip(straight, turned)])
-    return eight, lax.ppermute(eight, "core", shift(2, 1))
+    turned[2] = lax.ppermute(straight[2], "yh", shift(2, 1))
+    own = [jnp.stack(straight), jnp.stack(turned)]
+    return live, own + [lax.ppermute(four, "core", shift(2, 1)) for four in own]
 
 
 def last_rows():
@@ -125,15 +130,14 @@
         encode(lambda lo, hi: acc[pl.ds(lo, hi - lo), pl.ds(n * SLOT, SLOT)], out, n)
 
 
-def away_far_kernel(own, other, integrals, out, left, slabs, acc, sems):
+def away_far_kernel(a, b, c, d, integrals, out, left, slabs, acc, sems):
     x = lax.axis_index("x")
     copies = fetch(integrals, slabs, sems, 1 - lax.axis_index("yl"), FAR)
     left[pl.ds(TALL - 16, 16), :] = jnp.zeros((16, 4 * KB), jnp.bfloat16)
     for back in range(4):
         columns = pl.ds(pl.multiple_of(lax.rem(x - back + 4, 4) * KB, KB), KB)
-        for core, piece in enumerate((own, other)):
-            for yh in range(2):
-                left[pl.ds((core * 2 + yh) * USED, USED), columns] = piece[back, yh, pl.ds(0, USED), :]
+        for n, piece in enumerate((a, b, c, d)):
+            left[pl.ds(n * USED, USED), columns] = piece[back, pl.ds(0, USED), :]
     multiply(left, slabs, copies, acc)
     encode_all(acc, out)
 
@@ -174,16 +178,13 @@
 
 
 def sum_kernel(*refs):
-    offsets, *got, kept, out, total = refs
-    yh, x, core, yl, z = (lax.axis_index(a) for a in ROW + COL)
-    row = (yh * 4 + x) * 2 + core
-    slot = (yl * 8 + z) * SLOT + lax.broadcasted_iota(jnp.int32, (1, SLOT), 1)
-    live = (slot < offsets[row + 1] - offsets[row]).astype(jnp.float32)
+    *got, kept, live, out, total = refs
+    yh, core = lax.axis_index("yh"), lax.axis_index("core")
     for g, (lo, hi) in enumerate(GROUPS):
         part = kept[pl.ds(lo, hi - lo), :]
         for codes in got:
             part = part + decode(codes, lo, hi, g)
-        total[pl.ds(lo, hi - lo), :] = part * live
+        total[pl.ds(lo, hi - lo), :] = part * live[...]
     for b in range(4):
         rb = lax.rem(yh + b % 2, 2) * 2 + lax.rem(core + b // 2, 2)
         for case in range(4):
@@ -195,7 +196,7 @@
 
 
 def per_device(amplitudes, integrals, row_offsets, panel_owner):
-    own, other = gather_panels(amplitudes, panel_owner)
+    live, panels = gather_panels(amplitudes, row_offsets, panel_owner)
     def codes(*n):
         return jax.ShapeDtypeStruct(n + (TALL, SLOT), jnp.int16)
 
@@ -217,13 +218,13 @@
     away_far, left = pl.pallas_call(
         away_far_kernel,
         out_shape=[codes(far), jax.ShapeDtypeStruct((TALL, 4 * KB), jnp.bfloat16)],
-        in_specs=[VMEM, VMEM, HBM],
+        in_specs=[VMEM, VMEM, VMEM, VMEM, HBM],
         out_specs=[VMEM, VMEM],
         scratch_shapes=room(far) + wide(far) + sems(far),
         compiler_params=LARGE,
         cost_estimate=cost(far),
         name="away_far",
-    )(own, other, integrals)
+    )(*panels, integrals)
     got_far = lax.ppermute(away_far, "yl", shift(2, 1))
     away_near = pl.pallas_call(
         away_near_kernel,
@@ -268,12 +269,12 @@
     return pl.pallas_call(
         sum_kernel,
         out_shape=jax.ShapeDtypeStruct((STEPS, 4 * RB, SLOT), jnp.float32),
-        in_specs=[SMEM] + [VMEM] * 8,
+        in_specs=[VMEM] * 9,
         out_specs=VMEM,
         scratch_shapes=[pltpu.VMEM((TALL, SLOT), jnp.float32)],
         compiler_params=SMALL,
         name="sum",
-    )(row_offsets, *got, met_near[-1])
+    )(*got, met_near[-1], live)
 
 
 def solution(mesh):

time: 75.1 us -> 73 us (0.972)
  waiting for transfers between devices: 16.6 us -> 12.2 us
  starting transfers between devices: 25.2 us -> 28.1 us
    ppermute x3 -> x2, waiting for transfers between devices: 6.63 us -> 2.21 us  [gather_panels(): lax.ppermute(across, 'x', shift(4, d))]
    ppermute x1 -> x3, starting transfers between devices: 0.09 us -> 2.69 us  [the longest x1 2.5 us: gather_panels(): turned[2] = lax.ppermute(straight[2], 'yh', shift(2, 1))]
    ppermute x1 -> x3, waiting for transfers between devices: 2.32 us -> 2.99 us  [the longest x2 1.73 us: gather_panels(): lax.ppermute(four, 'core', shift(2, 1))]
    ppermute x3 -> x2, starting transfers between devices: 2.3 us -> 2.03 us  [gather_panels(): lax.ppermute(across, 'x', shift(4, d))]
  transfers between devices with their start and end apart: 17 -> 18, of which waited for: 9 -> 8; matrix products, arithmetic and copies ran while one was open for 0% -> 0% of each run, Pallas kernels for 10% -> 10%
where the time goes in v7:
time: 73 us; the launch traced here: 72.5 us
  starting transfers between devices  28.1 us (38%)
  blocking collectives  19.2 us (26%)
  waiting for transfers between devices  12.2 us (17%)
  Pallas kernels  11.7 us (16%)
  local copies, waits for them, and re-layouts  1.05 us (1%)
    all_to_all x1, blocking collectives, gather_panels(): held = lax.all_to_all(pieces, ROW, 0, 0)  19.2 us
    ppermute x3, starting transfers between devices, per_device(): got = [lax.ppermute(c, 'z', shift(8, d)) for c, d in zip(met_far, FAR)]  11.4 us
    ppermute x4, starting transfers between devices, per_device(): lax.ppermute(c, 'z', shift(8, d))  6.24 us
    pallas_call x1, Pallas kernels, per_device(): pl.pallas_call(home_kernel, out_shape=jax.ShapeDtypeStruct((TALL, 8 * SLO...  3.95 us
    ppermute x3, starting transfers between devices, gather_panels(): lax.ppermute(mine, 'x', shift(4, d))  3.01 us
    pallas_call x1, Pallas kernels, per_device(): pl.pallas_call(away_near_kernel, out_shape=codes(near), in_specs=[VMEM, H...  2.99 us
    ppermute x4, waiting for transfers between devices, per_device(): lax.ppermute(c, 'z', shift(8, d))  2.91 us
    ppermute x1, waiting for transfers between devices, gather_panels(): across = lax.ppermute(mine, 'yh', shift(2, 1))  2.59 us
  transfers between devices with their start and end apart: 18, of which 8 were waited for; matrix products, arithmetic and copies ran while one was open for 0% of the time, Pallas kernels for 10%

profile of v7, /device:TPU:32, one launch (start us, length us, event | category | flops | bytes accessed | tf_op | source)
XLA Modules:
  0.0 72.5 jit_solution(3556626129691006487)
XLA Ops:
  0.0 1.0 %copy-done = bf16[100,2560]{1,0:T(8,128)(2,1)S(1)} copy-done((bf16[100,2560]{1,0:T(8,128)(2,1)S(1)}, bf16[100,2560]{1,0:T(8,128)(2,1)}, u32[]{:S(2)}) %copy-start) | copy-done | bytes 512024
  1.0 0.3 cut.1
  1.3 19.2 %all_to_all.5.held = bf16[16,128,128]{2,1,0:T(8,128)(2,1)S(1)} all-to-all(bf16[16,128,128]{2,1,0:T(8,128)(2,1)S(1)} %cut.1), channel_id=1, replica_groups=mesh['yh'=2,'x'=4,'core'=2,'yl'=2,'z'=8] {'yh','x','core'}, dimensions={0} | all-to-all | bytes 1048576 | tf_op jit(solution)/shard_map/all_to_all | solution.py:63
  20.5 0.6 pick.1
  21.1 0.6 collective-permute-start.3
  21.8 1.0 %collective-permute-start.1 = (bf16[80,640]{1,0:T(8,128)(2,1)S(1)}, bf16[80,640]{1,0:T(8,128)(2,1)S(1)}, u32[]{:S(2)}, u32[]{:S(2)}) collective-permute-start(bf16[80,640]{1,0:T(8,128)(2,1)S(1)} %get-tuple-element.20), channel_id=1, source_target_pairs={{0,64},{32,96},{64,0},{96,32},{1,65},{33,97},{65,1},{97,33},{2,66}... | collective-permute-start | bytes 307208 | tf_op jit(solution)/shard_map/ppermute | solution.py:73
  22.8 1.4 %collective-permute-start.2 = (bf16[80,640]{1,0:T(8,128)(2,1)S(1)}, bf16[80,640]{1,0:T(8,128)(2,1)S(1)}, u32[]{:S(2)}, u32[]{:S(2)}) collective-permute-start(bf16[80,640]{1,0:T(8,128)(2,1)S(1)} %get-tuple-element.20), channel_id=1, source_target_pairs={{0,96},{32,0},{64,32},{96,64},{1,97},{33,1},{65,33},{97,65},{2,98}... | collective-permute-start | bytes 307208 | tf_op jit(solution)/shard_map/ppermute | solution.py:73
  24.1 0.6 collective-permute-start
  24.8 2.6 %collective-permute-done.3 = bf16[80,640]{1,0:T(8,128)(2,1)S(1)} collective-permute-done((bf16[80,640]{1,0:T(8,128)(2,1)S(1)}, bf16[80,640]{1,0:T(8,128)(2,1)S(1)}, u32[]{:S(2)}, u32[]{:S(2)}) %collective-permute-start.3) | collective-permute-done | bytes 102432 | tf_op jit(solution)/shard_map/ppermute | solution.py:72
  27.4 1.1 %collective-permute-start.6 = (bf16[80,640]{1,0:T(8,128)(2,1)S(1)}, bf16[80,640]{1,0:T(8,128)(2,1)S(1)}, u32[]{:S(2)}, u32[]{:S(2)}) collective-permute-start(bf16[80,640]{1,0:T(8,128)(2,1)S(1)} %collective-permute-done.3), channel_id=1, source_target_pairs={{0,96},{32,0},{64,32},{96,64},{1,97},{33,1},{65,33},{97,65},{2,98}... | collective-permute-start | bytes 307208 | tf_op jit(solution)/shard_map/ppermute | solution.py:74
  28.4 1.0 %collective-permute-start.4 = (bf16[80,640]{1,0:T(8,128)(2,1)S(1)}, bf16[80,640]{1,0:T(8,128)(2,1)S(1)}, u32[]{:S(2)}, u32[]{:S(2)}) collective-permute-start(bf16[80,640]{1,0:T(8,128)(2,1)S(1)} %collective-permute-done.3), channel_id=1, source_target_pairs={{0,32},{32,64},{64,96},{96,0},{1,33},{33,65},{65,97},{97,1},{2,34}... | collective-permute-start | bytes 307208 | tf_op jit(solution)/shard_map/ppermute | solution.py:74
  29.4 2.5 %collective-permute-start.5 = (bf16[80,640]{1,0:T(8,128)(2,1)S(1)}, bf16[80,640]{1,0:T(8,128)(2,1)S(1)}, u32[]{:S(2)}, u32[]{:S(2)}) collective-permute-start(bf16[80,640]{1,0:T(8,128)(2,1)S(1)} %collective-permute-done.1), channel_id=1, source_target_pairs={{0,128},{128,0},{1,129},{129,1},{2,130},{130,2},{3,131},{131,3},{4... | collective-permute-start | bytes 307208 | tf_op jit(solution)/shard_map/ppermute | solution.py:75
  32.1 2.2 %collective-permute-done.4 = bf16[80,640]{1,0:T(8,128)(2,1)S(1)} collective-permute-done((bf16[80,640]{1,0:T(8,128)(2,1)S(1)}, bf16[80,640]{1,0:T(8,128)(2,1)S(1)}, u32[]{:S(2)}, u32[]{:S(2)}) %collective-permute-start.4) | collective-permute-done | bytes 102432 | tf_op jit(solution)/shard_map/ppermute | solution.py:74
  34.3 1.3 %collective-permute-done.5 = bf16[80,640]{1,0:T(8,128)(2,1)S(1)} collective-permute-done((bf16[80,640]{1,0:T(8,128)(2,1)S(1)}, bf16[80,640]{1,0:T(8,128)(2,1)S(1)}, u32[]{:S(2)}, u32[]{:S(2)}) %collective-permute-start.5) | collective-permute-done | bytes 102432 | tf_op jit(solution)/shard_map/ppermute | solution.py:75
  35.7 1.7 %collective-permute-done.8.d = bf16[4,80,640]{2,1,0:T(8,128)(2,1)S(1)} collective-permute-done((bf16[4,80,640]{2,1,0:T(8,128)(2,1)S(1)}, bf16[4,80,640]{2,1,0:T(8,128)(2,1)S(1)}, u32[]{:S(2)}, u32[]{:S(2)}) %collective-permute-start.8) | collective-permute-done | bytes 409632 | tf_op jit(solution)/shard_map/ppermute | solution.py:77
  37.5 2.6 %away_far.1 = (s16[3,304,128]{2,1,0:T(8,128)(2,1)S(1)}, bf16[304,2560]{1,0:T(8,128)(2,1)S(1)}) custom-call(bf16[4,80,640]{2,1,0:T(8,128)(2,1)S(1)} %pad_maximum_fusion.a, bf16[4,80,640]{2,1,0:T(8,128)(2,1)S(1)} %pad_maximum_fusion.1.b, bf16[4,80,640]{2,1,0:T(8,128)(2,1)S(1)} %collective-permute-done.7.c, bf16[4,80,640]{2,1,0:T(8,128)(2,1)S(1)} %collective-permute-done.8.d, ...), custom_call_target="tpu_custom_call" | custom-call | flops 597688320 | bytes 1966080 | tf_op jit(solution)/shard_map/away_far/pallas_call | solution.py:218
  40.1 0.8 %collective-permute-start.9 = (s16[3,304,128]{2,1,0:T(8,128)(2,1)S(1)}, s16[3,304,128]{2,1,0:T(8,128)(2,1)S(1)}, u32[]{:S(2)}, u32[]{:S(2)}) collective-permute-start(s16[3,304,128]{2,1,0:T(8,128)(2,1)S(1)} %get-tuple-element.21), channel_id=1, source_target_pairs={{0,8},{8,0},{1,9},{9,1},{2,10},{10,2},{3,11},{11,3},{4,12},{12,4},... | collective-permute-start | bytes 700424 | tf_op jit(solution)/shard_map/ppermute | solution.py:228
  40.8 3.0 %away_near.1.after = s16[5,304,128]{2,1,0:T(8,128)(2,1)S(1)} custom-call(bf16[304,2560]{1,0:T(8,128)(2,1)S(1)} %get-tuple-element.22.left, bf16[2048,2560]{1,0:T(8,128)(2,1)} %integrals.5), custom_call_target="tpu_custom_call" | custom-call | flops 996147200 | bytes 3276800 | tf_op jit(solution)/shard_map/away_near/pallas_call | solution.py:229
  43.8 3.9 %home.1.kept = f32[304,1024]{1,0:T(8,128)S(1)} custom-call(bf16[304,2560]{1,0:T(8,128)(2,1)S(1)} %get-tuple-element.22.left, bf16[2048,2560]{1,0:T(8,128)(2,1)} %integrals.5, s16[5,304,128]{2,1,0:T(8,128)(2,1)S(1)} %away_near.1.after), custom_call_target="tpu_custom_call" | custom-call | flops 1593835520 | bytes 5242880 | tf_op jit(solution)/shard_map/home/pallas_call | solution.py:239
  47.9 1.4 %collective-permute-start.13 = (s16[5,304,128]{2,1,0:T(8,128)(2,1)S(1)}, s16[5,304,128]{2,1,0:T(8,128)(2,1)S(1)}, u32[]{:S(2)}, u32[]{:S(2)}) collective-permute-start(s16[5,304,128]{2,1,0:T(8,128)(2,1)S(1)} %away_near.1.after), channel_id=1, source_target_pairs={{0,8},{8,0},{1,9},{9,1},{2,10},{10,2},{3,11},{11,3},{4,12},{12,4},... | collective-permute-start | bytes 1167368 | tf_op jit(solution)/shard_map/ppermute | solution.py:250
  49.2 0.2 meet_far.1
  49.4 5.9 %collective-permute-start.11 = (s16[304,128]{1,0:T(8,128)(2,1)S(1)}, s16[304,128]{1,0:T(8,128)(2,1)S(1)}, u32[]{:S(2)}, u32[]{:S(2)}) collective-permute-start(s16[304,128]{1,0:T(8,128)(2,1)S(1)} %get-tuple-element.26), channel_id=1, source_target_pairs={{0,3},{1,4},{2,5},{3,6},{4,7},{5,0},{6,1},{7,2},{8,11},{9,12},{10,... | collective-permute-start | bytes 233480 | tf_op jit(solution)/shard_map/ppermute | solution.py:267
  55.3 0.3 collective-permute-start.12
  55.6 5.2 %collective-permute-start.10 = (s16[304,128]{1,0:T(8,128)(2,1)S(1)}, s16[304,128]{1,0:T(8,128)(2,1)S(1)}, u32[]{:S(2)}, u32[]{:S(2)}) collective-permute-start(s16[304,128]{1,0:T(8,128)(2,1)S(1)} %get-tuple-element.25.after), channel_id=1, source_target_pairs={{0,4},{1,5},{2,6},{3,7},{4,0},{5,1},{6,2},{7,3},{8,12},{9,13},{10,... | collective-permute-start | bytes 233480 | tf_op jit(solution)/shard_map/ppermute | solution.py:267
  60.8 0.2 meet_near.1
  61.0 1.2 %collective-permute-start.14 = (s16[304,128]{1,0:T(8,128)(2,1)S(1)}, s16[304,128]{1,0:T(8,128)(2,1)S(1)}, u32[]{:S(2)}, u32[]{:S(2)}) collective-permute-start(s16[304,128]{1,0:T(8,128)(2,1)S(1)} %get-tuple-element.29), channel_id=1, source_target_pairs={{0,2},{1,3},{2,4},{3,5},{4,6},{5,7},{6,0},{7,1},{8,10},{9,11},{10,... | collective-permute-start | bytes 233480 | tf_op jit(solution)/shard_map/ppermute | solution.py:268
  62.3 3.0 %collective-permute-start.15 = (s16[304,128]{1,0:T(8,128)(2,1)S(1)}, s16[304,128]{1,0:T(8,128)(2,1)S(1)}, u32[]{:S(2)}, u32[]{:S(2)}) collective-permute-start(s16[304,128]{1,0:T(8,128)(2,1)S(1)} %get-tuple-element.30), channel_id=1, source_target_pairs={{0,6},{1,7},{2,0},{3,1},{4,2},{5,3},{6,4},{7,5},{8,14},{9,15},{10,... | collective-permute-start | bytes 233480 | tf_op jit(solution)/shard_map/ppermute | solution.py:268
  65.4 1.9 %collective-permute-start.17 = (s16[304,128]{1,0:T(8,128)(2,1)S(1)}, s16[304,128]{1,0:T(8,128)(2,1)S(1)}, u32[]{:S(2)}, u32[]{:S(2)}) collective-permute-start(s16[304,128]{1,0:T(8,128)(2,1)S(1)} %get-tuple-element.32), channel_id=1, source_target_pairs={{0,7},{1,0},{2,1},{3,2},{4,3},{5,4},{6,5},{7,6},{8,15},{9,8},{10,9... | collective-permute-start | bytes 233480 | tf_op jit(solution)/shard_map/ppermute | solution.py:268
  67.3 1.4 %collective-permute-done.10.refs_0_ = s16[304,128]{1,0:T(8,128)(2,1)S(1)} collective-permute-done((s16[304,128]{1,0:T(8,128)(2,1)S(1)}, s16[304,128]{1,0:T(8,128)(2,1)S(1)}, u32[]{:S(2)}, u32[]{:S(2)}) %collective-permute-start.10) | collective-permute-done | bytes 77856 | tf_op jit(solution)/shard_map/ppermute | solution.py:267
  68.7 0.5 collective-permute-done.14.refs_3_
  69.2 2.4 %collective-permute-done.15.refs_4_ = s16[304,128]{1,0:T(8,128)(2,1)S(1)} collective-permute-done((s16[304,128]{1,0:T(8,128)(2,1)S(1)}, s16[304,128]{1,0:T(8,128)(2,1)S(1)}, u32[]{:S(2)}, u32[]{:S(2)}) %collective-permute-start.15) | collective-permute-done | bytes 77856 | tf_op jit(solution)/shard_map/ppermute | solution.py:268
  71.6 0.9 %sum.1 = f32[3,100,128]{2,1,0:T(8,128)} custom-call(s16[304,128]{1,0:T(8,128)(2,1)S(1)} %collective-permute-done.10.refs_0_, s16[304,128]{1,0:T(8,128)(2,1)S(1)} %collective-permute-done.11.refs_1_, s16[304,128]{1,0:T(8,128)(2,1)S(1)} %collective-permute-done.12.refs_2_, s16[304,128]{1,0:T(8,128)(2,1)S(1)} %collective-permute-done.14.refs_3_, ...), custom_call_target="tpu_custom_call" | custom-call | tf_op jit(solution)/shard_map/sum/pallas_call | solution.py:269
  (21 shorter events, 0.6 us)
Async XLA Ops:
  0.0 1.0 %copy-start = (bf16[100,2560]{1,0:T(8,128)(2,1)S(1)}, bf16[100,2560]{1,0:T(8,128)(2,1)}, u32[]{:S(2)}) copy-start(bf16[100,2560]{1,0:T(8,128)(2,1)} %panel.1) | copy-start | bytes 1536004
  1.0 19.5 %copy-start.1 = (s32[3]{0:T(128)S(1)}, s32[3]{0:T(128)}, u32[]{:S(2)}) copy-start(s32[3]{0:T(128)} %owner.1) | copy-start | bytes 40
  1.0 19.5 %copy-start.2 = (s32[17]{0:T(128)S(1)}, s32[17]{0:T(128)}, u32[]{:S(2)}) copy-start(s32[17]{0:T(128)} %offsets.1) | copy-start | bytes 208
  21.1 6.3 %collective-permute-start.3 = (bf16[80,640]{1,0:T(8,128)(2,1)S(1)}, bf16[80,640]{1,0:T(8,128)(2,1)S(1)}, u32[]{:S(2)}, u32[]{:S(2)}) collective-permute-start(bf16[80,640]{1,0:T(8,128)(2,1)S(1)} %get-tuple-element.20), channel_id=1, source_target_pairs={{0,128},{128,0},{1,129},{129,1},{2,130},{130,2},{3,131},{131,3},{4... | collective-permute-start | bytes 307208 | tf_op jit(solution)/shard_map/ppermute | solution.py:72
  21.8 7.6 %collective-permute-start.1 = (bf16[80,640]{1,0:T(8,128)(2,1)S(1)}, bf16[80,640]{1,0:T(8,128)(2,1)S(1)}, u32[]{:S(2)}, u32[]{:S(2)}) collective-permute-start(bf16[80,640]{1,0:T(8,128)(2,1)S(1)} %get-tuple-element.20), channel_id=1, source_target_pairs={{0,64},{32,96},{64,0},{96,32},{1,65},{33,97},{65,1},{97,33},{2,66}... | collective-permute-start | bytes 307208 | tf_op jit(solution)/shard_map/ppermute | solution.py:73
  22.8 9.2 %collective-permute-start.2 = (bf16[80,640]{1,0:T(8,128)(2,1)S(1)}, bf16[80,640]{1,0:T(8,128)(2,1)S(1)}, u32[]{:S(2)}, u32[]{:S(2)}) collective-permute-start(bf16[80,640]{1,0:T(8,128)(2,1)S(1)} %get-tuple-element.20), channel_id=1, source_target_pairs={{0,96},{32,0},{64,32},{96,64},{1,97},{33,1},{65,33},{97,65},{2,98}... | collective-permute-start | bytes 307208 | tf_op jit(solution)/shard_map/ppermute | solution.py:73
  24.1 7.8 %collective-permute-start = (bf16[80,640]{1,0:T(8,128)(2,1)S(1)}, bf16[80,640]{1,0:T(8,128)(2,1)S(1)}, u32[]{:S(2)}, u32[]{:S(2)}) collective-permute-start(bf16[80,640]{1,0:T(8,128)(2,1)S(1)} %get-tuple-element.20), channel_id=1, source_target_pairs={{0,32},{32,64},{64,96},{96,0},{1,33},{33,65},{65,97},{97,1},{2,34}... | collective-permute-start | bytes 307208 | tf_op jit(solution)/shard_map/ppermute | solution.py:73
  27.4 4.7 %collective-permute-start.6 = (bf16[80,640]{1,0:T(8,128)(2,1)S(1)}, bf16[80,640]{1,0:T(8,128)(2,1)S(1)}, u32[]{:S(2)}, u32[]{:S(2)}) collective-permute-start(bf16[80,640]{1,0:T(8,128)(2,1)S(1)} %collective-permute-done.3), channel_id=1, source_target_pairs={{0,96},{32,0},{64,32},{96,64},{1,97},{33,1},{65,33},{97,65},{2,98}... | collective-permute-start | bytes 307208 | tf_op jit(solution)/shard_map/ppermute | solution.py:74
  28.4 5.9 %collective-permute-start.4 = (bf16[80,640]{1,0:T(8,128)(2,1)S(1)}, bf16[80,640]{1,0:T(8,128)(2,1)S(1)}, u32[]{:S(2)}, u32[]{:S(2)}) collective-permute-start(bf16[80,640]{1,0:T(8,128)(2,1)S(1)} %collective-permute-done.3), channel_id=1, source_target_pairs={{0,32},{32,64},{64,96},{96,0},{1,33},{33,65},{65,97},{97,1},{2,34}... | collective-permute-start | bytes 307208 | tf_op jit(solution)/shard_map/ppermute | solution.py:74
  29.4 6.2 %collective-permute-start.5 = (bf16[80,640]{1,0:T(8,128)(2,1)S(1)}, bf16[80,640]{1,0:T(8,128)(2,1)S(1)}, u32[]{:S(2)}, u32[]{:S(2)}) collective-permute-start(bf16[80,640]{1,0:T(8,128)(2,1)S(1)} %collective-permute-done.1), channel_id=1, source_target_pairs={{0,128},{128,0},{1,129},{129,1},{2,130},{130,2},{3,131},{131,3},{4... | collective-permute-start | bytes 307208 | tf_op jit(solution)/shard_map/ppermute | solution.py:75
  32.0 3.8 %collective-permute-start.7 = (bf16[4,80,640]{2,1,0:T(8,128)(2,1)S(1)}, bf16[4,80,640]{2,1,0:T(8,128)(2,1)S(1)}, u32[]{:S(2)}, u32[]{:S(2)}) collective-permute-start(bf16[4,80,640]{2,1,0:T(8,128)(2,1)S(1)} %pad_maximum_fusion.a), channel_id=1, source_target_pairs={{0,16},{16,0},{1,17},{17,1},{2,18},{18,2},{3,19},{19,3},{4,20},{20... | collective-permute-start | bytes 1228808 | tf_op jit(solution)/shard_map/ppermute | solution.py:77
  35.6 1.8 %collective-permute-start.8 = (bf16[4,80,640]{2,1,0:T(8,128)(2,1)S(1)}, bf16[4,80,640]{2,1,0:T(8,128)(2,1)S(1)}, u32[]{:S(2)}, u32[]{:S(2)}) collective-permute-start(bf16[4,80,640]{2,1,0:T(8,128)(2,1)S(1)} %pad_maximum_fusion.1.b), channel_id=1, source_target_pairs={{0,16},{16,0},{1,17},{17,1},{2,18},{18,2},{3,19},{19,3},{4,20},{20... | collective-permute-start | bytes 1228808 | tf_op jit(solution)/shard_map/ppermute | solution.py:77
  40.1 7.8 %collective-permute-start.9 = (s16[3,304,128]{2,1,0:T(8,128)(2,1)S(1)}, s16[3,304,128]{2,1,0:T(8,128)(2,1)S(1)}, u32[]{:S(2)}, u32[]{:S(2)}) collective-permute-start(s16[3,304,128]{2,1,0:T(8,128)(2,1)S(1)} %get-tuple-element.21), channel_id=1, source_target_pairs={{0,8},{8,0},{1,9},{9,1},{2,10},{10,2},{3,11},{11,3},{4,12},{12,4},... | collective-permute-start | bytes 700424 | tf_op jit(solution)/shard_map/ppermute | solution.py:228
  47.9 12.9 %collective-permute-start.13 = (s16[5,304,128]{2,1,0:T(8,128)(2,1)S(1)}, s16[5,304,128]{2,1,0:T(8,128)(2,1)S(1)}, u32[]{:S(2)}, u32[]{:S(2)}) collective-permute-start(s16[5,304,128]{2,1,0:T(8,128)(2,1)S(1)} %away_near.1.after), channel_id=1, source_target_pairs={{0,8},{8,0},{1,9},{9,1},{2,10},{10,2},{3,11},{11,3},{4,12},{12,4},... | collective-permute-start | bytes 1167368 | tf_op jit(solution)/shard_map/ppermute | solution.py:250
  49.4 15.9 %collective-permute-start.11 = (s16[304,128]{1,0:T(8,128)(2,1)S(1)}, s16[304,128]{1,0:T(8,128)(2,1)S(1)}, u32[]{:S(2)}, u32[]{:S(2)}) collective-permute-start(s16[304,128]{1,0:T(8,128)(2,1)S(1)} %get-tuple-element.26), channel_id=1, source_target_pairs={{0,3},{1,4},{2,5},{3,6},{4,7},{5,0},{6,1},{7,2},{8,11},{9,12},{10,... | collective-permute-start | bytes 233480 | tf_op jit(solution)/shard_map/ppermute | solution.py:267
  55.3 10.1 %collective-permute-start.12 = (s16[304,128]{1,0:T(8,128)(2,1)S(1)}, s16[304,128]{1,0:T(8,128)(2,1)S(1)}, u32[]{:S(2)}, u32[]{:S(2)}) collective-permute-start(s16[304,128]{1,0:T(8,128)(2,1)S(1)} %get-tuple-element.27), channel_id=1, source_target_pairs={{0,5},{1,6},{2,7},{3,0},{4,1},{5,2},{6,3},{7,4},{8,13},{9,14},{10,... | collective-permute-start | bytes 233480 | tf_op jit(solution)/shard_map/ppermute | solution.py:267
  55.6 13.1 %collective-permute-start.10 = (s16[304,128]{1,0:T(8,128)(2,1)S(1)}, s16[304,128]{1,0:T(8,128)(2,1)S(1)}, u32[]{:S(2)}, u32[]{:S(2)}) collective-permute-start(s16[304,128]{1,0:T(8,128)(2,1)S(1)} %get-tuple-element.25.after), channel_id=1, source_target_pairs={{0,4},{1,5},{2,6},{3,7},{4,0},{5,1},{6,2},{7,3},{8,12},{9,13},{10,... | collective-permute-start | bytes 233480 | tf_op jit(solution)/shard_map/ppermute | solution.py:267
  61.0 8.1 %collective-permute-start.14 = (s16[304,128]{1,0:T(8,128)(2,1)S(1)}, s16[304,128]{1,0:T(8,128)(2,1)S(1)}, u32[]{:S(2)}, u32[]{:S(2)}) collective-permute-start(s16[304,128]{1,0:T(8,128)(2,1)S(1)} %get-tuple-element.29), channel_id=1, source_target_pairs={{0,2},{1,3},{2,4},{3,5},{4,6},{5,7},{6,0},{7,1},{8,10},{9,11},{10,... | collective-permute-start | bytes 233480 | tf_op jit(solution)/shard_map/ppermute | solution.py:268
  62.3 9.4 %collective-permute-start.15 = (s16[304,128]{1,0:T(8,128)(2,1)S(1)}, s16[304,128]{1,0:T(8,128)(2,1)S(1)}, u32[]{:S(2)}, u32[]{:S(2)}) collective-permute-start(s16[304,128]{1,0:T(8,128)(2,1)S(1)} %get-tuple-element.30), channel_id=1, source_target_pairs={{0,6},{1,7},{2,0},{3,1},{4,2},{5,3},{6,4},{7,5},{8,14},{9,15},{10,... | collective-permute-start | bytes 233480 | tf_op jit(solution)/shard_map/ppermute | solution.py:268
  65.3 6.4 %collective-permute-start.16 = (s16[304,128]{1,0:T(8,128)(2,1)S(1)}, s16[304,128]{1,0:T(8,128)(2,1)S(1)}, u32[]{:S(2)}, u32[]{:S(2)}) collective-permute-start(s16[304,128]{1,0:T(8,128)(2,1)S(1)} %get-tuple-element.31), channel_id=1, source_target_pairs={{0,1},{1,2},{2,3},{3,4},{4,5},{5,6},{6,7},{7,0},{8,9},{9,10},{10,1... | collective-permute-start | bytes 233480 | tf_op jit(solution)/shard_map/ppermute | solution.py:268
  65.4 6.2 %collective-permute-start.17 = (s16[304,128]{1,0:T(8,128)(2,1)S(1)}, s16[304,128]{1,0:T(8,128)(2,1)S(1)}, u32[]{:S(2)}, u32[]{:S(2)}) collective-permute-start(s16[304,128]{1,0:T(8,128)(2,1)S(1)} %get-tuple-element.32), channel_id=1, source_target_pairs={{0,7},{1,0},{2,1},{3,2},{4,3},{5,4},{6,5},{7,6},{8,15},{9,8},{10,9... | collective-permute-start | bytes 233480 | tf_op jit(solution)/shard_map/ppermute | solution.py:268

commit v8 on v7

--- a/solution.py
+++ b/solution.py
@@ -32,12 +32,18 @@
     return [(i, (i + by) % size) for i in range(size)]
 
 
-def cut_kernel(panel, pieces):
-    for yh in range(2):
-        for core in range(2):
-            for x in range(4):
+def cut_kernel(panel, pieces, near, sems):
+    copies = []
+    for x in range(4):
+        columns = pl.ds(x * KB, KB)
+        copies.append(pltpu.make_async_copy(panel.at[:, columns], near.at[:, columns], sems.at[x]))
+        copies[-1].start()
+    for x in range(4):
+        copies[x].wait()
+        for yh in range(2):
+            for core in range(2):
                 for t in range(TILES):
-                    block = panel[pl.ds((yh * 2 + core) * RB, RB), pl.ds(x * KB + t * 128, 128)]
+                    block = near[pl.ds((yh * 2 + core) * RB, RB), pl.ds(x * KB + t * 128, 128)]
                     pieces[yh * 8 + x * 2 + core, pl.ds(t * RB, RB), :] = block
 
 
@@ -55,9 +61,10 @@
     pieces = pl.pallas_call(
         cut_kernel,
         out_shape=jax.ShapeDtypeStruct((16, 128, 128), jnp.bfloat16),
-        in_specs=[VMEM],
-        out_specs=VMEM,
-        compiler_params=SMALL,
+        in_specs=[HBM],
+        out_specs=VMEM,
+        scratch_shapes=[pltpu.VMEM((4 * RB, 4 * KB), jnp.bfloat16), pltpu.SemaphoreType.DMA((4,))],
+        compiler_params=pltpu.CompilerParams(vmem_limit_bytes=61 << 20),
         name="cut",
     )(amplitudes)
     held = lax.all_to_all(pieces, ROW, 0, 0)

time: 73 us -> 74 us (1.014)
  Pallas kernels: 11.7 us -> 13.5 us
  local copies, waits for them, and re-layouts: 1.05 us -> 0.01 us
    pallas_call x1, Pallas kernels: 0.26 us -> 2.05 us  [gather_panels(): pl.pallas_call(cut_kernel, out_shape=jax.ShapeDtypeStruct((16, 128, 128),...]
    unnamed x6 -> x4, local copies, waits for them, and re-layouts: 1.05 us -> 0.01 us
where the time goes in v8:
time: 74 us; the launch traced here: 73.5 us
  starting transfers between devices  28.1 us (38%)
  blocking collectives  19.4 us (26%)
  Pallas kernels  13.5 us (18%)
  waiting for transfers between devices  12.2 us (16%)
    all_to_all x1, blocking collectives, gather_panels(): held = lax.all_to_all(pieces, ROW, 0, 0)  19.4 us
    ppermute x3, starting transfers between devices, per_device(): got = [lax.ppermute(c, 'z', shift(8, d)) for c, d in zip(met_far, FAR)]  11.4 us
    ppermute x4, starting transfers between devices, per_device(): lax.ppermute(c, 'z', shift(8, d))  6.24 us
    pallas_call x1, Pallas kernels, per_device(): pl.pallas_call(home_kernel, out_shape=jax.ShapeDtypeStruct((TALL, 8 * SLO...  3.94 us
    ppermute x3, starting transfers between devices, gather_panels(): lax.ppermute(mine, 'x', shift(4, d))  3.01 us
    pallas_call x1, Pallas kernels, per_device(): pl.pallas_call(away_near_kernel, out_shape=codes(near), in_specs=[VMEM, H...  2.99 us
    ppermute x4, waiting for transfers between devices, per_device(): lax.ppermute(c, 'z', shift(8, d))  2.89 us
    ppermute x1, waiting for transfers between devices, gather_panels(): across = lax.ppermute(mine, 'yh', shift(2, 1))  2.59 us
  transfers between devices with their start and end apart: 18, of which 8 were waited for; matrix products, arithmetic and copies ran while one was open for 0% of the time, Pallas kernels for 10%

profile of v8, /device:TPU:32, one launch (start us, length us, event | category | flops | bytes accessed | tf_op | source)
XLA Modules:
  0.0 73.5 jit_solution(9044167953437953467)
XLA Ops:
  0.0 2.1 %cut.1 = bf16[16,128,128]{2,1,0:T(8,128)(2,1)} custom-call(bf16[100,2560]{1,0:T(8,128)(2,1)} %panel.1), custom_call_target="tpu_custom_call" | custom-call | tf_op jit(solution)/shard_map/cut/pallas_call | solution.py:61
  2.1 19.4 %all_to_all.5.held = bf16[16,128,128]{2,1,0:T(8,128)(2,1)S(1)} all-to-all(bf16[16,128,128]{2,1,0:T(8,128)(2,1)} %cut.1), channel_id=1, replica_groups=mesh['yh'=2,'x'=4,'core'=2,'yl'=2,'z'=8] {'yh','x','core'}, dimensions={0} | all-to-all | bytes 1048576 | tf_op jit(solution)/shard_map/all_to_all | solution.py:70
  21.5 0.6 pick.1
  22.1 0.6 collective-permute-start.3
  22.7 1.0 %collective-permute-start.1 = (bf16[80,640]{1,0:T(8,128)(2,1)S(1)}, bf16[80,640]{1,0:T(8,128)(2,1)S(1)}, u32[]{:S(2)}, u32[]{:S(2)}) collective-permute-start(bf16[80,640]{1,0:T(8,128)(2,1)S(1)} %get-tuple-element.20), channel_id=1, source_target_pairs={{0,64},{32,96},{64,0},{96,32},{1,65},{33,97},{65,1},{97,33},{2,66}... | collective-permute-start | bytes 307208 | tf_op jit(solution)/shard_map/ppermute | solution.py:80
  23.7 1.4 %collective-permute-start.2 = (bf16[80,640]{1,0:T(8,128)(2,1)S(1)}, bf16[80,640]{1,0:T(8,128)(2,1)S(1)}, u32[]{:S(2)}, u32[]{:S(2)}) collective-permute-start(bf16[80,640]{1,0:T(8,128)(2,1)S(1)} %get-tuple-element.20), channel_id=1, source_target_pairs={{0,96},{32,0},{64,32},{96,64},{1,97},{33,1},{65,33},{97,65},{2,98}... | collective-permute-start | bytes 307208 | tf_op jit(solution)/shard_map/ppermute | solution.py:80
  25.1 0.6 collective-permute-start
  25.7 2.6 %collective-permute-done.3 = bf16[80,640]{1,0:T(8,128)(2,1)S(1)} collective-permute-done((bf16[80,640]{1,0:T(8,128)(2,1)S(1)}, bf16[80,640]{1,0:T(8,128)(2,1)S(1)}, u32[]{:S(2)}, u32[]{:S(2)}) %collective-permute-start.3) | collective-permute-done | bytes 102432 | tf_op jit(solution)/shard_map/ppermute | solution.py:79
  28.3 1.1 %collective-permute-start.6 = (bf16[80,640]{1,0:T(8,128)(2,1)S(1)}, bf16[80,640]{1,0:T(8,128)(2,1)S(1)}, u32[]{:S(2)}, u32[]{:S(2)}) collective-permute-start(bf16[80,640]{1,0:T(8,128)(2,1)S(1)} %collective-permute-done.3), channel_id=1, source_target_pairs={{0,96},{32,0},{64,32},{96,64},{1,97},{33,1},{65,33},{97,65},{2,98}... | collective-permute-start | bytes 307208 | tf_op jit(solution)/shard_map/ppermute | solution.py:81
  29.4 1.0 %collective-permute-start.4 = (bf16[80,640]{1,0:T(8,128)(2,1)S(1)}, bf16[80,640]{1,0:T(8,128)(2,1)S(1)}, u32[]{:S(2)}, u32[]{:S(2)}) collective-permute-start(bf16[80,640]{1,0:T(8,128)(2,1)S(1)} %collective-permute-done.3), channel_id=1, source_target_pairs={{0,32},{32,64},{64,96},{96,0},{1,33},{33,65},{65,97},{97,1},{2,34}... | collective-permute-start | bytes 307208 | tf_op jit(solution)/shard_map/ppermute | solution.py:81
  30.4 2.5 %collective-permute-start.5 = (bf16[80,640]{1,0:T(8,128)(2,1)S(1)}, bf16[80,640]{1,0:T(8,128)(2,1)S(1)}, u32[]{:S(2)}, u32[]{:S(2)}) collective-permute-start(bf16[80,640]{1,0:T(8,128)(2,1)S(1)} %collective-permute-done.1), channel_id=1, source_target_pairs={{0,128},{128,0},{1,129},{129,1},{2,130},{130,2},{3,131},{131,3},{4... | collective-permute-start | bytes 307208 | tf_op jit(solution)/shard_map/ppermute | solution.py:82
  33.1 2.2 %collective-permute-done.4 = bf16[80,640]{1,0:T(8,128)(2,1)S(1)} collective-permute-done((bf16[80,640]{1,0:T(8,128)(2,1)S(1)}, bf16[80,640]{1,0:T(8,128)(2,1)S(1)}, u32[]{:S(2)}, u32[]{:S(2)}) %collective-permute-start.4) | collective-permute-done | bytes 102432 | tf_op jit(solution)/shard_map/ppermute | solution.py:81
  35.3 1.3 %collective-permute-done.5 = bf16[80,640]{1,0:T(8,128)(2,1)S(1)} collective-permute-done((bf16[80,640]{1,0:T(8,128)(2,1)S(1)}, bf16[80,640]{1,0:T(8,128)(2,1)S(1)}, u32[]{:S(2)}, u32[]{:S(2)}) %collective-permute-start.5) | collective-permute-done | bytes 102432 | tf_op jit(solution)/shard_map/ppermute | solution.py:82
  36.7 1.7 %collective-permute-done.8.d = bf16[4,80,640]{2,1,0:T(8,128)(2,1)S(1)} collective-permute-done((bf16[4,80,640]{2,1,0:T(8,128)(2,1)S(1)}, bf16[4,80,640]{2,1,0:T(8,128)(2,1)S(1)}, u32[]{:S(2)}, u32[]{:S(2)}) %collective-permute-start.8) | collective-permute-done | bytes 409632 | tf_op jit(solution)/shard_map/ppermute | solution.py:84
  38.4 2.6 %away_far.1 = (s16[3,304,128]{2,1,0:T(8,128)(2,1)S(1)}, bf16[304,2560]{1,0:T(8,128)(2,1)S(1)}) custom-call(bf16[4,80,640]{2,1,0:T(8,128)(2,1)S(1)} %pad_maximum_fusion.a, bf16[4,80,640]{2,1,0:T(8,128)(2,1)S(1)} %pad_maximum_fusion.1.b, bf16[4,80,640]{2,1,0:T(8,128)(2,1)S(1)} %collective-permute-done.7.c, bf16[4,80,640]{2,1,0:T(8,128)(2,1)S(1)} %collective-permute-done.8.d, ...), custom_call_target="tpu_custom_call" | custom-call | flops 597688320 | bytes 1966080 | tf_op jit(solution)/shard_map/away_far/pallas_call | solution.py:225
  41.0 0.8 %collective-permute-start.9 = (s16[3,304,128]{2,1,0:T(8,128)(2,1)S(1)}, s16[3,304,128]{2,1,0:T(8,128)(2,1)S(1)}, u32[]{:S(2)}, u32[]{:S(2)}) collective-permute-start(s16[3,304,128]{2,1,0:T(8,128)(2,1)S(1)} %get-tuple-element.21), channel_id=1, source_target_pairs={{0,8},{8,0},{1,9},{9,1},{2,10},{10,2},{3,11},{11,3},{4,12},{12,4},... | collective-permute-start | bytes 700424 | tf_op jit(solution)/shard_map/ppermute | solution.py:235
  41.8 3.0 %away_near.1.after = s16[5,304,128]{2,1,0:T(8,128)(2,1)S(1)} custom-call(bf16[304,2560]{1,0:T(8,128)(2,1)S(1)} %get-tuple-element.22.left, bf16[2048,2560]{1,0:T(8,128)(2,1)} %integrals.5), custom_call_target="tpu_custom_call" | custom-call | flops 996147200 | bytes 3276800 | tf_op jit(solution)/shard_map/away_near/pallas_call | solution.py:236
  44.8 3.9 %home.1.kept = f32[304,1024]{1,0:T(8,128)S(1)} custom-call(bf16[304,2560]{1,0:T(8,128)(2,1)S(1)} %get-tuple-element.22.left, bf16[2048,2560]{1,0:T(8,128)(2,1)} %integrals.5, s16[5,304,128]{2,1,0:T(8,128)(2,1)S(1)} %away_near.1.after), custom_call_target="tpu_custom_call" | custom-call | flops 1593835520 | bytes 5242880 | tf_op jit(solution)/shard_map/home/pallas_call | solution.py:246
  48.8 1.4 %collective-permute-start.13 = (s16[5,304,128]{2,1,0:T(8,128)(2,1)S(1)}, s16[5,304,128]{2,1,0:T(8,128)(2,1)S(1)}, u32[]{:S(2)}, u32[]{:S(2)}) collective-permute-start(s16[5,304,128]{2,1,0:T(8,128)(2,1)S(1)} %away_near.1.after), channel_id=1, source_target_pairs={{0,8},{8,0},{1,9},{9,1},{2,10},{10,2},{3,11},{11,3},{4,12},{12,4},... | collective-permute-start | bytes 1167368 | tf_op jit(solution)/shard_map/ppermute | solution.py:257
  50.2 0.2 meet_far.1
  50.4 5.9 %collective-permute-start.11 = (s16[304,128]{1,0:T(8,128)(2,1)S(1)}, s16[304,128]{1,0:T(8,128)(2,1)S(1)}, u32[]{:S(2)}, u32[]{:S(2)}) collective-permute-start(s16[304,128]{1,0:T(8,128)(2,1)S(1)} %get-tuple-element.26), channel_id=1, source_target_pairs={{0,3},{1,4},{2,5},{3,6},{4,7},{5,0},{6,1},{7,2},{8,11},{9,12},{10,... | collective-permute-start | bytes 233480 | tf_op jit(solution)/shard_map/ppermute | solution.py:274
  56.3 0.3 collective-permute-start.12
  56.6 5.2 %collective-permute-start.10 = (s16[304,128]{1,0:T(8,128)(2,1)S(1)}, s16[304,128]{1,0:T(8,128)(2,1)S(1)}, u32[]{:S(2)}, u32[]{:S(2)}) collective-permute-start(s16[304,128]{1,0:T(8,128)(2,1)S(1)} %get-tuple-element.25.after), channel_id=1, source_target_pairs={{0,4},{1,5},{2,6},{3,7},{4,0},{5,1},{6,2},{7,3},{8,12},{9,13},{10,... | collective-permute-start | bytes 233480 | tf_op jit(solution)/shard_map/ppermute | solution.py:274
  61.7 0.2 meet_near.1
  62.0 1.2 %collective-permute-start.14 = (s16[304,128]{1,0:T(8,128)(2,1)S(1)}, s16[304,128]{1,0:T(8,128)(2,1)S(1)}, u32[]{:S(2)}, u32[]{:S(2)}) collective-permute-start(s16[304,128]{1,0:T(8,128)(2,1)S(1)} %get-tuple-element.29), channel_id=1, source_target_pairs={{0,2},{1,3},{2,4},{3,5},{4,6},{5,7},{6,0},{7,1},{8,10},{9,11},{10,... | collective-permute-start | bytes 233480 | tf_op jit(solution)/shard_map/ppermute | solution.py:275
  63.2 3.0 %collective-permute-start.15 = (s16[304,128]{1,0:T(8,128)(2,1)S(1)}, s16[304,128]{1,0:T(8,128)(2,1)S(1)}, u32[]{:S(2)}, u32[]{:S(2)}) collective-permute-start(s16[304,128]{1,0:T(8,128)(2,1)S(1)} %get-tuple-element.30), channel_id=1, source_target_pairs={{0,6},{1,7},{2,0},{3,1},{4,2},{5,3},{6,4},{7,5},{8,14},{9,15},{10,... | collective-permute-start | bytes 233480 | tf_op jit(solution)/shard_map/ppermute | solution.py:275
  66.2 0.2 collective-permute-start.16
  66.4 1.9 %collective-permute-start.17 = (s16[304,128]{1,0:T(8,128)(2,1)S(1)}, s16[304,128]{1,0:T(8,128)(2,1)S(1)}, u32[]{:S(2)}, u32[]{:S(2)}) collective-permute-start(s16[304,128]{1,0:T(8,128)(2,1)S(1)} %get-tuple-element.32), channel_id=1, source_target_pairs={{0,7},{1,0},{2,1},{3,2},{4,3},{5,4},{6,5},{7,6},{8,15},{9,8},{10,9... | collective-permute-start | bytes 233480 | tf_op jit(solution)/shard_map/ppermute | solution.py:275
  68.2 1.4 %collective-permute-done.10.refs_0_ = s16[304,128]{1,0:T(8,128)(2,1)S(1)} collective-permute-done((s16[304,128]{1,0:T(8,128)(2,1)S(1)}, s16[304,128]{1,0:T(8,128)(2,1)S(1)}, u32[]{:S(2)}, u32[]{:S(2)}) %collective-permute-start.10) | collective-permute-done | bytes 77856 | tf_op jit(solution)/shard_map/ppermute | solution.py:274
  69.7 0.4 collective-permute-done.14.refs_3_
  70.1 2.5 %collective-permute-done.15.refs_4_ = s16[304,128]{1,0:T(8,128)(2,1)S(1)} collective-permute-done((s16[304,128]{1,0:T(8,128)(2,1)S(1)}, s16[304,128]{1,0:T(8,128)(2,1)S(1)}, u32[]{:S(2)}, u32[]{:S(2)}) %collective-permute-start.15) | collective-permute-done | bytes 77856 | tf_op jit(solution)/shard_map/ppermute | solution.py:275
  72.6 0.9 %sum.1 = f32[3,100,128]{2,1,0:T(8,128)} custom-call(s16[304,128]{1,0:T(8,128)(2,1)S(1)} %collective-permute-done.10.refs_0_, s16[304,128]{1,0:T(8,128)(2,1)S(1)} %collective-permute-done.11.refs_1_, s16[304,128]{1,0:T(8,128)(2,1)S(1)} %collective-permute-done.12.refs_2_, s16[304,128]{1,0:T(8,128)(2,1)S(1)} %collective-permute-done.14.refs_3_, ...), custom_call_target="tpu_custom_call" | custom-call | tf_op jit(solution)/shard_map/sum/pallas_call | solution.py:276
  (19 shorter events, 0.4 us)
Async XLA Ops:
  0.0 21.5 %copy-start = (s32[3]{0:T(128)S(1)}, s32[3]{0:T(128)}, u32[]{:S(2)}) copy-start(s32[3]{0:T(128)} %owner.1) | copy-start | bytes 40
  0.0 21.5 %copy-start.1 = (s32[17]{0:T(128)S(1)}, s32[17]{0:T(128)}, u32[]{:S(2)}) copy-start(s32[17]{0:T(128)} %offsets.1) | copy-start | bytes 208
  22.1 6.3 %collective-permute-start.3 = (bf16[80,640]{1,0:T(8,128)(2,1)S(1)}, bf16[80,640]{1,0:T(8,128)(2,1)S(1)}, u32[]{:S(2)}, u32[]{:S(2)}) collective-permute-start(bf16[80,640]{1,0:T(8,128)(2,1)S(1)} %get-tuple-element.20), channel_id=1, source_target_pairs={{0,128},{128,0},{1,129},{129,1},{2,130},{130,2},{3,131},{131,3},{4... | collective-permute-start | bytes 307208 | tf_op jit(solution)/shard_map/ppermute | solution.py:79
  22.7 7.6 %collective-permute-start.1 = (bf16[80,640]{1,0:T(8,128)(2,1)S(1)}, bf16[80,640]{1,0:T(8,128)(2,1)S(1)}, u32[]{:S(2)}, u32[]{:S(2)}) collective-permute-start(bf16[80,640]{1,0:T(8,128)(2,1)S(1)} %get-tuple-element.20), channel_id=1, source_target_pairs={{0,64},{32,96},{64,0},{96,32},{1,65},{33,97},{65,1},{97,33},{2,66}... | collective-permute-start | bytes 307208 | tf_op jit(solution)/shard_map/ppermute | solution.py:80
  23.7 9.2 %collective-permute-start.2 = (bf16[80,640]{1,0:T(8,128)(2,1)S(1)}, bf16[80,640]{1,0:T(8,128)(2,1)S(1)}, u32[]{:S(2)}, u32[]{:S(2)}) collective-permute-start(bf16[80,640]{1,0:T(8,128)(2,1)S(1)} %get-tuple-element.20), channel_id=1, source_target_pairs={{0,96},{32,0},{64,32},{96,64},{1,97},{33,1},{65,33},{97,65},{2,98}... | collective-permute-start | bytes 307208 | tf_op jit(solution)/shard_map/ppermute | solution.py:80
  25.1 7.8 %collective-permute-start = (bf16[80,640]{1,0:T(8,128)(2,1)S(1)}, bf16[80,640]{1,0:T(8,128)(2,1)S(1)}, u32[]{:S(2)}, u32[]{:S(2)}) collective-permute-start(bf16[80,640]{1,0:T(8,128)(2,1)S(1)} %get-tuple-element.20), channel_id=1, source_target_pairs={{0,32},{32,64},{64,96},{96,0},{1,33},{33,65},{65,97},{97,1},{2,34}... | collective-permute-start | bytes 307208 | tf_op jit(solution)/shard_map/ppermute | solution.py:80
  28.3 4.7 %collective-permute-start.6 = (bf16[80,640]{1,0:T(8,128)(2,1)S(1)}, bf16[80,640]{1,0:T(8,128)(2,1)S(1)}, u32[]{:S(2)}, u32[]{:S(2)}) collective-permute-start(bf16[80,640]{1,0:T(8,128)(2,1)S(1)} %collective-permute-done.3), channel_id=1, source_target_pairs={{0,96},{32,0},{64,32},{96,64},{1,97},{33,1},{65,33},{97,65},{2,98}... | collective-permute-start | bytes 307208 | tf_op jit(solution)/shard_map/ppermute | solution.py:81
  29.4 5.9 %collective-permute-start.4 = (bf16[80,640]{1,0:T(8,128)(2,1)S(1)}, bf16[80,640]{1,0:T(8,128)(2,1)S(1)}, u32[]{:S(2)}, u32[]{:S(2)}) collective-permute-start(bf16[80,640]{1,0:T(8,128)(2,1)S(1)} %collective-permute-done.3), channel_id=1, source_target_pairs={{0,32},{32,64},{64,96},{96,0},{1,33},{33,65},{65,97},{97,1},{2,34}... | collective-permute-start | bytes 307208 | tf_op jit(solution)/shard_map/ppermute | solution.py:81
  30.4 6.2 %collective-permute-start.5 = (bf16[80,640]{1,0:T(8,128)(2,1)S(1)}, bf16[80,640]{1,0:T(8,128)(2,1)S(1)}, u32[]{:S(2)}, u32[]{:S(2)}) collective-permute-start(bf16[80,640]{1,0:T(8,128)(2,1)S(1)} %collective-permute-done.1), channel_id=1, source_target_pairs={{0,128},{128,0},{1,129},{129,1},{2,130},{130,2},{3,131},{131,3},{4... | collective-permute-start | bytes 307208 | tf_op jit(solution)/shard_map/ppermute | solution.py:82
  32.9 3.8 %collective-permute-start.7 = (bf16[4,80,640]{2,1,0:T(8,128)(2,1)S(1)}, bf16[4,80,640]{2,1,0:T(8,128)(2,1)S(1)}, u32[]{:S(2)}, u32[]{:S(2)}) collective-permute-start(bf16[4,80,640]{2,1,0:T(8,128)(2,1)S(1)} %pad_maximum_fusion.a), channel_id=1, source_target_pairs={{0,16},{16,0},{1,17},{17,1},{2,18},{18,2},{3,19},{19,3},{4,20},{20... | collective-permute-start | bytes 1228808 | tf_op jit(solution)/shard_map/ppermute | solution.py:84
  36.6 1.8 %collective-permute-start.8 = (bf16[4,80,640]{2,1,0:T(8,128)(2,1)S(1)}, bf16[4,80,640]{2,1,0:T(8,128)(2,1)S(1)}, u32[]{:S(2)}, u32[]{:S(2)}) collective-permute-start(bf16[4,80,640]{2,1,0:T(8,128)(2,1)S(1)} %pad_maximum_fusion.1.b), channel_id=1, source_target_pairs={{0,16},{16,0},{1,17},{17,1},{2,18},{18,2},{3,19},{19,3},{4,20},{20... | collective-permute-start | bytes 1228808 | tf_op jit(solution)/shard_map/ppermute | solution.py:84
  41.0 7.8 %collective-permute-start.9 = (s16[3,304,128]{2,1,0:T(8,128)(2,1)S(1)}, s16[3,304,128]{2,1,0:T(8,128)(2,1)S(1)}, u32[]{:S(2)}, u32[]{:S(2)}) collective-permute-start(s16[3,304,128]{2,1,0:T(8,128)(2,1)S(1)} %get-tuple-element.21), channel_id=1, source_target_pairs={{0,8},{8,0},{1,9},{9,1},{2,10},{10,2},{3,11},{11,3},{4,12},{12,4},... | collective-permute-start | bytes 700424 | tf_op jit(solution)/shard_map/ppermute | solution.py:235
  48.8 12.9 %collective-permute-start.13 = (s16[5,304,128]{2,1,0:T(8,128)(2,1)S(1)}, s16[5,304,128]{2,1,0:T(8,128)(2,1)S(1)}, u32[]{:S(2)}, u32[]{:S(2)}) collective-permute-start(s16[5,304,128]{2,1,0:T(8,128)(2,1)S(1)} %away_near.1.after), channel_id=1, source_target_pairs={{0,8},{8,0},{1,9},{9,1},{2,10},{10,2},{3,11},{11,3},{4,12},{12,4},... | collective-permute-start | bytes 1167368 | tf_op jit(solution)/shard_map/ppermute | solution.py:257
  50.4 15.9 %collective-permute-start.11 = (s16[304,128]{1,0:T(8,128)(2,1)S(1)}, s16[304,128]{1,0:T(8,128)(2,1)S(1)}, u32[]{:S(2)}, u32[]{:S(2)}) collective-permute-start(s16[304,128]{1,0:T(8,128)(2,1)S(1)} %get-tuple-element.26), channel_id=1, source_target_pairs={{0,3},{1,4},{2,5},{3,6},{4,7},{5,0},{6,1},{7,2},{8,11},{9,12},{10,... | collective-permute-start | bytes 233480 | tf_op jit(solution)/shard_map/ppermute | solution.py:274
  56.3 10.1 %collective-permute-start.12 = (s16[304,128]{1,0:T(8,128)(2,1)S(1)}, s16[304,128]{1,0:T(8,128)(2,1)S(1)}, u32[]{:S(2)}, u32[]{:S(2)}) collective-permute-start(s16[304,128]{1,0:T(8,128)(2,1)S(1)} %get-tuple-element.27), channel_id=1, source_target_pairs={{0,5},{1,6},{2,7},{3,0},{4,1},{5,2},{6,3},{7,4},{8,13},{9,14},{10,... | collective-permute-start | bytes 233480 | tf_op jit(solution)/shard_map/ppermute | solution.py:274
  56.6 13.1 %collective-permute-start.10 = (s16[304,128]{1,0:T(8,128)(2,1)S(1)}, s16[304,128]{1,0:T(8,128)(2,1)S(1)}, u32[]{:S(2)}, u32[]{:S(2)}) collective-permute-start(s16[304,128]{1,0:T(8,128)(2,1)S(1)} %get-tuple-element.25.after), channel_id=1, source_target_pairs={{0,4},{1,5},{2,6},{3,7},{4,0},{5,1},{6,2},{7,3},{8,12},{9,13},{10,... | collective-permute-start | bytes 233480 | tf_op jit(solution)/shard_map/ppermute | solution.py:274
  62.0 8.1 %collective-permute-start.14 = (s16[304,128]{1,0:T(8,128)(2,1)S(1)}, s16[304,128]{1,0:T(8,128)(2,1)S(1)}, u32[]{:S(2)}, u32[]{:S(2)}) collective-permute-start(s16[304,128]{1,0:T(8,128)(2,1)S(1)} %get-tuple-element.29), channel_id=1, source_target_pairs={{0,2},{1,3},{2,4},{3,5},{4,6},{5,7},{6,0},{7,1},{8,10},{9,11},{10,... | collective-permute-start | bytes 233480 | tf_op jit(solution)/shard_map/ppermute | solution.py:275
  63.2 9.4 %collective-permute-start.15 = (s16[304,128]{1,0:T(8,128)(2,1)S(1)}, s16[304,128]{1,0:T(8,128)(2,1)S(1)}, u32[]{:S(2)}, u32[]{:S(2)}) collective-permute-start(s16[304,128]{1,0:T(8,128)(2,1)S(1)} %get-tuple-element.30), channel_id=1, source_target_pairs={{0,6},{1,7},{2,0},{3,1},{4,2},{5,3},{6,4},{7,5},{8,14},{9,15},{10,... | collective-permute-start | bytes 233480 | tf_op jit(solution)/shard_map/ppermute | solution.py:275
  66.2 6.4 %collective-permute-start.16 = (s16[304,128]{1,0:T(8,128)(2,1)S(1)}, s16[304,128]{1,0:T(8,128)(2,1)S(1)}, u32[]{:S(2)}, u32[]{:S(2)}) collective-permute-start(s16[304,128]{1,0:T(8,128)(2,1)S(1)} %get-tuple-element.31), channel_id=1, source_target_pairs={{0,1},{1,2},{2,3},{3,4},{4,5},{5,6},{6,7},{7,0},{8,9},{9,10},{10,1... | collective-permute-start | bytes 233480 | tf_op jit(solution)/shard_map/ppermute | solution.py:275
  66.4 6.2 %collective-permute-start.17 = (s16[304,128]{1,0:T(8,128)(2,1)S(1)}, s16[304,128]{1,0:T(8,128)(2,1)S(1)}, u32[]{:S(2)}, u32[]{:S(2)}) collective-permute-start(s16[304,128]{1,0:T(8,128)(2,1)S(1)} %get-tuple-element.32), channel_id=1, source_target_pairs={{0,7},{1,0},{2,1},{3,2},{4,3},{5,4},{6,5},{7,6},{8,15},{9,8},{10,9... | collective-permute-start | bytes 233480 | tf_op jit(solution)/shard_map/ppermute | solution.py:275
